TPU v7x, 32 devices: a whole 2x2x4 slice. The times are simulated.
32 devices in a mesh: tp: 4 (over y, core), dp: 8 (over z, x).
Axes of the slice: x: 2, y: 2, z: 4, core: 2. Of those that a mesh axis runs over, the one named last changes fastest.
Arguments:
- tokens: bfloat16 [24, 1024, 768], P('dp', 'tp'), may hold values from -6 to 6
- lengths: int32 [24], P('dp'), may hold values from 196 to 1024, as said below
- ln_gain: float32 [768], replicated, may hold values from 0.1 to 1.9
- w_qkv: bfloat16 [768, 2304], P(None, 'tp'), may hold values from -0.21875 to 0.21875
- q_gain: float32 [12, 64], P('tp'), may hold values from 0.1 to 1.9
- k_gain: float32 [12, 64], P('tp'), may hold values from 0.1 to 1.9
- w_proj: bfloat16 [768, 768], P('tp'), may hold values from -1.75 to 1.75
- w_fc1: bfloat16 [768, 3072], P(None, 'tp'), may hold values from -0.21875 to 0.21875
- b_fc1: float32 [3072], P('tp'), may hold values from -3 to 3
- w_fc2: bfloat16 [3072, 768], P('tp'), may hold values from -0.109375 to 0.109375
- b_fc2: float32 [768], replicated, may hold values from -2 to 2
- d_out: bfloat16 [24, 1024, 768], P('dp', 'tp'), may hold values from -6 to 6
Outputs:
- output: bfloat16 [24, 1024, 768], P('dp', 'tp')
- d_tokens: float32 [24, 1024, 768], P('dp', 'tp')
- d_ln_gain: float32 [768], replicated
- d_qkv: float32 [768, 2304], P(None, 'tp')
- d_q_gain: float32 [12, 64], P('tp')
- d_k_gain: float32 [12, 64], P('tp')
- d_proj: float32 [768, 768], P('tp')
- d_fc1: float32 [768, 3072], P(None, 'tp')
- d_bias_one: float32 [3072], P('tp')
- d_fc2: float32 [3072, 768], P('tp')
- d_bias_two: float32 [768], replicated
Inputs may be any that keep to these rules, and one draw needn't show every extreme that they name: `lengths`: each image's length is one of 196, 576 and 1024; every draw holds all three.
All inputs are finite; a program needn't handle non-finite values.
Results may differ from a plain program's by a relative error of at most 0.014.
Values may be sent and summed in bfloat16 or wider, within the bound.
No kernel may reach another device: no remote copies, remote signals or barrier semaphores. Data moves between devices by JAX's collectives and lax.ppermute only.
A program may use at most 192 MiB of HBM per device.

v0:
```python
import functools
import math

import jax
import jax.numpy as jnp
from jax import lax
from jax.experimental import pallas as pl
from jax.experimental.pallas import tpu as pltpu
from jax.sharding import PartitionSpec as P


EPS = 1e-06
F32 = jnp.float32
BF16 = jnp.bfloat16
NN = (((1,), (0,)), ((), ()))
NT = (((1,), (1,)), ((), ()))
TN = (((0,), (0,)), ((), ()))
VMEM_SPEC = pl.BlockSpec(memory_space=pltpu.VMEM)
ANY_SPEC = pl.BlockSpec(memory_space=pl.ANY)
SMEM_SPEC = pl.BlockSpec(memory_space=pltpu.SMEM)


def mm(a, b, dims=NN):
    return lax.dot_general(a, b, dims, preferred_element_type=F32)


def call(kernel, outs, n_smem, *args, n_any=0, any_outs=0, scratch=(), flops=0):
    in_specs = [SMEM_SPEC] * n_smem + [ANY_SPEC] * n_any + [VMEM_SPEC] * (len(args) - n_smem - n_any)
    moved = sum(a.size * a.dtype.itemsize for a in args)
    moved += sum(math.prod(s) * jnp.dtype(d).itemsize for s, d in outs)
    return pl.pallas_call(
        kernel,
        out_shape=[jax.ShapeDtypeStruct(s, d) for s, d in outs],
        in_specs=in_specs,
        out_specs=[ANY_SPEC] * any_outs + [VMEM_SPEC] * (len(outs) - any_outs),
        scratch_shapes=list(scratch),
        compiler_params=pltpu.CompilerParams(vmem_limit_bytes=60 * 1024 * 1024),
        cost_estimate=pl.CostEstimate(flops=flops, transcendentals=0, bytes_accessed=moved),
    )(*args)


def norm_kernel(begin, tokens, d_out, gain_ref, *refs):
    out_refs, (held, sem, sem_out) = refs[:-3], refs[-3:]
    rows = tokens.shape[1]
    reads, copies = [], []
    for i, out in enumerate(out_refs):
        reads.append(pltpu.make_async_copy(tokens.at[begin + i], held.at[i], sem.at[i]))
        reads[-1].start()
    for i, out in enumerate(out_refs):
        copies.append(pltpu.make_async_copy(d_out.at[begin + i], out.at[pl.ds(rows, rows)], sem_out.at[i]))
        copies[-1].start()
    for i, out in enumerate(out_refs):
        reads[i].wait()
        v = held[i].astype(F32)
        c = v - jnp.mean(v, axis=-1, keepdims=True)
        r = lax.rsqrt(jnp.mean(c * c, axis=-1, keepdims=True) + EPS)
        out[0:rows] = (c * r * gain_ref[...].reshape(1, -1)).astype(BF16)
    for copy in copies:
        copy.wait()


def as_row(column):
    return jnp.broadcast_to(column, (column.shape[0], 128)).T[0:1]


def emit_pieces(acc, pos, keep_a, send_a, keep_b, *send_b):
    third = acc.shape[0] // 3
    half, step = third, keep_b.shape[0]
    keep_a[...] = acc[pl.ds(pl.multiple_of(pos[0] * half, half), half), :]
    send_a[0:half] = acc[pl.ds(pl.multiple_of((1 - pos[0]) * half, half), half), :].astype(BF16)
    for k, out in enumerate((keep_b,) + send_b):
        at = pl.multiple_of(2 * third + (pos[1] ^ k) * step, step)
        out[...] = acc[pl.ds(at, step), :].astype(out.dtype)


def ff_kernel(first, last, blocks, owned, *refs):
    refs = list(refs)
    take = lambda n: [refs.pop(0) for _ in range(n)]
    packs = take(blocks)
    prior = [] if first else take(1)
    w1, w2, b1 = take(3)
    prior_bias = [] if first else take(1)
    o_ff, n_ff = take(2)
    if last:
        summed, accb = take(2)
    else:
        acc, accb = take(2)
    buf, sem, prior_sem = take(3)
    if last:
        (acc,) = take(1)
    rows = packs[0].shape[0] // 2
    width = w1.shape[0]
    inv_sqrt2 = 2.0**-0.5

    def fetch(j, slot):
        return pltpu.make_async_copy(packs[j], buf.at[slot], sem.at[slot])

    fetch(0, 0).start()
    if prior:
        held = pltpu.make_async_copy(prior[0], acc, prior_sem)
        held.start()
        accb[...] = prior_bias[0][...]
    else:
        acc[...] = jnp.zeros(acc.shape, F32)
        accb[...] = jnp.zeros(accb.shape, F32)

    def step(k, carry):
        slot = k & 1
        fetch(0, slot).wait()
        for j in range(1, blocks):

            @pl.when(k + 1 == j)
            def _(j=j):
                fetch(j, 1 - slot).start()

        sl = pl.ds(pl.multiple_of(k * rows, rows), rows)
        x = buf[slot, 0:rows]
        g = buf[slot, rows : 2 * rows]
        h = mm(x, w1[...]) + b1[...].reshape(1, -1)
        da = mm(g, w2[...], NT)
        cdf = 0.5 * (1.0 + lax.erf(h * inv_sqrt2))
        pdf = jnp.exp(-0.5 * h * h) * (1.0 / math.sqrt(2.0 * math.pi))
        act = (h * cdf).astype(BF16)
        dh = (da * (cdf + h * pdf)).astype(BF16)
        o_ff[sl, :] = mm(act, w2[...]).astype(BF16)
        n_ff[sl, :] = mm(dh, w1[...], NT).astype(BF16)
        accb[0:1] += jnp.sum(dh.astype(F32), axis=0, keepdims=True)
        if owned:

            @pl.when(k % 2 == 0)
            def _():
                accb[1:2] += jnp.sum(g.astype(F32), axis=0, keepdims=True)

        if prior:

            @pl.when(k == 0)
            def _():
                held.wait()

        acc[0:width] += mm(x, dh, TN)
        acc[width:] += mm(act, g, TN)
        return carry

    lax.fori_loop(0, blocks, step, 0)
    if last:
        accb[2:3] = as_row(jnp.sum(w1[...].astype(F32) * acc[0:width], axis=1, keepdims=True))
        summed[...] = acc[...].astype(BF16)


def att_kernel(first, last, blocks, heads, size, starts, *refs):
    refs = list(refs)
    take = lambda n: [refs.pop(0) for _ in range(n)]
    length, pos = take(2)
    ff_parts = take(4)
    prior = [] if first else take(1)
    packs = take(blocks)
    wqkv, wproj, qg, kg = take(4)
    prior_gain = [] if first else take(1)
    ff_small = take(1) if last else []
    keep_near, keep_far, send = take(3)
    if last:
        pieces = take(len(refs) - 22)
        (small,) = take(1)
    else:
        acc, accg = take(2)
    jt, dot_s, qs_t, q_s, k_s, kt_s, v_s, vt_s, es, dqt, dk, dv, ot, djt = take(14)
    ff_s, ff_sem, prior_sem, out_s, out_sem = take(5)
    if last:
        acc, accg = take(2)
    rows = packs[0].shape[0] // 2
    later = []
    for k in range(4):
        rows_of = pl.ds(starts[k // 2], 2 * rows)
        later.append(pltpu.make_async_copy(ff_parts[k].at[rows_of], ff_s.at[k % 2, k // 2], ff_sem.at[k]))
        later[-1].start()
    if prior:
        later.append(pltpu.make_async_copy(prior[0], acc, prior_sem))
        later[-1].start()
    xs = [p.at[0:rows] for p in packs]
    gs = [p.at[rows : 2 * rows] for p in packs]
    joined = wqkv.shape[0]
    total = rows * blocks
    scale = size**-0.5
    up = scale * math.log2(math.e)
    for k in range(blocks):
        cols = slice(k * rows, (k + 1) * rows)
        jt[:, cols] = mm(wqkv[...], xs[k][...], NT)
        dot_s[:, cols] = mm(wproj[...], gs[k][...], NT)

    def normed(u):
        c = u - jnp.mean(u, axis=0, keepdims=True)
        r = lax.rsqrt(jnp.mean(c * c, axis=0, keepdims=True) + EPS)
        return c * r, r

    ones = jnp.concatenate(
        [jnp.ones((1, rows), F32), jnp.zeros((15, rows), F32)], axis=0
    ).astype(BF16)

    def prepare(h, carry):
        base = pl.multiple_of(h * 3 * size, size)
        gh = pl.ds(pl.multiple_of(h * size, size), size)
        part = lambda c: jt[pl.ds(pl.multiple_of(base + c * size, size), size), :]
        qt = normed(part(0))[0] * qg[gh, :]
        kt = normed(part(1))[0] * kg[gh, :]
        vt = part(2)
        qs_t[h] = (qt * up).astype(BF16)
        q_s[h] = qt.T.astype(BF16)
        k_s[h] = kt.T.astype(BF16)
        v_s[h] = vt.T.astype(BF16)
        for k in range(blocks):
            cols = slice(k * rows, (k + 1) * rows)
            kt_s[h, k] = kt[:, cols].astype(BF16)
            vt_s[h, k, 0:size] = vt[:, cols].astype(BF16)
            vt_s[h, k, size : size + 16] = ones
        return carry

    lax.fori_loop(0, heads, prepare, 0)

    live = length[0]
    count = (live + rows - 1) // rows

    dk[...] = jnp.zeros(dk.shape, F32)
    dv[...] = jnp.zeros(dv.shape, F32)

    def head(h, carry):
        def forward(j, acc):
            b = j ^ pos[0]
            start = pl.multiple_of(b * rows, rows)
            s = mm(k_s[h, pl.ds(start, rows), :], qs_t[h])
            slot = lax.broadcasted_iota(jnp.int32, (rows, 1), 0) + j * rows
            e = jnp.where(slot < live, jnp.exp2(s), 0.0).astype(BF16)
            es[b] = e
            return acc + mm(vt_s[h, b], e)

        acc = lax.fori_loop(0, count, forward, jnp.zeros((size + 16, total), F32))
        inv = 1.0 / acc[size : size + 1]
        o = acc[0:size] * inv
        hs = pl.ds(pl.multiple_of(h * size, size), size)
        ot[hs, :] = o.astype(BF16)
        dof = dot_s[hs, :] * inv
        dot_b = dof.astype(BF16)
        do_b = dof.T.astype(BF16)
        r = jnp.sum(dot_b.astype(F32) * o, axis=0, keepdims=True)
        q_h = q_s[h]

        def backward(j, acc):
            b = j ^ pos[0]
            start = pl.multiple_of(b * rows, rows)
            dp = mm(v_s[h, pl.ds(start, rows), :], dot_b)
            e = es[b]
            ds = (e.astype(F32) * (dp - r)).astype(BF16)
            dv[h, pl.ds(start, rows), :] = mm(e, do_b)
            dk[h, pl.ds(start, rows), :] = mm(ds, q_h)
            return acc + mm(kt_s[h, b], ds)

        dqt[h] = lax.fori_loop(0, count, backward, jnp.zeros((size, total), F32))
        return carry

    lax.fori_loop(0, heads, head, 0)

    def undo(h, carry):
        base = pl.multiple_of(h * 3 * size, size)
        gh = pl.multiple_of(h * size, size)
        for c, gain, grad in ((0, qg, dqt[h]), (1, kg, dk[h].T)):
            at = pl.ds(pl.multiple_of(base + c * size, size), size)
            n, r = normed(jt[at, :])
            grad = grad * scale
            y = grad * gain[pl.ds(gh, size), :]
            back = r * (
                y
                - jnp.mean(y, axis=0, keepdims=True)
                - n * jnp.mean(y * n, axis=0, keepdims=True)
            )
            djt[at, :] = back.astype(BF16)
            accg[pl.ds(pl.multiple_of(c * heads * size + gh, size), size), :] = jnp.sum(grad * n, axis=1, keepdims=True)
        djt[pl.ds(pl.multiple_of(base + 2 * size, size), size), :] = dv[h].T.astype(BF16)
        return carry

    lax.fori_loop(0, heads, undo, 0)
    if prior:
        accg[...] += prior_gain[0][...]

    for copy in later:
        copy.wait()

    targets = [keep_near, send.at[pl.ds(0, 2 * rows)], keep_far, send.at[pl.ds(2 * rows, 2 * rows)]]
    writes = [pltpu.make_async_copy(out_s.at[k], targets[k], out_sem.at[k]) for k in range(blocks)]

    def give(k, carry):
        cols = pl.ds(pl.multiple_of(k * rows, rows), rows)
        part = pl.ds(pl.multiple_of((k & 1) * rows, rows), rows)
        n = ff_s[1, k >> 1, part, :].astype(F32) + mm(djt[:, cols], wqkv[...], TN)
        o = ff_s[0, k >> 1, part, :].astype(F32) + mm(ot[:, cols], wproj[...], TN)
        out_s[k, 0:rows] = o.astype(BF16)
        out_s[k, rows : 2 * rows] = n.astype(BF16)
        for j in range(blocks):

            @pl.when(k == j)
            def _(j=j):
                writes[j].start()

        return carry

    lax.fori_loop(0, blocks, give, 0)
    tq = tp = None
    for k in range(blocks):
        cols = slice(k * rows, (k + 1) * rows)
        p = mm(djt[:, cols], xs[k][...])
        tq = p if tq is None else tq + p
        p = mm(ot[:, cols], gs[k][...])
        tp = p if tp is None else tp + p
    if prior:
        tq = tq + acc[0:joined]
        tp = tp + acc[joined:]
    acc[0:joined] = tq
    acc[joined:] = tp
    if last:
        ln = jnp.sum(wqkv[...].astype(F32) * tq, axis=0, keepdims=True) + ff_small[0][2:3]
        gain_row = as_row(accg[...])
        pad = jnp.zeros((1, ln.shape[1] - gain_row.shape[1]), F32)
        lines = [jnp.concatenate([gain_row, pad], axis=1), ff_small[0][0:2], ln, jnp.zeros((4, ln.shape[1]), F32)]
        small[...] = jnp.concatenate(lines, axis=0).astype(BF16)
        emit_pieces(acc, pos.at[1:3], *pieces)
        third = pieces[0].shape[0]
        pieces[1][third : third + 8] = small[...]
    for write in writes:
        write.wait()


def final_kernel(images, *refs):
    tokens, d_out, gain, bias = refs[:4]
    ins = refs[4 : 4 + 3 * images]
    out, d_tokens = refs[-2:]
    rows = tokens.shape[1]
    for i in range(images):

        @pl.when(pl.program_id(0) == i)
        def _(i=i):
            keep, near, far = ins[3 * i : 3 * i + 3]
            both = [
                keep[at].astype(F32) + near[at].astype(F32) + far[at].astype(F32)
                for at in (slice(0, rows), slice(rows, 2 * rows))
            ]
            v = tokens[0].astype(F32)
            c = v - jnp.mean(v, axis=-1, keepdims=True)
            r = lax.rsqrt(jnp.mean(c * c, axis=-1, keepdims=True) + EPS)
            xhat = c * r
            out[0] = (v + both[0] + bias[...].reshape(1, -1)).astype(BF16)
            z = both[1] * gain[...].reshape(1, -1)
            back = r * (
                z
                - jnp.mean(z, axis=-1, keepdims=True)
                - xhat * jnp.mean(z * xhat, axis=-1, keepdims=True)
            )
            d_tokens[0] = d_out[0].astype(F32) + back


def join_kernel(n, *refs):
    pos, own, far, pairs = refs[0], refs[1 : 1 + n], refs[1 + n], refs[2 + n : 2 + 2 * n]
    one, two, whole = refs[2 + 2 * n :]
    step = own[0].shape[0]
    third = step * n
    for k in range(n):
        z = pos[1] ^ k
        at = pl.multiple_of(pos[0] * third + z * step, step)
        whole[pl.ds(at, step), :] = own[k][...].astype(F32)
        at = pl.multiple_of((1 - pos[0]) * third + z * step, step)
        whole[pl.ds(at, step), :] = far[k * step : (k + 1) * step].astype(F32)
        half = step // 2
        for s in range(2):
            at = pl.multiple_of(2 * third + z * step + (pos[0] ^ s) * half, half)
            whole[pl.ds(at, half), :] = pairs[k][s * half : (s + 1) * half].astype(F32)
    cut = one.shape[0]
    one[...] = whole[0:cut]
    two[...] = whole[cut:]


def block(dp_size, tp_size, *args):
    (tokens, lengths, ln_gain, w_qkv, q_gain, k_gain, w_proj, w_fc1, b_fc1, w_fc2, b_fc2, d_out) = args
    images, rows, width = tokens.shape
    heads, size = q_gain.shape
    hidden = w_fc1.shape[1]
    total = rows * tp_size
    blocks = tp_size
    joined = heads * 3 * size
    inner = heads * size
    n = dp_size // 2
    t = lax.axis_index("tp").astype(jnp.int32)
    d = lax.axis_index("dp").astype(jnp.int32)
    x, z = d & 1, d >> 1

    def swap(v, axis, mask):
        count = tp_size if axis == "tp" else dp_size
        return lax.ppermute(v, axis, [(i, i ^ mask) for i in range(count)])

    def after(v, dep):
        return lax.optimization_barrier((v, dep))[0]

    def norm(begin, end):
        count = end - begin
        return call(
            functools.partial(norm_kernel, begin), [((2 * rows, width), BF16)] * count, 0,
            tokens, d_out, ln_gain, n_any=2,
            scratch=[
                pltpu.VMEM((count, rows, width), BF16),
                pltpu.SemaphoreType.DMA((count,)),
                pltpu.SemaphoreType.DMA((count,)),
            ],
        )

    own = norm(0, images)
    far = [swap(v, "tp", 2) for v in own]
    near = [swap(v, "tp", 1) for v in own]
    cross = [None] * images

    def forward(i, dep):
        cross[i] = swap(after(far[i], dep), "tp", 1)

    b1 = b_fc1
    pos = jnp.stack([x, z])

    def pieces_of(third, columns):
        step = third // n
        return [((third, columns), F32), ((third + 8, columns), BF16), ((step, columns), F32)] + [
            ((step, columns), BF16)
        ] * (n - 1)

    qp_pieces = pieces_of((joined + inner) // 3, width)

    def ff(first, last, packs, state):
        count = len(packs)
        outs = [((count * rows, width), BF16)] * 2
        scratch = [
            pltpu.VMEM((2, 2 * rows, width), BF16),
            pltpu.SemaphoreType.DMA((2,)),
            pltpu.SemaphoreType.DMA,
        ]
        if last:
            outs += [((width + hidden, width), BF16), ((8, width), F32)]
            scratch += [pltpu.VMEM((width + hidden, width), F32)]
        else:
            outs += [((width + hidden, width), F32), ((8, width), F32)]
        res = call(
            functools.partial(ff_kernel, first, last, count, first), outs, 0,
            *packs, *state[:1], w_fc1, w_fc2, b1, *state[1:], n_any=count + len(state[:1]),
            scratch=scratch, flops=12 * count * rows * width * hidden,
        )
        return res[0], res[1], res[2:]

    qg = q_gain.reshape(-1, 1)
    kg = k_gain.reshape(-1, 1)
    w_t = w_qkv.T
    att_pos = jnp.stack([t, x, z])
    keeps = []

    def att(i, ff_parts, starts, state, ff_small=()):
        first, last = i == 0, i == images - 1
        outs = [((2 * rows, width), BF16)] * 2 + [((4 * rows, width), BF16)]
        scratch = [
            pltpu.VMEM((joined, total), F32),
            pltpu.VMEM((inner, total), F32),
            pltpu.VMEM((heads, size, total), BF16),
            pltpu.VMEM((heads, total, size), BF16),
            pltpu.VMEM((heads, total, size), BF16),
            pltpu.VMEM((heads, blocks, size, rows), BF16),
            pltpu.VMEM((heads, total, size), BF16),
            pltpu.VMEM((heads, blocks, size + 16, rows), BF16),
            pltpu.VMEM((blocks, rows, total), BF16),
            pltpu.VMEM((heads, size, total), F32),
            pltpu.VMEM((heads, total, size), F32),
            pltpu.VMEM((heads, total, size), F32),
            pltpu.VMEM((inner, total), BF16),
            pltpu.VMEM((joined, total), BF16),
            pltpu.VMEM((2, 2, 2 * rows, width), BF16),
            pltpu.SemaphoreType.DMA((4,)),
            pltpu.SemaphoreType.DMA,
            pltpu.VMEM((blocks, 2 * rows, width), BF16),
            pltpu.SemaphoreType.DMA((blocks,)),
        ]
        if last:
            outs += qp_pieces + [((8, width), BF16)]
            scratch += [pltpu.VMEM((joined + inner, width), F32), pltpu.VMEM((2 * inner, 1), F32)]
        else:
            outs += [((joined + inner, width), F32), ((2 * inner, 1), F32)]
        res = call(
            functools.partial(att_kernel, first, last, blocks, heads, size, starts), outs, 2,
            lengths[i : i + 1], att_pos, *ff_parts, *state[:1], own[i], near[i], far[i], cross[i],
            w_t, w_proj, qg, kg, *state[1:], *ff_small, n_any=4 + len(state[:1]), any_outs=3,
            scratch=scratch,
            flops=6 * 8 * heads * total * total * size + 8 * total * width * (joined + inner),
        )
        keep_near, keep_far, send = res[:3]
        got = swap(send, "tp", 1)
        summed = (keep_far.astype(F32) + got[2 * rows :].astype(F32)).astype(BF16)
        keeps.extend([keep_near, got, swap(summed, "tp", 2)])
        return res[3:]

    def reduce_weight(small, keep_a, send_a, keep_b, *send_b):
        extra = small.shape[0]
        got = swap(send_a, "dp", 1)
        half = keep_a + got[:-extra].astype(F32)
        small = (small.astype(F32) + got[-extra:].astype(F32)).astype(BF16)
        done_b = keep_b
        for k in range(1, n):
            done_b = done_b + swap(send_b[k - 1], "dp", 2 * k).astype(F32)
        step = keep_b.shape[0]
        piece = lambda k: lax.dynamic_slice_in_dim(half, (z ^ k) * step, step, 0)
        cut = step // 2
        sent = lax.dynamic_slice_in_dim(done_b, (1 - x) * cut, cut, 0).astype(BF16)
        done_b = lax.dynamic_slice_in_dim(done_b, x * cut, cut, 0) + swap(sent, "dp", 1).astype(F32)
        done_b = done_b.astype(BF16)
        done_a = piece(0)
        smalls = [small]
        for k in range(1, n):
            got = swap(jnp.concatenate([piece(k).astype(BF16), small], axis=0), "dp", 2 * k)
            done_a = done_a + got[:-extra].astype(F32)
            smalls.append(got[-extra:])
        done_a = done_a.astype(BF16)
        smalls = jnp.stack(smalls).astype(F32)
        small = sum(lax.dynamic_index_in_dim(smalls, z ^ k, 0, keepdims=False) for k in range(n))
        pair = jnp.concatenate([done_b, swap(done_b, "dp", 1)], axis=0)
        near_a = [done_a] + [swap(done_a, "dp", 2 * k) for k in range(1, n)]
        pairs = [pair] + [swap(pair, "dp", 2 * k) for k in range(1, n)]
        far_a = swap(jnp.concatenate(near_a, axis=0), "dp", 1)
        return near_a + [far_a] + pairs, small

    def join(parts, shapes):
        return call(
            functools.partial(join_kernel, n), [(s, F32) for s in shapes], 1, pos, *parts,
            scratch=[pltpu.VMEM((3 * n * parts[0].shape[0], width), F32)],
        )

    a_parts = ff(True, False, [b for i in range(images) for b in (own[i], near[i])], [])
    forward(0, a_parts[0])
    b_parts = ff(False, False, [far[0], cross[0]], a_parts[2])
    forward(1, b_parts[0])
    att_state = att(0, a_parts[:2] + b_parts[:2], (0, 0), [])
    for i in range(2, images):
        forward(i, att_state[1])
    c_parts = ff(False, True, [b for i in range(1, images) for b in (far[i], cross[i])], b_parts[2])
    state = c_parts[2]
    ff_out, ff_small = state
    fc = lax.psum(ff_out, "dp")
    for i in range(1, images):
        starts = (2 * rows * i, 2 * rows * (i - 1))
        att_state = att(i, a_parts[:2] + c_parts[:2], starts, att_state, [ff_small] if i == images - 1 else [])
    *qp_out, small = att_state
    qp_parts, late = reduce_weight(small, *qp_out)
    d_q_gain = late[0, :inner].reshape(heads, size)
    d_k_gain = late[0, inner : 2 * inner].reshape(heads, size)
    d_bias_one = late[1]
    both = late[2:4]
    both = both + swap(both, "tp", 1)
    both = both + swap(both, "tp", 2)
    d_bias_two = both[0]
    d_ln_gain = both[1] / ln_gain

    d_fc1, d_fc2 = fc[:width].astype(F32), fc[width:].astype(F32)
    d_qkv_t, d_proj = join(qp_parts, [(joined, width), (inner, width)])
    d_qkv = d_qkv_t.T

    def finish(begin, end, earlier):
        block = pl.BlockSpec((1, rows, width), lambda i: (begin + i, 0, 0))
        vector = pl.BlockSpec((width,), lambda i: (0,))
        first = pl.BlockSpec((2 * rows, width), lambda i: (0, 0))
        ins = keeps[3 * begin : 3 * end]
        return pl.pallas_call(
            functools.partial(final_kernel, end - begin),
            grid=(end - begin,),
            out_shape=[
                jax.ShapeDtypeStruct((images, rows, width), BF16),
                jax.ShapeDtypeStruct((images, rows, width), F32),
            ],
            in_specs=[block, block, vector, vector] + [first] * len(ins) + [ANY_SPEC] * len(earlier),
            out_specs=[block, block],
            input_output_aliases={4 + len(ins) + k: k for k in range(len(earlier))},
        )(tokens, d_out, ln_gain, b_fc2, *ins, *earlier)

    results = finish(0, images - 1, [])
    output, d_tokens = finish(images - 1, images, results)
    return (output, d_tokens, d_ln_gain, d_qkv, d_q_gain, d_k_gain, d_proj, d_fc1, d_bias_one, d_fc2, d_bias_two)


def solution(mesh):
    rows = P("dp", "tp", None)
    wide = P(None, "tp")
    tall = P("tp", None)
    return jax.shard_map(
        functools.partial(block, mesh.shape["dp"], mesh.shape["tp"]),
        mesh=mesh,
        in_specs=(rows, P("dp"), P(), wide, tall, tall, tall, wide, P("tp"), tall, P(), rows),
        out_specs=(rows, rows, P(), wide, tall, tall, tall, wide, P("tp"), tall, P()),
        check_vma=False,
    )
```

profile of v0, /device:TPU:0, one launch (start us, length us, event | category | flops | bytes accessed | tf_op | source)
XLA Modules:
  0.0 316.5 jit_solution(9375456414167955994)
XLA Ops:
  7.2 4.0 %shard_map.203 = (bf16[512,768]{1,0:T(8,128)(2,1)}, bf16[512,768]{1,0:T(8,128)(2,1)}, bf16[512,768]{1,0:T(8,128)(2,1)}) custom-call(bf16[3,256,768]{2,1,0:T(8,128)(2,1)} %refs_0_.3, bf16[3,256,768]{2,1,0:T(8,128)(2,1)} %refs_1_.3, f32[768]{0:T(1024)} %refs_2_.3), custom_call_target="tpu_custom_call" | custom-call | bytes 4721664 | tf_op jit(solution)/shard_map/pallas_call | solution.py:31
  12.4 2.6 collective-permute-start.4
  15.0 0.8 copy-done.27
  16.7 0.9 copy-done.23
  17.6 19.3 %shard_map.204 = (bf16[1536,768]{1,0:T(8,128)(2,1)}, bf16[1536,768]{1,0:T(8,128)(2,1)}, f32[1536,768]{1,0:T(8,128)}, f32[8,768]{1,0:T(8,128)}) custom-call(bf16[512,768]{1,0:T(8,128)(2,1)} %get-tuple-element.55.refs_0_.refs_6_, bf16[512,768]{1,0:T(8,128)(2,1)} %copy-done.27, bf16[512,768]{1,0:T(8,128)(2,1)} %get-tuple-element.56.refs_2_.refs_7_, ...), custom_call_target="tpu_custom_call" | custom-call | flops 10871635968 | bytes 16542720 | tf_op jit(solution)/shard_map/pallas_call | solution.py:31
  37.1 2.3 collective-permute-start.3
  39.5 0.8 reshape.36.refs_12_.refs_13_
  40.3 0.8 reshape.37.refs_13_.refs_14_
  42.3 9.4 %shard_map.205 = (bf16[512,768]{1,0:T(8,128)(2,1)}, bf16[512,768]{1,0:T(8,128)(2,1)}, f32[1536,768]{1,0:T(8,128)}, f32[8,768]{1,0:T(8,128)}) custom-call(bf16[512,768]{1,0:T(8,128)(2,1)} %collective-permute-done.4.refs_0_.refs_8_, bf16[512,768]{1,0:T(8,128)(2,1)} %collective-permute-done.5.refs_1_.refs_9_, f32[1536,768]{1,0:T(8,128)} %get-tuple-element.61.refs_2_, ...), custom_call_target="tpu_custom_call" | custom-call | flops 3623878656 | bytes 14994432 | tf_op jit(solution)/shard_map/pallas_call | solution.py:31
  51.7 6.1 %collective-permute-done.3.refs_0_.refs_9_ = bf16[512,768]{1,0:T(8,128)(2,1)S(1)} collective-permute-done((bf16[512,768]{1,0:T(8,128)(2,1)S(1)}, bf16[512,768]{1,0:T(8,128)(2,1)S(1)}, u32[]{:S(2)}, u32[]{:S(2)}) %collective-permute-start.3) | collective-permute-done | bytes 786464 | tf_op jit(solution)/shard_map/ppermute | solution.py:394
  57.8 17.0 %shard_map.206 = (bf16[512,768]{1,0:T(8,128)(2,1)}, bf16[512,768]{1,0:T(8,128)(2,1)}, bf16[1024,768]{1,0:T(8,128)(2,1)}, f32[768,768]{1,0:T(8,128)}, f32[384,1]{1,0:T(8,128)}) custom-call(s32[1]{0:T(128)} %get-tuple-element.113.refs_0_, s32[3]{0:T(128)} %pad_add_fusion.refs_1_, bf16[1536,768]{1,0:T(8,128)(2,1)} %get-tuple-element.58.refs_2_, ...), custom_call_target="tpu_custom_call" | custom-call | flops 14495514624 | bytes 16124944 | tf_op jit(solution)/shard_map/pallas_call | solution.py:31
  75.4 1.9 collective-permute-done.8.refs_3_.refs_10_
  77.3 0.9 copy-done.29
  78.2 13.8 %shard_map.207 = (bf16[1024,768]{1,0:T(8,128)(2,1)}, bf16[1024,768]{1,0:T(8,128)(2,1)}, bf16[1536,768]{1,0:T(8,128)(2,1)}, f32[8,768]{1,0:T(8,128)}) custom-call(bf16[512,768]{1,0:T(8,128)(2,1)} %copy-done.28, bf16[512,768]{1,0:T(8,128)(2,1)} %collective-permute-done.6.refs_1_.refs_10_, bf16[512,768]{1,0:T(8,128)(2,1)} %copy-done.26, ...), custom_call_target="tpu_custom_call" | custom-call | flops 7247757312 | bytes 15780864 | tf_op jit(solution)/shard_map/pallas_call | solution.py:31
  92.1 23.6 %shard_map.208 = (bf16[512,768]{1,0:T(8,128)(2,1)}, bf16[512,768]{1,0:T(8,128)(2,1)}, bf16[1024,768]{1,0:T(8,128)(2,1)}, f32[768,768]{1,0:T(8,128)}, f32[384,1]{1,0:T(8,128)}) custom-call(s32[1]{0:T(128)} %get-tuple-element.111.refs_0_, s32[3]{0:T(128)} %pad_add_fusion.refs_1_, bf16[1536,768]{1,0:T(8,128)(2,1)} %get-tuple-element.58.refs_2_, ...), custom_call_target="tpu_custom_call" | custom-call | flops 14495514624 | bytes 20058640 | tf_op jit(solution)/shard_map/pallas_call | solution.py:31
  115.7 26.9 %shard_map.209 = (bf16[512,768]{1,0:T(8,128)(2,1)}, bf16[512,768]{1,0:T(8,128)(2,1)}, bf16[1024,768]{1,0:T(8,128)(2,1)}, f32[256,768]{1,0:T(8,128)}, bf16[264,76...) custom-call(s32[1]{0:T(128)} %get-tuple-element.112.refs_0_, ...), custom_call_target="tpu_custom_call" | custom-call | flops 14495514624 | bytes 19418128 | tf_op jit(solution)/shard_map/pallas_call | solution.py:31
  142.6 7.4 %collective-permute-start.27 = (bf16[64,768]{1,0:T(8,128)(2,1)}, bf16[64,768]{1,0:T(8,128)(2,1)S(1)}, u32[]{:S(2)}, u32[]{:S(2)}) collective-permute-start(bf16[64,768]{1,0:T(8,128)(2,1)} %get-tuple-element.95), channel_id=1, source_target_pairs={{0,6},{1,7},{2,4},{3,5},{4,2},{5,3},{6,0},{7,1},{8,14},{9,15},{10,... | collective-permute-start | bytes 294920 | tf_op jit(solution)/shard_map/ppermute | solution.py:394
  150.0 2.3 collective-permute-start.26
  153.5 6.4 %collective-permute-done.26 = bf16[64,768]{1,0:T(8,128)(2,1)S(1)} collective-permute-done((bf16[64,768]{1,0:T(8,128)(2,1)}, bf16[64,768]{1,0:T(8,128)(2,1)S(1)}, u32[]{:S(2)}, u32[]{:S(2)}) %collective-permute-start.26) | collective-permute-done | bytes 98336 | tf_op jit(solution)/shard_map/ppermute | solution.py:394
  160.0 1.0 convert_add_fusion.1
  162.2 3.0 collective-permute-done.28
  165.5 1.4 convert_add_fusion
  167.8 3.2 %collective-permute-start.18 = (bf16[72,768]{1,0:T(8,128)(2,1)S(1)}, bf16[72,768]{1,0:T(8,128)(2,1)S(1)}, u32[]{:S(2)}, u32[]{:S(2)}) collective-permute-start(bf16[72,768]{1,0:T(8,128)(2,1)S(1)} %get-tuple-element.110), channel_id=1, source_target_pairs={{0,6},{1,7},{2,4},{3,5},{4,2},{5,3},{6,0},{7,1},{8,14},{9,15},{10,... | collective-permute-start | bytes 331784 | tf_op jit(solution)/shard_map/ppermute | solution.py:394
  171.0 1.2 collective-permute-start.16
  172.3 5.6 %collective-permute-done.18 = bf16[72,768]{1,0:T(8,128)(2,1)S(1)} collective-permute-done((bf16[72,768]{1,0:T(8,128)(2,1)S(1)}, bf16[72,768]{1,0:T(8,128)(2,1)S(1)}, u32[]{:S(2)}, u32[]{:S(2)}) %collective-permute-start.18) | collective-permute-done | bytes 110624 | tf_op jit(solution)/shard_map/ppermute | solution.py:394
  177.9 13.3 %collective-permute-done.17 = bf16[72,768]{1,0:T(8,128)(2,1)S(1)} collective-permute-done((bf16[72,768]{1,0:T(8,128)(2,1)S(1)}, bf16[72,768]{1,0:T(8,128)(2,1)S(1)}, u32[]{:S(2)}, u32[]{:S(2)}) %collective-permute-start.17) | collective-permute-done | bytes 110624 | tf_op jit(solution)/shard_map/ppermute | solution.py:394
  191.3 2.7 collective-permute-start.22
  194.1 6.0 %collective-permute-done.21.refs_2_ = bf16[64,768]{1,0:T(8,128)(2,1)S(1)} collective-permute-done((bf16[64,768]{1,0:T(8,128)(2,1)S(1)}, bf16[64,768]{1,0:T(8,128)(2,1)S(1)}, u32[]{:S(2)}, u32[]{:S(2)}) %collective-permute-start.21) | collective-permute-done | bytes 98336 | tf_op jit(solution)/shard_map/ppermute | solution.py:394
  200.1 3.0 collective-permute-start.23
  203.1 2.1 collective-permute-done.22.refs_3_
  205.2 4.2 %collective-permute-done.23.refs_4_ = bf16[64,768]{1,0:T(8,128)(2,1)S(1)} collective-permute-done((bf16[64,768]{1,0:T(8,128)(2,1)S(1)}, bf16[64,768]{1,0:T(8,128)(2,1)S(1)}, u32[]{:S(2)}, u32[]{:S(2)}) %collective-permute-start.23) | collective-permute-done | bytes 98336 | tf_op jit(solution)/shard_map/ppermute | solution.py:394
  210.2 1.5 collective-permute-start.24
  211.7 1.1 add_convert_fusion.1
  212.8 1.5 collective-permute-start.12
  214.3 1.2 add_convert_fusion
  216.2 1.1 add_convert_fusion.2
  217.3 1.4 collective-permute-start.10
  221.4 45.2 %collective-permute-done.20 = f32[2,768]{1,0:T(2,128)S(1)} collective-permute-done((f32[2,768]{1,0:T(2,128)S(1)}, f32[2,768]{1,0:T(2,128)S(1)}, u32[]{:S(2)}, u32[]{:S(2)}) %collective-permute-start.20) | collective-permute-done | bytes 6176 | tf_op jit(solution)/shard_map/ppermute | solution.py:394
  266.6 3.6 %collective-permute-start.31 = (bf16[64,768]{1,0:T(8,128)(2,1)S(1)}, bf16[64,768]{1,0:T(8,128)(2,1)S(1)}, u32[]{:S(2)}, u32[]{:S(2)}) collective-permute-start(bf16[64,768]{1,0:T(8,128)(2,1)S(1)} %pad_maximum_fusion.4.refs_6_), channel_id=1, source_target_pairs={{0,4},{1,5},{2,6},{3,7},{4,0},{5,1},{6,2},{7,3},{8,12},{9,13},{10,... | collective-permute-start | bytes 294920 | tf_op jit(solution)/shard_map/ppermute | solution.py:394
  270.8 11.4 %collective-permute-done.31.refs_8_ = bf16[64,768]{1,0:T(8,128)(2,1)S(1)} collective-permute-done((bf16[64,768]{1,0:T(8,128)(2,1)S(1)}, bf16[64,768]{1,0:T(8,128)(2,1)S(1)}, u32[]{:S(2)}, u32[]{:S(2)}) %collective-permute-start.31) | collective-permute-done | bytes 98336 | tf_op jit(solution)/shard_map/ppermute | solution.py:394
  282.2 1.0 collective-permute-start.32
  284.4 6.7 %collective-permute-done.32.refs_9_ = bf16[64,768]{1,0:T(8,128)(2,1)S(1)} collective-permute-done((bf16[64,768]{1,0:T(8,128)(2,1)S(1)}, bf16[64,768]{1,0:T(8,128)(2,1)S(1)}, u32[]{:S(2)}, u32[]{:S(2)}) %collective-permute-start.32) | collective-permute-done | bytes 98336 | tf_op jit(solution)/shard_map/ppermute | solution.py:394
  291.8 3.0 shard_map.212
  294.8 0.9 copy-done.5
  295.8 5.2 %shard_map.210 = (bf16[3,256,768]{2,1,0:T(8,128)(2,1)}, f32[3,256,768]{2,1,0:T(8,128)}) custom-call(bf16[3,256,768]{2,1,0:T(8,128)(2,1)} %refs_0_.3, bf16[3,256,768]{2,1,0:T(8,128)(2,1)} %refs_1_.3, f32[768]{0:T(1024)} %refs_2_.3, f32[768]{0:T(1024)} %refs_3_.5, bf16[512,768]{1,0:T(8,128)(2,1)} %get-tuple-element.79.refs_4_, bf16[1024,768]{1,0:T(8,128)(2,1)} %copy-done.1, ...), custom_call_target="tpu_custom_call" | custom-call | tf_op jit(solution)/shard_map/pallas_call | solution.py:567
  301.0 4.2 %slice_convert_fusion = (f32[768,768]{1,0:T(8,128)}, f32[768,768]{1,0:T(8,128)}) fusion(bf16[1536,768]{1,0:T(8,128)(2,1)} %all-reduce.2.cloned.1.call-done), kind=kLoop, calls=%fused_computation.3 | loop fusion | flops 1179648 | bytes 7077888 | tf_op jit(solution)/shard_map/convert_element_type | solution.py:558
  305.2 0.9 copy-done.4
  306.1 3.5 %shard_map.211 = (bf16[3,256,768]{2,1,0:T(8,128)(2,1)}, f32[3,256,768]{2,1,0:T(8,128)}) custom-call(bf16[3,256,768]{2,1,0:T(8,128)(2,1)} %refs_0_.3, bf16[3,256,768]{2,1,0:T(8,128)(2,1)} %refs_1_.3, f32[768]{0:T(1024)} %refs_2_.3, f32[768]{0:T(1024)} %refs_3_.5, ...), custom_call_target="tpu_custom_call", output_to_operand_aliasing={{0}: (7, {}), {1}: (8, {})} | custom-call | tf_op jit(solution)/shard_map/pallas_call | solution.py:567
  (125 shorter events, 14.7 us)
Async XLA Ops:
  7.2 293.8 %all-reduce.2.cloned.1.call-start = ((), (), s32[]{:S(2)}) async-start(), calls=%async_computation | async-start | bytes 4718592 | tf_op jit(solution)/shard_map/psum | solution.py:543
  11.2 3.7 %collective-permute-start = (bf16[512,768]{1,0:T(8,128)(2,1)}, bf16[512,768]{1,0:T(8,128)(2,1)S(1)}, u32[]{:S(2)}, u32[]{:S(2)}) collective-permute-start(bf16[512,768]{1,0:T(8,128)(2,1)} %get-tuple-element.55.refs_0_.refs_6_), channel_id=1, source_target_pairs={{0,8},{8,0},{16,24},{24,16},{1,9},{9,1},{17,25},{25,17},{2,10},{10... | collective-permute-start | bytes 2359304 | tf_op jit(solution)/shard_map/ppermute | solution.py:394
  11.8 3.2 %collective-permute-start.1 = (bf16[512,768]{1,0:T(8,128)(2,1)}, bf16[512,768]{1,0:T(8,128)(2,1)S(1)}, u32[]{:S(2)}, u32[]{:S(2)}) collective-permute-start(bf16[512,768]{1,0:T(8,128)(2,1)} %get-tuple-element.56.refs_2_.refs_7_), channel_id=1, source_target_pairs={{0,8},{8,0},{16,24},{24,16},{1,9},{9,1},{17,25},{25,17},{2,10},{10... | collective-permute-start | bytes 2359304 | tf_op jit(solution)/shard_map/ppermute | solution.py:394
  11.8 25.3 %copy-start.24 = (bf16[512,768]{1,0:T(8,128)(2,1)S(1)}, bf16[512,768]{1,0:T(8,128)(2,1)}, u32[]{:S(2)}) copy-start(bf16[512,768]{1,0:T(8,128)(2,1)} %get-tuple-element.56.refs_2_.refs_7_) | copy-start | bytes 2359300
  11.8 27.6 %copy-start.22 = (bf16[512,768]{1,0:T(8,128)(2,1)S(1)}, bf16[512,768]{1,0:T(8,128)(2,1)}, u32[]{:S(2)}) copy-start(bf16[512,768]{1,0:T(8,128)(2,1)} %get-tuple-element.57.refs_4_.refs_7_) | copy-start | bytes 2359300
  11.8 27.7 %copy-start.19 = (f32[3,64]{1,0:T(4,128)S(1)}, f32[3,64]{1,0:T(4,128)}, u32[]{:S(2)}) copy-start(f32[3,64]{1,0:T(4,128)} %param.16) | copy-start | bytes 2308
  11.8 28.4 %copy-start.20 = (f32[3,64]{1,0:T(4,128)S(1)}, f32[3,64]{1,0:T(4,128)}, u32[]{:S(2)}) copy-start(f32[3,64]{1,0:T(4,128)} %param.17) | copy-start | bytes 2308
  11.8 29.8 %copy-start.18 = (s32[3]{0:T(128)S(1)}, s32[3]{0:T(128)}, u32[]{:S(2)}) copy-start(s32[3]{0:T(128)} %param.13) | copy-start | bytes 40
  11.9 4.3 %collective-permute-start.2 = (bf16[512,768]{1,0:T(8,128)(2,1)}, bf16[512,768]{1,0:T(8,128)(2,1)S(1)}, u32[]{:S(2)}, u32[]{:S(2)}) collective-permute-start(bf16[512,768]{1,0:T(8,128)(2,1)} %get-tuple-element.57.refs_4_.refs_7_), channel_id=1, source_target_pairs={{0,8},{8,0},{16,24},{24,16},{1,9},{9,1},{17,25},{25,17},{2,10},{10... | collective-permute-start | bytes 2359304 | tf_op jit(solution)/shard_map/ppermute | solution.py:394
  12.4 24.6 %collective-permute-start.4 = (bf16[512,768]{1,0:T(8,128)(2,1)}, bf16[512,768]{1,0:T(8,128)(2,1)}, u32[]{:S(2)}, u32[]{:S(2)}) collective-permute-start(bf16[512,768]{1,0:T(8,128)(2,1)} %get-tuple-element.55.refs_0_.refs_6_), channel_id=1, source_target_pairs={{0,16},{8,24},{16,0},{24,8},{1,17},{9,25},{17,1},{25,9},{2,18},{10... | collective-permute-start | bytes 2359304 | tf_op jit(solution)/shard_map/ppermute | solution.py:394
  36.9 5.3 %collective-permute-start.5 = (bf16[512,768]{1,0:T(8,128)(2,1)}, bf16[512,768]{1,0:T(8,128)(2,1)}, u32[]{:S(2)}, u32[]{:S(2)}) collective-permute-start(bf16[512,768]{1,0:T(8,128)(2,1)} %collective-permute-done.4.refs_0_.refs_8_), channel_id=1, source_target_pairs={{0,8},{8,0},{16,24},{24,16},{1,9},{9,1},{17,25},{25,17},{2,10},{10... | collective-permute-start | bytes 2359304 | tf_op jit(solution)/shard_map/ppermute | solution.py:394
  37.1 20.7 %collective-permute-start.3 = (bf16[512,768]{1,0:T(8,128)(2,1)S(1)}, bf16[512,768]{1,0:T(8,128)(2,1)S(1)}, u32[]{:S(2)}, u32[]{:S(2)}) collective-permute-start(bf16[512,768]{1,0:T(8,128)(2,1)S(1)} %copy-done.24), channel_id=1, source_target_pairs={{0,16},{8,24},{16,0},{24,8},{1,17},{9,25},{17,1},{25,9},{2,18},{10... | collective-permute-start | bytes 2359304 | tf_op jit(solution)/shard_map/ppermute | solution.py:394
  39.4 35.4 %collective-permute-start.7 = (bf16[512,768]{1,0:T(8,128)(2,1)S(1)}, bf16[512,768]{1,0:T(8,128)(2,1)S(1)}, u32[]{:S(2)}, u32[]{:S(2)}) collective-permute-start(bf16[512,768]{1,0:T(8,128)(2,1)S(1)} %copy-done.22), channel_id=1, source_target_pairs={{0,16},{8,24},{16,0},{24,8},{1,17},{9,25},{17,1},{25,9},{2,18},{10... | collective-permute-start | bytes 2359304 | tf_op jit(solution)/shard_map/ppermute | solution.py:394
  57.8 17.0 %copy-start.28 = (bf16[512,768]{1,0:T(8,128)(2,1)}, bf16[512,768]{1,0:T(8,128)(2,1)S(1)}, u32[]{:S(2)}) copy-start(bf16[512,768]{1,0:T(8,128)(2,1)S(1)} %collective-permute-done.3.refs_0_.refs_9_) | copy-start | bytes 2359300
  57.8 17.6 %collective-permute-start.6 = (bf16[512,768]{1,0:T(8,128)(2,1)S(1)}, bf16[512,768]{1,0:T(8,128)(2,1)}, u32[]{:S(2)}, u32[]{:S(2)}) collective-permute-start(bf16[512,768]{1,0:T(8,128)(2,1)S(1)} %collective-permute-done.3.refs_0_.refs_9_), channel_id=1, source_target_pairs={{0,8},{8,0},{16,24},{24,16},{1,9},{9,1},{17,25},{25,17},{2,10},{10... | collective-permute-start | bytes 2359304 | tf_op jit(solution)/shard_map/ppermute | solution.py:394
  74.8 2.5 collective-permute-start.8
  142.6 11.0 %collective-permute-start.27 = (bf16[64,768]{1,0:T(8,128)(2,1)}, bf16[64,768]{1,0:T(8,128)(2,1)S(1)}, u32[]{:S(2)}, u32[]{:S(2)}) collective-permute-start(bf16[64,768]{1,0:T(8,128)(2,1)} %get-tuple-element.95), channel_id=1, source_target_pairs={{0,6},{1,7},{2,4},{3,5},{4,2},{5,3},{6,0},{7,1},{8,14},{9,15},{10,... | collective-permute-start | bytes 294920 | tf_op jit(solution)/shard_map/ppermute | solution.py:394
  150.0 10.0 %collective-permute-start.26 = (bf16[64,768]{1,0:T(8,128)(2,1)}, bf16[64,768]{1,0:T(8,128)(2,1)S(1)}, u32[]{:S(2)}, u32[]{:S(2)}) collective-permute-start(bf16[64,768]{1,0:T(8,128)(2,1)} %get-tuple-element.94), channel_id=1, source_target_pairs={{0,4},{1,5},{2,6},{3,7},{4,0},{5,1},{6,2},{7,3},{8,12},{9,13},{10,... | collective-permute-start | bytes 294920 | tf_op jit(solution)/shard_map/ppermute | solution.py:394
  152.3 7.7 %collective-permute-start.25 = (bf16[64,768]{1,0:T(8,128)(2,1)}, bf16[64,768]{1,0:T(8,128)(2,1)S(1)}, u32[]{:S(2)}, u32[]{:S(2)}) collective-permute-start(bf16[64,768]{1,0:T(8,128)(2,1)} %get-tuple-element.93), channel_id=1, source_target_pairs={{0,2},{1,3},{2,0},{3,1},{4,6},{5,7},{6,4},{7,5},{8,10},{9,11},{10,... | collective-permute-start | bytes 294920 | tf_op jit(solution)/shard_map/ppermute | solution.py:394
  152.8 12.7 %collective-permute-start.15 = (bf16[264,768]{1,0:T(8,128)(2,1)}, bf16[264,768]{1,0:T(8,128)(2,1)}, u32[]{:S(2)}, u32[]{:S(2)}) collective-permute-start(bf16[264,768]{1,0:T(8,128)(2,1)} %get-tuple-element.90), channel_id=1, source_target_pairs={{0,1},{1,0},{2,3},{3,2},{4,5},{5,4},{6,7},{7,6},{8,9},{9,8},{10,11... | collective-permute-start | bytes 1216520 | tf_op jit(solution)/shard_map/ppermute | solution.py:394
  161.0 4.2 %collective-permute-start.28 = (bf16[32,768]{1,0:T(8,128)(2,1)S(1)}, bf16[32,768]{1,0:T(8,128)(2,1)S(1)}, u32[]{:S(2)}, u32[]{:S(2)}) collective-permute-start(bf16[32,768]{1,0:T(8,128)(2,1)S(1)} %dynamic-slice_convert_fusion.3), channel_id=1, source_target_pairs={{0,1},{1,0},{2,3},{3,2},{4,5},{5,4},{6,7},{7,6},{8,9},{9,8},{10,11... | collective-permute-start | bytes 147464 | tf_op jit(solution)/shard_map/ppermute | solution.py:394
  161.6 48.6 %collective-permute-start.11 = (bf16[1024,768]{1,0:T(8,128)(2,1)}, bf16[1024,768]{1,0:T(8,128)(2,1)S(1)}, u32[]{:S(2)}, u32[]{:S(2)}) collective-permute-start(bf16[1024,768]{1,0:T(8,128)(2,1)} %get-tuple-element.80), channel_id=1, source_target_pairs={{0,8},{8,0},{16,24},{24,16},{1,9},{9,1},{17,25},{25,17},{2,10},{10... | collective-permute-start | bytes 4718600 | tf_op jit(solution)/shard_map/ppermute | solution.py:394
  161.6 53.9 %collective-permute-start.9 = (bf16[1024,768]{1,0:T(8,128)(2,1)}, bf16[1024,768]{1,0:T(8,128)(2,1)S(1)}, u32[]{:S(2)}, u32[]{:S(2)}) collective-permute-start(bf16[1024,768]{1,0:T(8,128)(2,1)} %get-tuple-element.77), channel_id=1, source_target_pairs={{0,8},{8,0},{16,24},{24,16},{1,9},{9,1},{17,25},{25,17},{2,10},{10... | collective-permute-start | bytes 4718600 | tf_op jit(solution)/shard_map/ppermute | solution.py:394
  165.2 5.9 %collective-permute-start.29 = (bf16[32,768]{1,0:T(8,128)(2,1)S(1)}, bf16[32,768]{1,0:T(8,128)(2,1)S(1)}, u32[]{:S(2)}, u32[]{:S(2)}) collective-permute-start(bf16[32,768]{1,0:T(8,128)(2,1)S(1)} %add_convert_fusion.4), channel_id=1, source_target_pairs={{0,1},{1,0},{2,3},{3,2},{4,5},{5,4},{6,7},{7,6},{8,9},{9,8},{10,11... | collective-permute-start | bytes 147464 | tf_op jit(solution)/shard_map/ppermute | solution.py:394
  165.5 12.4 %copy-start.21 = (bf16[1024,768]{1,0:T(8,128)(2,1)S(1)}, bf16[1024,768]{1,0:T(8,128)(2,1)}, u32[]{:S(2)}) copy-start(bf16[1024,768]{1,0:T(8,128)(2,1)} %get-tuple-element.83) | copy-start | bytes 4718596
  166.9 44.8 %copy-start.6 = (bf16[512,768]{1,0:T(8,128)(2,1)S(1)}, bf16[512,768]{1,0:T(8,128)(2,1)}, u32[]{:S(2)}) copy-start(bf16[512,768]{1,0:T(8,128)(2,1)} %get-tuple-element.81) | copy-start | bytes 2359300
  167.8 10.1 %collective-permute-start.18 = (bf16[72,768]{1,0:T(8,128)(2,1)S(1)}, bf16[72,768]{1,0:T(8,128)(2,1)S(1)}, u32[]{:S(2)}, u32[]{:S(2)}) collective-permute-start(bf16[72,768]{1,0:T(8,128)(2,1)S(1)} %get-tuple-element.110), channel_id=1, source_target_pairs={{0,6},{1,7},{2,4},{3,5},{4,2},{5,3},{6,0},{7,1},{8,14},{9,15},{10,... | collective-permute-start | bytes 331784 | tf_op jit(solution)/shard_map/ppermute | solution.py:394
  171.0 20.2 %collective-permute-start.17 = (bf16[72,768]{1,0:T(8,128)(2,1)S(1)}, bf16[72,768]{1,0:T(8,128)(2,1)S(1)}, u32[]{:S(2)}, u32[]{:S(2)}) collective-permute-start(bf16[72,768]{1,0:T(8,128)(2,1)S(1)} %get-tuple-element.109), channel_id=1, source_target_pairs={{0,4},{1,5},{2,6},{3,7},{4,0},{5,1},{6,2},{7,3},{8,12},{9,13},{10,... | collective-permute-start | bytes 331784 | tf_op jit(solution)/shard_map/ppermute | solution.py:394
  171.0 20.1 %collective-permute-start.16 = (bf16[72,768]{1,0:T(8,128)(2,1)S(1)}, bf16[72,768]{1,0:T(8,128)(2,1)S(1)}, u32[]{:S(2)}, u32[]{:S(2)}) collective-permute-start(bf16[72,768]{1,0:T(8,128)(2,1)S(1)} %get-tuple-element.108), channel_id=1, source_target_pairs={{0,2},{1,3},{2,0},{3,1},{4,6},{5,7},{6,4},{7,5},{8,10},{9,11},{10,... | collective-permute-start | bytes 331784 | tf_op jit(solution)/shard_map/ppermute | solution.py:394
  172.3 109.9 %copy-start.12 = (bf16[64,768]{1,0:T(8,128)(2,1)}, bf16[64,768]{1,0:T(8,128)(2,1)S(1)}, u32[]{:S(2)}) copy-start(bf16[64,768]{1,0:T(8,128)(2,1)S(1)} %pad_maximum_fusion.4.refs_6_) | copy-start | bytes 294916
  177.9 34.9 %collective-permute-start.13 = (bf16[1024,768]{1,0:T(8,128)(2,1)S(1)}, bf16[1024,768]{1,0:T(8,128)(2,1)S(1)}, u32[]{:S(2)}, u32[]{:S(2)}) collective-permute-start(bf16[1024,768]{1,0:T(8,128)(2,1)S(1)} %copy-done.21), channel_id=1, source_target_pairs={{0,8},{8,0},{16,24},{24,16},{1,9},{9,1},{17,25},{25,17},{2,10},{10... | collective-permute-start | bytes 4718600 | tf_op jit(solution)/shard_map/ppermute | solution.py:394
  191.2 21.5 %copy-start.3 = (bf16[64,768]{1,0:T(8,128)(2,1)}, bf16[64,768]{1,0:T(8,128)(2,1)S(1)}, u32[]{:S(2)}) copy-start(bf16[64,768]{1,0:T(8,128)(2,1)S(1)} %add_convert_fusion.3.refs_1_) | copy-start | bytes 294916
  191.2 8.8 %collective-permute-start.21 = (bf16[64,768]{1,0:T(8,128)(2,1)S(1)}, bf16[64,768]{1,0:T(8,128)(2,1)S(1)}, u32[]{:S(2)}, u32[]{:S(2)}) collective-permute-start(bf16[64,768]{1,0:T(8,128)(2,1)S(1)} %add_convert_fusion.3.refs_1_), channel_id=1, source_target_pairs={{0,2},{1,3},{2,0},{3,1},{4,6},{5,7},{6,4},{7,5},{8,10},{9,11},{10,... | collective-permute-start | bytes 294920 | tf_op jit(solution)/shard_map/ppermute | solution.py:394
  191.3 13.9 %collective-permute-start.22 = (bf16[64,768]{1,0:T(8,128)(2,1)S(1)}, bf16[64,768]{1,0:T(8,128)(2,1)S(1)}, u32[]{:S(2)}, u32[]{:S(2)}) collective-permute-start(bf16[64,768]{1,0:T(8,128)(2,1)S(1)} %add_convert_fusion.3.refs_1_), channel_id=1, source_target_pairs={{0,4},{1,5},{2,6},{3,7},{4,0},{5,1},{6,2},{7,3},{8,12},{9,13},{10,... | collective-permute-start | bytes 294920 | tf_op jit(solution)/shard_map/ppermute | solution.py:394
  200.1 12.7 %copy-start.9 = (bf16[64,768]{1,0:T(8,128)(2,1)}, bf16[64,768]{1,0:T(8,128)(2,1)S(1)}, u32[]{:S(2)}) copy-start(bf16[64,768]{1,0:T(8,128)(2,1)S(1)} %collective-permute-done.21.refs_2_) | copy-start | bytes 294916
  200.1 9.3 %collective-permute-start.23 = (bf16[64,768]{1,0:T(8,128)(2,1)S(1)}, bf16[64,768]{1,0:T(8,128)(2,1)S(1)}, u32[]{:S(2)}, u32[]{:S(2)}) collective-permute-start(bf16[64,768]{1,0:T(8,128)(2,1)S(1)} %add_convert_fusion.3.refs_1_), channel_id=1, source_target_pairs={{0,6},{1,7},{2,4},{3,5},{4,2},{5,3},{6,0},{7,1},{8,14},{9,15},{10,... | collective-permute-start | bytes 294920 | tf_op jit(solution)/shard_map/ppermute | solution.py:394
  203.1 11.2 %copy-start.7 = (bf16[512,768]{1,0:T(8,128)(2,1)S(1)}, bf16[512,768]{1,0:T(8,128)(2,1)}, u32[]{:S(2)}) copy-start(bf16[512,768]{1,0:T(8,128)(2,1)} %get-tuple-element.84) | copy-start | bytes 2359300
  205.2 13.5 %collective-permute-start.30 = (bf16[64,768]{1,0:T(8,128)(2,1)S(1)}, bf16[64,768]{1,0:T(8,128)(2,1)S(1)}, u32[]{:S(2)}, u32[]{:S(2)}) collective-permute-start(bf16[64,768]{1,0:T(8,128)(2,1)S(1)} %pad_maximum_fusion.4.refs_6_), channel_id=1, source_target_pairs={{0,2},{1,3},{2,0},{3,1},{4,6},{5,7},{6,4},{7,5},{8,10},{9,11},{10,... | collective-permute-start | bytes 294920 | tf_op jit(solution)/shard_map/ppermute | solution.py:394
  209.4 7.9 %collective-permute-start.19 = (f32[2,768]{1,0:T(2,128)S(1)}, f32[2,768]{1,0:T(2,128)S(1)}, u32[]{:S(2)}, u32[]{:S(2)}) collective-permute-start(f32[2,768]{1,0:T(2,128)S(1)} %slice_bitcast_fusion.3), channel_id=1, source_target_pairs={{0,8},{8,0},{16,24},{24,16},{1,9},{9,1},{17,25},{25,17},{2,10},{10... | collective-permute-start | bytes 18440 | tf_op jit(solution)/shard_map/ppermute | solution.py:394
  210.2 80.9 %collective-permute-start.24 = (bf16[256,768]{1,0:T(8,128)(2,1)}, bf16[256,768]{1,0:T(8,128)(2,1)}, u32[]{:S(2)}, u32[]{:S(2)}) collective-permute-start(bf16[256,768]{1,0:T(8,128)(2,1)} %pad_maximum_fusion), channel_id=1, source_target_pairs={{0,1},{1,0},{2,3},{3,2},{4,5},{5,4},{6,7},{7,6},{8,9},{9,8},{10,11... | collective-permute-start | bytes 1179656 | tf_op jit(solution)/shard_map/ppermute | solution.py:394
  212.8 82.0 %collective-permute-start.12 = (bf16[512,768]{1,0:T(8,128)(2,1)}, bf16[512,768]{1,0:T(8,128)(2,1)}, u32[]{:S(2)}, u32[]{:S(2)}) collective-permute-start(bf16[512,768]{1,0:T(8,128)(2,1)} %add_convert_fusion.1), channel_id=1, source_target_pairs={{0,16},{8,24},{16,0},{24,8},{1,17},{9,25},{17,1},{25,9},{2,18},{10... | collective-permute-start | bytes 2359304 | tf_op jit(solution)/shard_map/ppermute | solution.py:394
  215.5 68.3 %copy-start.16 = (f32[768]{0:T(1024)S(1)}, f32[768]{0:T(1024)}, u32[]{:S(2)}) copy-start(f32[768]{0:T(1024)} %refs_2_.3) | copy-start | bytes 9220
  215.5 79.3 %copy-start = (bf16[1024,768]{1,0:T(8,128)(2,1)}, bf16[1024,768]{1,0:T(8,128)(2,1)S(1)}, u32[]{:S(2)}) copy-start(bf16[1024,768]{1,0:T(8,128)(2,1)S(1)} %collective-permute-done.9.refs_5_) | copy-start | bytes 4718596
  215.5 79.3 %collective-permute-start.14 = (bf16[512,768]{1,0:T(8,128)(2,1)}, bf16[512,768]{1,0:T(8,128)(2,1)S(1)}, u32[]{:S(2)}, u32[]{:S(2)}) collective-permute-start(bf16[512,768]{1,0:T(8,128)(2,1)} %add_convert_fusion), channel_id=1, source_target_pairs={{0,16},{8,24},{16,0},{24,8},{1,17},{9,25},{17,1},{25,9},{2,18},{10... | collective-permute-start | bytes 2359304 | tf_op jit(solution)/shard_map/ppermute | solution.py:394
  217.3 87.9 %collective-permute-start.10 = (bf16[512,768]{1,0:T(8,128)(2,1)}, bf16[512,768]{1,0:T(8,128)(2,1)S(1)}, u32[]{:S(2)}, u32[]{:S(2)}) collective-permute-start(bf16[512,768]{1,0:T(8,128)(2,1)} %add_convert_fusion.2), channel_id=1, source_target_pairs={{0,16},{8,24},{16,0},{24,8},{1,17},{9,25},{17,1},{25,9},{2,18},{10... | collective-permute-start | bytes 2359304 | tf_op jit(solution)/shard_map/ppermute | solution.py:394
  219.4 47.2 %collective-permute-start.20 = (f32[2,768]{1,0:T(2,128)S(1)}, f32[2,768]{1,0:T(2,128)S(1)}, u32[]{:S(2)}, u32[]{:S(2)}) collective-permute-start(f32[2,768]{1,0:T(2,128)S(1)} %fusion), channel_id=1, source_target_pairs={{0,16},{8,24},{16,0},{24,8},{1,17},{9,25},{17,1},{25,9},{2,18},{10... | collective-permute-start | bytes 18440 | tf_op jit(solution)/shard_map/ppermute | solution.py:394
  266.6 15.6 %collective-permute-start.31 = (bf16[64,768]{1,0:T(8,128)(2,1)S(1)}, bf16[64,768]{1,0:T(8,128)(2,1)S(1)}, u32[]{:S(2)}, u32[]{:S(2)}) collective-permute-start(bf16[64,768]{1,0:T(8,128)(2,1)S(1)} %pad_maximum_fusion.4.refs_6_), channel_id=1, source_target_pairs={{0,4},{1,5},{2,6},{3,7},{4,0},{5,1},{6,2},{7,3},{8,12},{9,13},{10,... | collective-permute-start | bytes 294920 | tf_op jit(solution)/shard_map/ppermute | solution.py:394
  282.2 8.9 %collective-permute-start.32 = (bf16[64,768]{1,0:T(8,128)(2,1)S(1)}, bf16[64,768]{1,0:T(8,128)(2,1)S(1)}, u32[]{:S(2)}, u32[]{:S(2)}) collective-permute-start(bf16[64,768]{1,0:T(8,128)(2,1)S(1)} %pad_maximum_fusion.4.refs_6_), channel_id=1, source_target_pairs={{0,6},{1,7},{2,4},{3,5},{4,2},{5,3},{6,0},{7,1},{8,14},{9,15},{10,... | collective-permute-start | bytes 294920 | tf_op jit(solution)/shard_map/ppermute | solution.py:394
  (16 other events, 47.1 us)
Sparse Core Ops, SparseCore 0:
  162.3 136.8 all-reduce.1
where the time goes:
time: 317 us
  Pallas kernels  126 us (40%)
  waiting for transfers between devices  113 us (36%)
  starting transfers between devices  38.5 us (12%)
  between operations  14.4 us (5%)
  other arithmetic  13.4 us (4%)
  local copies, waits for them, and re-layouts  11.3 us (4%)
    pallas_call x8, Pallas kernels, call(): pl.pallas_call(kernel, out_shape=[jax.ShapeDtypeStruct(s, d) for s, d in...  117 us
    ppermute x33, waiting for transfers between devices, swap(): return lax.ppermute(v, axis, [(i, i ^ mask) for i in range(count)])  113 us
    ppermute x33, starting transfers between devices, swap(): return lax.ppermute(v, axis, [(i, i ^ mask) for i in range(count)])  38.5 us
    pallas_call x2, Pallas kernels, finish(): pl.pallas_call(functools.partial(final_kernel, end - begin), grid=(end -...  8.78 us
    unnamed x60, local copies, waits for them, and re-layouts  6.45 us
  transfers between devices with their start and end apart: 34, of which 15 were waited for; matrix products, arithmetic and copies ran while one was open for 6% of the time, Pallas kernels for 17%

commit v1 on v0

--- a/solution.py
+++ b/solution.py
@@ -151,23 +151,38 @@
     refs = list(refs)
     take = lambda n: [refs.pop(0) for _ in range(n)]
     length, pos = take(2)
+    parts = take(blocks)
     ff_parts = take(4)
     prior = [] if first else take(1)
-    packs = take(blocks)
     wqkv, wproj, qg, kg = take(4)
     prior_gain = [] if first else take(1)
     ff_small = take(1) if last else []
     keep_near, keep_far, send = take(3)
     if last:
-        pieces = take(len(refs) - 22)
+        pieces = take(len(refs) - 26)
         (small,) = take(1)
     else:
         acc, accg = take(2)
-    jt, dot_s, qs_t, q_s, k_s, kt_s, v_s, vt_s, es, dqt, dk, dv, ot, djt = take(14)
-    ff_s, ff_sem, prior_sem, out_s, out_sem = take(5)
+    jt, dot_s, qs_t, qt_s, k_s, kt_s, v_s, vt_s, es, dqt, dk, dv, ot, djt = take(14)
+    ff_s, ff_sem, prior_sem, out_s, out_sem, dot_bs, r_s, pack_s, pack_sem = take(9)
     if last:
         acc, accg = take(2)
-    rows = packs[0].shape[0] // 2
+    rows = parts[0].shape[0] // 2
+    joined = wqkv.shape[0]
+    total = rows * blocks
+    scale = size**-0.5
+    up = scale * math.log2(math.e)
+    for k in range(blocks):
+        pltpu.make_async_copy(parts[k], pack_s.at[k], pack_sem.at[k]).start()
+
+    def project(k, carry):
+        pltpu.make_async_copy(parts[0], pack_s.at[k], pack_sem.at[k]).wait()
+        cols = pl.ds(pl.multiple_of(k * rows, rows), rows)
+        jt[:, cols] = mm(wqkv[...], pack_s[k, 0:rows], NT)
+        dot_s[:, cols] = mm(wproj[...], pack_s[k, rows : 2 * rows], NT)
+        return carry
+
+    lax.fori_loop(0, blocks, project, 0)
     later = []
     for k in range(4):
         rows_of = pl.ds(starts[k // 2], 2 * rows)
@@ -176,16 +191,8 @@
     if prior:
         later.append(pltpu.make_async_copy(prior[0], acc, prior_sem))
         later[-1].start()
-    xs = [p.at[0:rows] for p in packs]
-    gs = [p.at[rows : 2 * rows] for p in packs]
-    joined = wqkv.shape[0]
-    total = rows * blocks
-    scale = size**-0.5
-    up = scale * math.log2(math.e)
-    for k in range(blocks):
-        cols = slice(k * rows, (k + 1) * rows)
-        jt[:, cols] = mm(wqkv[...], xs[k][...], NT)
-        dot_s[:, cols] = mm(wproj[...], gs[k][...], NT)
+    else:
+        acc[...] = jnp.zeros(acc.shape, F32)
 
     def normed(u):
         c = u - jnp.mean(u, axis=0, keepdims=True)
@@ -204,7 +211,7 @@
         kt = normed(part(1))[0] * kg[gh, :]
         vt = part(2)
         qs_t[h] = (qt * up).astype(BF16)
-        q_s[h] = qt.T.astype(BF16)
+        qt_s[h] = qt.astype(BF16)
         k_s[h] = kt.T.astype(BF16)
         v_s[h] = vt.T.astype(BF16)
         for k in range(blocks):
@@ -222,46 +229,52 @@
     dk[...] = jnp.zeros(dk.shape, F32)
     dv[...] = jnp.zeros(dv.shape, F32)
 
-    def head(h, carry):
-        def forward(j, acc):
-            b = j ^ pos[0]
-            start = pl.multiple_of(b * rows, rows)
+    def forward(j, accs):
+        b = j ^ pos[0]
+        start = pl.multiple_of(b * rows, rows)
+        slot = lax.broadcasted_iota(jnp.int32, (rows, 1), 0) + j * rows
+        out = []
+        for h in range(heads):
             s = mm(k_s[h, pl.ds(start, rows), :], qs_t[h])
-            slot = lax.broadcasted_iota(jnp.int32, (rows, 1), 0) + j * rows
             e = jnp.where(slot < live, jnp.exp2(s), 0.0).astype(BF16)
-            es[b] = e
-            return acc + mm(vt_s[h, b], e)
-
-        acc = lax.fori_loop(0, count, forward, jnp.zeros((size + 16, total), F32))
-        inv = 1.0 / acc[size : size + 1]
-        o = acc[0:size] * inv
-        hs = pl.ds(pl.multiple_of(h * size, size), size)
-        ot[hs, :] = o.astype(BF16)
-        dof = dot_s[hs, :] * inv
-        dot_b = dof.astype(BF16)
-        do_b = dof.T.astype(BF16)
-        r = jnp.sum(dot_b.astype(F32) * o, axis=0, keepdims=True)
-        q_h = q_s[h]
-
-        def backward(j, acc):
-            b = j ^ pos[0]
-            start = pl.multiple_of(b * rows, rows)
+            es[h, b] = e
+            out.append(accs[h] + mm(vt_s[h, b], e))
+        return tuple(out)
+
+    zero = jnp.zeros((size + 16, total), F32)
+    accs = lax.fori_loop(0, count, forward, (zero,) * heads)
+    for h in range(heads):
+        inv = 1.0 / accs[h][size : size + 1]
+        o = accs[h][0:size] * inv
+        hs = slice(h * size, (h + 1) * size)
+        ot[hs] = o.astype(BF16)
+        dot_b = (dot_s[hs] * inv).astype(BF16)
+        dot_bs[hs] = dot_b
+        r_s[h : h + 1] = jnp.sum(dot_b.astype(F32) * o, axis=0, keepdims=True)
+
+    def backward(j, accs):
+        b = j ^ pos[0]
+        start = pl.multiple_of(b * rows, rows)
+        out = []
+        for h in range(heads):
+            dot_b = dot_bs[h * size : (h + 1) * size]
             dp = mm(v_s[h, pl.ds(start, rows), :], dot_b)
-            e = es[b]
-            ds = (e.astype(F32) * (dp - r)).astype(BF16)
-            dv[h, pl.ds(start, rows), :] = mm(e, do_b)
-            dk[h, pl.ds(start, rows), :] = mm(ds, q_h)
-            return acc + mm(kt_s[h, b], ds)
-
-        dqt[h] = lax.fori_loop(0, count, backward, jnp.zeros((size, total), F32))
-        return carry
-
-    lax.fori_loop(0, heads, head, 0)
+            e = es[h, b]
+            ds = (e.astype(F32) * (dp - r_s[h : h + 1])).astype(BF16)
+            dv[h, b] = mm(dot_b, e, NT)
+            dk[h, b] = mm(qt_s[h], ds, NT)
+            out.append(accs[h] + mm(kt_s[h, b], ds))
+        return tuple(out)
+
+    zero = jnp.zeros((size, total), F32)
+    accs = lax.fori_loop(0, count, backward, (zero,) * heads)
+    for h in range(heads):
+        dqt[h] = accs[h]
 
     def undo(h, carry):
         base = pl.multiple_of(h * 3 * size, size)
         gh = pl.multiple_of(h * size, size)
-        for c, gain, grad in ((0, qg, dqt[h]), (1, kg, dk[h].T)):
+        for c, gain, grad in ((0, qg, dqt[h]), (1, kg, jnp.concatenate([dk[h, k] for k in range(blocks)], axis=1))):
             at = pl.ds(pl.multiple_of(base + c * size, size), size)
             n, r = normed(jt[at, :])
             grad = grad * scale
@@ -273,7 +286,8 @@
             )
             djt[at, :] = back.astype(BF16)
             accg[pl.ds(pl.multiple_of(c * heads * size + gh, size), size), :] = jnp.sum(grad * n, axis=1, keepdims=True)
-        djt[pl.ds(pl.multiple_of(base + 2 * size, size), size), :] = dv[h].T.astype(BF16)
+        values = jnp.concatenate([dv[h, k] for k in range(blocks)], axis=1)
+        djt[pl.ds(pl.multiple_of(base + 2 * size, size), size), :] = values.astype(BF16)
         return carry
 
     lax.fori_loop(0, heads, undo, 0)
@@ -293,6 +307,8 @@
         o = ff_s[0, k >> 1, part, :].astype(F32) + mm(ot[:, cols], wproj[...], TN)
         out_s[k, 0:rows] = o.astype(BF16)
         out_s[k, rows : 2 * rows] = n.astype(BF16)
+        acc[0:joined] += mm(djt[:, cols], pack_s[k, 0:rows])
+        acc[joined:] += mm(ot[:, cols], pack_s[k, rows : 2 * rows])
         for j in range(blocks):
 
             @pl.when(k == j)
@@ -302,20 +318,8 @@
         return carry
 
     lax.fori_loop(0, blocks, give, 0)
-    tq = tp = None
-    for k in range(blocks):
-        cols = slice(k * rows, (k + 1) * rows)
-        p = mm(djt[:, cols], xs[k][...])
-        tq = p if tq is None else tq + p
-        p = mm(ot[:, cols], gs[k][...])
-        tp = p if tp is None else tp + p
-    if prior:
-        tq = tq + acc[0:joined]
-        tp = tp + acc[joined:]
-    acc[0:joined] = tq
-    acc[joined:] = tp
     if last:
-        ln = jnp.sum(wqkv[...].astype(F32) * tq, axis=0, keepdims=True) + ff_small[0][2:3]
+        ln = jnp.sum(wqkv[...].astype(F32) * acc[0:joined], axis=0, keepdims=True) + ff_small[0][2:3]
         gain_row = as_row(accg[...])
         pad = jnp.zeros((1, ln.shape[1] - gain_row.shape[1]), F32)
         lines = [jnp.concatenate([gain_row, pad], axis=1), ff_small[0][0:2], ln, jnp.zeros((4, ln.shape[1]), F32)]
@@ -460,20 +464,24 @@
             pltpu.VMEM((joined, total), F32),
             pltpu.VMEM((inner, total), F32),
             pltpu.VMEM((heads, size, total), BF16),
-            pltpu.VMEM((heads, total, size), BF16),
+            pltpu.VMEM((heads, size, total), BF16),
             pltpu.VMEM((heads, total, size), BF16),
             pltpu.VMEM((heads, blocks, size, rows), BF16),
             pltpu.VMEM((heads, total, size), BF16),
             pltpu.VMEM((heads, blocks, size + 16, rows), BF16),
-            pltpu.VMEM((blocks, rows, total), BF16),
+            pltpu.VMEM((heads, blocks, rows, total), BF16),
             pltpu.VMEM((heads, size, total), F32),
-            pltpu.VMEM((heads, total, size), F32),
-            pltpu.VMEM((heads, total, size), F32),
+            pltpu.VMEM((heads, blocks, size, rows), F32),
+            pltpu.VMEM((heads, blocks, size, rows), F32),
             pltpu.VMEM((inner, total), BF16),
             pltpu.VMEM((joined, total), BF16),
             pltpu.VMEM((2, 2, 2 * rows, width), BF16),
             pltpu.SemaphoreType.DMA((4,)),
             pltpu.SemaphoreType.DMA,
+            pltpu.VMEM((blocks, 2 * rows, width), BF16),
+            pltpu.SemaphoreType.DMA((blocks,)),
+            pltpu.VMEM((inner, total), BF16),
+            pltpu.VMEM((8, total), F32),
             pltpu.VMEM((blocks, 2 * rows, width), BF16),
             pltpu.SemaphoreType.DMA((blocks,)),
         ]
@@ -484,8 +492,8 @@
             outs += [((joined + inner, width), F32), ((2 * inner, 1), F32)]
         res = call(
             functools.partial(att_kernel, first, last, blocks, heads, size, starts), outs, 2,
-            lengths[i : i + 1], att_pos, *ff_parts, *state[:1], own[i], near[i], far[i], cross[i],
-            w_t, w_proj, qg, kg, *state[1:], *ff_small, n_any=4 + len(state[:1]), any_outs=3,
+            lengths[i : i + 1], att_pos, own[i], near[i], far[i], cross[i], *ff_parts, *state[:1],
+            w_t, w_proj, qg, kg, *state[1:], *ff_small, n_any=blocks + 4 + len(state[:1]), any_outs=3,
             scratch=scratch,
             flops=6 * 8 * heads * total * total * size + 8 * total * width * (joined + inner),
         )

time: 317 us -> 309 us (0.975)
  starting transfers between devices: 38.5 us -> 32.2 us
    ppermute x33, starting transfers between devices: 38.5 us -> 32.2 us  [swap(): return lax.ppermute(v, axis, [(i, i ^ mask) for i in range(count)])]
  transfers between devices with their start and end apart: 34 -> 34, of which waited for: 15 -> 15; matrix products, arithmetic and copies ran while one was open for 6% -> 6% of each run, Pallas kernels for 17% -> 18%
where the time goes in v1:
time: 309 us; the launch traced here: 308 us
  Pallas kernels  124 us (40%)
  waiting for transfers between devices  115 us (37%)
  starting transfers between devices  32.2 us (10%)
  between operations  14.4 us (5%)
  other arithmetic  13.6 us (4%)
  local copies, waits for them, and re-layouts  9.85 us (3%)
    ppermute x33, waiting for transfers between devices, swap(): return lax.ppermute(v, axis, [(i, i ^ mask) for i in range(count)])  115 us
    pallas_call x8, Pallas kernels, call(): pl.pallas_call(kernel, out_shape=[jax.ShapeDtypeStruct(s, d) for s, d in...  115 us
    ppermute x33, starting transfers between devices, swap(): return lax.ppermute(v, axis, [(i, i ^ mask) for i in range(count)])  32.2 us
    pallas_call x2, Pallas kernels, finish(): pl.pallas_call(functools.partial(final_kernel, end - begin), grid=(end -...  8.78 us
  transfers between devices with their start and end apart: 34, of which 15 were waited for; matrix products, arithmetic and copies ran while one was open for 6% of the time, Pallas kernels for 18%

profile of v1, /device:TPU:0, one launch (start us, length us, event | category | flops | bytes accessed | tf_op | source)
XLA Modules:
  0.0 308.4 jit_solution(12932909544279884980)
XLA Ops:
  7.2 4.0 %shard_map.203 = (bf16[512,768]{1,0:T(8,128)(2,1)}, bf16[512,768]{1,0:T(8,128)(2,1)}, bf16[512,768]{1,0:T(8,128)(2,1)}) custom-call(bf16[3,256,768]{2,1,0:T(8,128)(2,1)} %refs_0_.3, bf16[3,256,768]{2,1,0:T(8,128)(2,1)} %refs_1_.3, f32[768]{0:T(1024)} %refs_2_.3), custom_call_target="tpu_custom_call" | custom-call | bytes 4721664 | tf_op jit(solution)/shard_map/pallas_call | solution.py:31
  12.4 2.6 collective-permute-start.3
  15.1 1.0 collective-permute-done.4.refs_3_
  16.1 0.9 copy-done.25
  17.0 19.3 %shard_map.204 = (bf16[1536,768]{1,0:T(8,128)(2,1)}, bf16[1536,768]{1,0:T(8,128)(2,1)}, f32[1536,768]{1,0:T(8,128)}, f32[8,768]{1,0:T(8,128)}) custom-call(bf16[512,768]{1,0:T(8,128)(2,1)} %get-tuple-element.56.refs_0_.refs_2_, bf16[512,768]{1,0:T(8,128)(2,1)} %collective-permute-done.2.refs_1_.refs_3_, bf16[512,768]{1,0:T(8,128)(2,1)} %get-tuple-element.57.refs_2_, ...), custom_call_target="tpu_custom_call" | custom-call | flops 10871635968 | bytes 16542720 | tf_op jit(solution)/shard_map/pallas_call | solution.py:31
  36.8 2.6 collective-permute-start.1
  40.3 0.8 reshape.37.refs_13_.refs_14_
  42.3 9.4 %shard_map.205 = (bf16[512,768]{1,0:T(8,128)(2,1)}, bf16[512,768]{1,0:T(8,128)(2,1)}, f32[1536,768]{1,0:T(8,128)}, f32[8,768]{1,0:T(8,128)}) custom-call(bf16[512,768]{1,0:T(8,128)(2,1)} %collective-permute-done.3.refs_0_.refs_4_, bf16[512,768]{1,0:T(8,128)(2,1)} %collective-permute-done.5.refs_1_.refs_5_, f32[1536,768]{1,0:T(8,128)} %get-tuple-element.61.refs_2_, ...), custom_call_target="tpu_custom_call" | custom-call | flops 3623878656 | bytes 14994432 | tf_op jit(solution)/shard_map/pallas_call | solution.py:31
  51.7 17.5 %shard_map.206 = (bf16[512,768]{1,0:T(8,128)(2,1)}, bf16[512,768]{1,0:T(8,128)(2,1)}, bf16[1024,768]{1,0:T(8,128)(2,1)}, f32[768,768]{1,0:T(8,128)}, f32[384,1]{1,0:T(8,128)}) custom-call(s32[1]{0:T(128)} %get-tuple-element.113.refs_0_, s32[3]{0:T(128)} %pad_add_fusion.refs_1_, bf16[512,768]{1,0:T(8,128)(2,1)} %get-tuple-element.56.refs_0_.refs_2_, ...), custom_call_target="tpu_custom_call" | custom-call | flops 14495514624 | bytes 16124944 | tf_op jit(solution)/shard_map/pallas_call | solution.py:31
  69.4 4.9 %collective-permute-done.7.refs_0_.refs_4_ = bf16[512,768]{1,0:T(8,128)(2,1)S(1)} collective-permute-done((bf16[512,768]{1,0:T(8,128)(2,1)S(1)}, bf16[512,768]{1,0:T(8,128)(2,1)S(1)}, u32[]{:S(2)}, u32[]{:S(2)}) %collective-permute-start.7) | collective-permute-done | bytes 786464 | tf_op jit(solution)/shard_map/ppermute | solution.py:398
  74.4 2.3 collective-permute-done.8.refs_1_.refs_5_
  76.6 0.9 copy-done.29
  77.5 13.7 %shard_map.207 = (bf16[1024,768]{1,0:T(8,128)(2,1)}, bf16[1024,768]{1,0:T(8,128)(2,1)}, bf16[1536,768]{1,0:T(8,128)(2,1)}, f32[8,768]{1,0:T(8,128)}) custom-call(bf16[512,768]{1,0:T(8,128)(2,1)} %copy-done.27, bf16[512,768]{1,0:T(8,128)(2,1)} %copy-done.29, bf16[512,768]{1,0:T(8,128)(2,1)} %copy-done.26, bf16[512,768]{1,0:T(8,128)(2,1)} %copy-done.28, ...), custom_call_target="tpu_custom_call" | custom-call | flops 7247757312 | bytes 15780864 | tf_op jit(solution)/shard_map/pallas_call | solution.py:31
  91.2 22.6 %shard_map.208 = (bf16[512,768]{1,0:T(8,128)(2,1)}, bf16[512,768]{1,0:T(8,128)(2,1)}, bf16[1024,768]{1,0:T(8,128)(2,1)}, f32[768,768]{1,0:T(8,128)}, f32[384,1]{1,0:T(8,128)}) custom-call(s32[1]{0:T(128)} %get-tuple-element.111.refs_0_, s32[3]{0:T(128)} %pad_add_fusion.refs_1_, bf16[512,768]{1,0:T(8,128)(2,1)} %get-tuple-element.57.refs_2_, ...), custom_call_target="tpu_custom_call" | custom-call | flops 14495514624 | bytes 20058640 | tf_op jit(solution)/shard_map/pallas_call | solution.py:31
  113.8 25.3 %shard_map.209 = (bf16[512,768]{1,0:T(8,128)(2,1)}, bf16[512,768]{1,0:T(8,128)(2,1)}, bf16[1024,768]{1,0:T(8,128)(2,1)}, f32[256,768]{1,0:T(8,128)}, bf16[264,76...) custom-call(s32[1]{0:T(128)} %get-tuple-element.112.refs_0_, ...), custom_call_target="tpu_custom_call" | custom-call | flops 14495514624 | bytes 19418128 | tf_op jit(solution)/shard_map/pallas_call | solution.py:31
  139.1 3.0 collective-permute-start.27
  142.1 1.8 collective-permute-start.26
  144.4 1.7 collective-permute-done.27
  146.2 6.2 %collective-permute-done.26 = bf16[64,768]{1,0:T(8,128)(2,1)S(1)} collective-permute-done((bf16[64,768]{1,0:T(8,128)(2,1)}, bf16[64,768]{1,0:T(8,128)(2,1)S(1)}, u32[]{:S(2)}, u32[]{:S(2)}) %collective-permute-start.26) | collective-permute-done | bytes 98336 | tf_op jit(solution)/shard_map/ppermute | solution.py:398
  152.4 1.0 convert_add_fusion.1
  154.6 2.9 collective-permute-done.28
  157.7 1.4 convert_add_fusion
  160.0 3.0 collective-permute-start.18
  162.9 1.5 collective-permute-start.16
  164.4 5.5 %collective-permute-done.18 = bf16[72,768]{1,0:T(8,128)(2,1)S(1)} collective-permute-done((bf16[72,768]{1,0:T(8,128)(2,1)S(1)}, bf16[72,768]{1,0:T(8,128)(2,1)S(1)}, u32[]{:S(2)}, u32[]{:S(2)}) %collective-permute-start.18) | collective-permute-done | bytes 110624 | tf_op jit(solution)/shard_map/ppermute | solution.py:398
  169.9 12.8 %collective-permute-done.17 = bf16[72,768]{1,0:T(8,128)(2,1)S(1)} collective-permute-done((bf16[72,768]{1,0:T(8,128)(2,1)S(1)}, bf16[72,768]{1,0:T(8,128)(2,1)S(1)}, u32[]{:S(2)}, u32[]{:S(2)}) %collective-permute-start.17) | collective-permute-done | bytes 110624 | tf_op jit(solution)/shard_map/ppermute | solution.py:398
  182.9 2.5 collective-permute-start.22
  185.5 6.9 %collective-permute-done.21.refs_2_ = bf16[64,768]{1,0:T(8,128)(2,1)S(1)} collective-permute-done((bf16[64,768]{1,0:T(8,128)(2,1)S(1)}, bf16[64,768]{1,0:T(8,128)(2,1)S(1)}, u32[]{:S(2)}, u32[]{:S(2)}) %collective-permute-start.21) | collective-permute-done | bytes 98336 | tf_op jit(solution)/shard_map/ppermute | solution.py:398
  192.4 2.2 collective-permute-start.23
  194.6 2.3 collective-permute-done.22.refs_3_
  196.9 4.0 %collective-permute-done.23.refs_4_ = bf16[64,768]{1,0:T(8,128)(2,1)S(1)} collective-permute-done((bf16[64,768]{1,0:T(8,128)(2,1)S(1)}, bf16[64,768]{1,0:T(8,128)(2,1)S(1)}, u32[]{:S(2)}, u32[]{:S(2)}) %collective-permute-start.23) | collective-permute-done | bytes 98336 | tf_op jit(solution)/shard_map/ppermute | solution.py:398
  201.8 2.3 collective-permute-start.24
  204.1 1.1 add_convert_fusion.1
  205.2 1.9 collective-permute-start.12
  207.2 1.2 add_convert_fusion
  208.6 1.3 add_convert_fusion.2
  209.8 1.8 collective-permute-start.10
  213.9 45.2 %collective-permute-done.20 = f32[2,768]{1,0:T(2,128)S(1)} collective-permute-done((f32[2,768]{1,0:T(2,128)S(1)}, f32[2,768]{1,0:T(2,128)S(1)}, u32[]{:S(2)}, u32[]{:S(2)}) %collective-permute-start.20) | collective-permute-done | bytes 6176 | tf_op jit(solution)/shard_map/ppermute | solution.py:398
  259.1 2.5 collective-permute-start.31
  262.3 11.9 %collective-permute-done.31.refs_8_ = bf16[64,768]{1,0:T(8,128)(2,1)S(1)} collective-permute-done((bf16[64,768]{1,0:T(8,128)(2,1)S(1)}, bf16[64,768]{1,0:T(8,128)(2,1)S(1)}, u32[]{:S(2)}, u32[]{:S(2)}) %collective-permute-start.31) | collective-permute-done | bytes 98336 | tf_op jit(solution)/shard_map/ppermute | solution.py:398
  274.1 0.9 collective-permute-start.32
  276.2 6.8 %collective-permute-done.32.refs_9_ = bf16[64,768]{1,0:T(8,128)(2,1)S(1)} collective-permute-done((bf16[64,768]{1,0:T(8,128)(2,1)S(1)}, bf16[64,768]{1,0:T(8,128)(2,1)S(1)}, u32[]{:S(2)}, u32[]{:S(2)}) %collective-permute-start.32) | collective-permute-done | bytes 98336 | tf_op jit(solution)/shard_map/ppermute | solution.py:398
  283.7 3.0 shard_map.212
  286.7 0.9 copy-done.5
  287.7 5.2 %shard_map.210 = (bf16[3,256,768]{2,1,0:T(8,128)(2,1)}, f32[3,256,768]{2,1,0:T(8,128)}) custom-call(bf16[3,256,768]{2,1,0:T(8,128)(2,1)} %refs_0_.3, bf16[3,256,768]{2,1,0:T(8,128)(2,1)} %refs_1_.3, f32[768]{0:T(1024)} %refs_2_.3, f32[768]{0:T(1024)} %refs_3_.5, bf16[512,768]{1,0:T(8,128)(2,1)} %get-tuple-element.79.refs_4_, bf16[1024,768]{1,0:T(8,128)(2,1)} %copy-done.1, ...), custom_call_target="tpu_custom_call" | custom-call | tf_op jit(solution)/shard_map/pallas_call | solution.py:575
  292.9 4.2 %slice_convert_fusion = (f32[768,768]{1,0:T(8,128)}, f32[768,768]{1,0:T(8,128)}) fusion(bf16[1536,768]{1,0:T(8,128)(2,1)} %all-reduce.2.cloned.1.call-done), kind=kLoop, calls=%fused_computation.3 | loop fusion | flops 1179648 | bytes 7077888 | tf_op jit(solution)/shard_map/convert_element_type | solution.py:566
  297.1 0.9 copy-done.4
  298.0 3.5 %shard_map.211 = (bf16[3,256,768]{2,1,0:T(8,128)(2,1)}, f32[3,256,768]{2,1,0:T(8,128)}) custom-call(bf16[3,256,768]{2,1,0:T(8,128)(2,1)} %refs_0_.3, bf16[3,256,768]{2,1,0:T(8,128)(2,1)} %refs_1_.3, f32[768]{0:T(1024)} %refs_2_.3, f32[768]{0:T(1024)} %refs_3_.5, ...), custom_call_target="tpu_custom_call", output_to_operand_aliasing={{0}: (7, {}), {1}: (8, {})} | custom-call | tf_op jit(solution)/shard_map/pallas_call | solution.py:575
  (125 shorter events, 12.8 us)
Async XLA Ops:
  7.2 285.7 %all-reduce.2.cloned.1.call-start = ((), (), s32[]{:S(2)}) async-start(), calls=%async_computation | async-start | bytes 4718592 | tf_op jit(solution)/shard_map/psum | solution.py:551
  11.2 3.7 %collective-permute-start = (bf16[512,768]{1,0:T(8,128)(2,1)}, bf16[512,768]{1,0:T(8,128)(2,1)S(1)}, u32[]{:S(2)}, u32[]{:S(2)}) collective-permute-start(bf16[512,768]{1,0:T(8,128)(2,1)} %get-tuple-element.55.refs_4_.refs_2_), channel_id=1, source_target_pairs={{0,8},{8,0},{16,24},{24,16},{1,9},{9,1},{17,25},{25,17},{2,10},{10... | collective-permute-start | bytes 2359304 | tf_op jit(solution)/shard_map/ppermute | solution.py:398
  11.8 3.4 %collective-permute-start.2 = (bf16[512,768]{1,0:T(8,128)(2,1)}, bf16[512,768]{1,0:T(8,128)(2,1)}, u32[]{:S(2)}, u32[]{:S(2)}) collective-permute-start(bf16[512,768]{1,0:T(8,128)(2,1)} %get-tuple-element.56.refs_0_.refs_2_), channel_id=1, source_target_pairs={{0,8},{8,0},{16,24},{24,16},{1,9},{9,1},{17,25},{25,17},{2,10},{10... | collective-permute-start | bytes 2359304 | tf_op jit(solution)/shard_map/ppermute | solution.py:398
  11.8 24.9 %copy-start.22 = (bf16[512,768]{1,0:T(8,128)(2,1)S(1)}, bf16[512,768]{1,0:T(8,128)(2,1)}, u32[]{:S(2)}) copy-start(bf16[512,768]{1,0:T(8,128)(2,1)} %get-tuple-element.55.refs_4_.refs_2_) | copy-start | bytes 2359300
  11.8 27.6 %copy-start.24 = (bf16[512,768]{1,0:T(8,128)(2,1)S(1)}, bf16[512,768]{1,0:T(8,128)(2,1)}, u32[]{:S(2)}) copy-start(bf16[512,768]{1,0:T(8,128)(2,1)} %get-tuple-element.57.refs_2_) | copy-start | bytes 2359300
  11.8 27.6 %copy-start.19 = (f32[3,64]{1,0:T(4,128)S(1)}, f32[3,64]{1,0:T(4,128)}, u32[]{:S(2)}) copy-start(f32[3,64]{1,0:T(4,128)} %param.16) | copy-start | bytes 2308
  11.8 28.4 %copy-start.20 = (f32[3,64]{1,0:T(4,128)S(1)}, f32[3,64]{1,0:T(4,128)}, u32[]{:S(2)}) copy-start(f32[3,64]{1,0:T(4,128)} %param.17) | copy-start | bytes 2308
  11.8 29.9 %copy-start.18 = (s32[3]{0:T(128)S(1)}, s32[3]{0:T(128)}, u32[]{:S(2)}) copy-start(s32[3]{0:T(128)} %param.13) | copy-start | bytes 40
  11.9 4.3 %collective-permute-start.4 = (bf16[512,768]{1,0:T(8,128)(2,1)}, bf16[512,768]{1,0:T(8,128)(2,1)S(1)}, u32[]{:S(2)}, u32[]{:S(2)}) collective-permute-start(bf16[512,768]{1,0:T(8,128)(2,1)} %get-tuple-element.57.refs_2_), channel_id=1, source_target_pairs={{0,8},{8,0},{16,24},{24,16},{1,9},{9,1},{17,25},{25,17},{2,10},{10... | collective-permute-start | bytes 2359304 | tf_op jit(solution)/shard_map/ppermute | solution.py:398
  12.4 24.0 %collective-permute-start.3 = (bf16[512,768]{1,0:T(8,128)(2,1)}, bf16[512,768]{1,0:T(8,128)(2,1)}, u32[]{:S(2)}, u32[]{:S(2)}) collective-permute-start(bf16[512,768]{1,0:T(8,128)(2,1)} %get-tuple-element.56.refs_0_.refs_2_), channel_id=1, source_target_pairs={{0,16},{8,24},{16,0},{24,8},{1,17},{9,25},{17,1},{25,9},{2,18},{10... | collective-permute-start | bytes 2359304 | tf_op jit(solution)/shard_map/ppermute | solution.py:398
  36.3 6.0 %collective-permute-start.5 = (bf16[512,768]{1,0:T(8,128)(2,1)}, bf16[512,768]{1,0:T(8,128)(2,1)}, u32[]{:S(2)}, u32[]{:S(2)}) collective-permute-start(bf16[512,768]{1,0:T(8,128)(2,1)} %collective-permute-done.3.refs_0_.refs_4_), channel_id=1, source_target_pairs={{0,8},{8,0},{16,24},{24,16},{1,9},{9,1},{17,25},{25,17},{2,10},{10... | collective-permute-start | bytes 2359304 | tf_op jit(solution)/shard_map/ppermute | solution.py:398
  36.8 32.5 %collective-permute-start.1 = (bf16[512,768]{1,0:T(8,128)(2,1)S(1)}, bf16[512,768]{1,0:T(8,128)(2,1)S(1)}, u32[]{:S(2)}, u32[]{:S(2)}) collective-permute-start(bf16[512,768]{1,0:T(8,128)(2,1)S(1)} %copy-done.22), channel_id=1, source_target_pairs={{0,16},{8,24},{16,0},{24,8},{1,17},{9,25},{17,1},{25,9},{2,18},{10... | collective-permute-start | bytes 2359304 | tf_op jit(solution)/shard_map/ppermute | solution.py:398
  39.4 34.9 %collective-permute-start.7 = (bf16[512,768]{1,0:T(8,128)(2,1)S(1)}, bf16[512,768]{1,0:T(8,128)(2,1)S(1)}, u32[]{:S(2)}, u32[]{:S(2)}) collective-permute-start(bf16[512,768]{1,0:T(8,128)(2,1)S(1)} %copy-done.24), channel_id=1, source_target_pairs={{0,16},{8,24},{16,0},{24,8},{1,17},{9,25},{17,1},{25,9},{2,18},{10... | collective-permute-start | bytes 2359304 | tf_op jit(solution)/shard_map/ppermute | solution.py:398
  69.3 5.1 %collective-permute-start.6 = (bf16[512,768]{1,0:T(8,128)(2,1)S(1)}, bf16[512,768]{1,0:T(8,128)(2,1)S(1)}, u32[]{:S(2)}, u32[]{:S(2)}) collective-permute-start(bf16[512,768]{1,0:T(8,128)(2,1)S(1)} %collective-permute-done.1.refs_2_.refs_4_), channel_id=1, source_target_pairs={{0,8},{8,0},{16,24},{24,16},{1,9},{9,1},{17,25},{25,17},{2,10},{10... | collective-permute-start | bytes 2359304 | tf_op jit(solution)/shard_map/ppermute | solution.py:398
  74.3 2.3 collective-permute-start.8
  139.1 7.0 %collective-permute-start.27 = (bf16[64,768]{1,0:T(8,128)(2,1)}, bf16[64,768]{1,0:T(8,128)(2,1)S(1)}, u32[]{:S(2)}, u32[]{:S(2)}) collective-permute-start(bf16[64,768]{1,0:T(8,128)(2,1)} %get-tuple-element.95), channel_id=1, source_target_pairs={{0,6},{1,7},{2,4},{3,5},{4,2},{5,3},{6,0},{7,1},{8,14},{9,15},{10,... | collective-permute-start | bytes 294920 | tf_op jit(solution)/shard_map/ppermute | solution.py:398
  142.1 10.2 %collective-permute-start.26 = (bf16[64,768]{1,0:T(8,128)(2,1)}, bf16[64,768]{1,0:T(8,128)(2,1)S(1)}, u32[]{:S(2)}, u32[]{:S(2)}) collective-permute-start(bf16[64,768]{1,0:T(8,128)(2,1)} %get-tuple-element.94), channel_id=1, source_target_pairs={{0,4},{1,5},{2,6},{3,7},{4,0},{5,1},{6,2},{7,3},{8,12},{9,13},{10,... | collective-permute-start | bytes 294920 | tf_op jit(solution)/shard_map/ppermute | solution.py:398
  143.9 8.5 %collective-permute-start.25 = (bf16[64,768]{1,0:T(8,128)(2,1)}, bf16[64,768]{1,0:T(8,128)(2,1)S(1)}, u32[]{:S(2)}, u32[]{:S(2)}) collective-permute-start(bf16[64,768]{1,0:T(8,128)(2,1)} %get-tuple-element.93), channel_id=1, source_target_pairs={{0,2},{1,3},{2,0},{3,1},{4,6},{5,7},{6,4},{7,5},{8,10},{9,11},{10,... | collective-permute-start | bytes 294920 | tf_op jit(solution)/shard_map/ppermute | solution.py:398
  144.4 13.2 %collective-permute-start.15 = (bf16[264,768]{1,0:T(8,128)(2,1)}, bf16[264,768]{1,0:T(8,128)(2,1)}, u32[]{:S(2)}, u32[]{:S(2)}) collective-permute-start(bf16[264,768]{1,0:T(8,128)(2,1)} %get-tuple-element.90), channel_id=1, source_target_pairs={{0,1},{1,0},{2,3},{3,2},{4,5},{5,4},{6,7},{7,6},{8,9},{9,8},{10,11... | collective-permute-start | bytes 1216520 | tf_op jit(solution)/shard_map/ppermute | solution.py:398
  153.4 4.2 %collective-permute-start.28 = (bf16[32,768]{1,0:T(8,128)(2,1)S(1)}, bf16[32,768]{1,0:T(8,128)(2,1)S(1)}, u32[]{:S(2)}, u32[]{:S(2)}) collective-permute-start(bf16[32,768]{1,0:T(8,128)(2,1)S(1)} %dynamic-slice_convert_fusion.3), channel_id=1, source_target_pairs={{0,1},{1,0},{2,3},{3,2},{4,5},{5,4},{6,7},{7,6},{8,9},{9,8},{10,11... | collective-permute-start | bytes 147464 | tf_op jit(solution)/shard_map/ppermute | solution.py:398
  154.1 47.7 %collective-permute-start.11 = (bf16[1024,768]{1,0:T(8,128)(2,1)}, bf16[1024,768]{1,0:T(8,128)(2,1)S(1)}, u32[]{:S(2)}, u32[]{:S(2)}) collective-permute-start(bf16[1024,768]{1,0:T(8,128)(2,1)} %get-tuple-element.80), channel_id=1, source_target_pairs={{0,8},{8,0},{16,24},{24,16},{1,9},{9,1},{17,25},{25,17},{2,10},{10... | collective-permute-start | bytes 4718600 | tf_op jit(solution)/shard_map/ppermute | solution.py:398
  154.1 54.2 %collective-permute-start.9 = (bf16[1024,768]{1,0:T(8,128)(2,1)}, bf16[1024,768]{1,0:T(8,128)(2,1)S(1)}, u32[]{:S(2)}, u32[]{:S(2)}) collective-permute-start(bf16[1024,768]{1,0:T(8,128)(2,1)} %get-tuple-element.77), channel_id=1, source_target_pairs={{0,8},{8,0},{16,24},{24,16},{1,9},{9,1},{17,25},{25,17},{2,10},{10... | collective-permute-start | bytes 4718600 | tf_op jit(solution)/shard_map/ppermute | solution.py:398
  157.6 5.4 %collective-permute-start.29 = (bf16[32,768]{1,0:T(8,128)(2,1)S(1)}, bf16[32,768]{1,0:T(8,128)(2,1)S(1)}, u32[]{:S(2)}, u32[]{:S(2)}) collective-permute-start(bf16[32,768]{1,0:T(8,128)(2,1)S(1)} %add_convert_fusion.4), channel_id=1, source_target_pairs={{0,1},{1,0},{2,3},{3,2},{4,5},{5,4},{6,7},{7,6},{8,9},{9,8},{10,11... | collective-permute-start | bytes 147464 | tf_op jit(solution)/shard_map/ppermute | solution.py:398
  157.7 12.3 %copy-start.21 = (bf16[1024,768]{1,0:T(8,128)(2,1)S(1)}, bf16[1024,768]{1,0:T(8,128)(2,1)}, u32[]{:S(2)}) copy-start(bf16[1024,768]{1,0:T(8,128)(2,1)} %get-tuple-element.83) | copy-start | bytes 4718596
  159.1 45.0 %copy-start.6 = (bf16[512,768]{1,0:T(8,128)(2,1)S(1)}, bf16[512,768]{1,0:T(8,128)(2,1)}, u32[]{:S(2)}) copy-start(bf16[512,768]{1,0:T(8,128)(2,1)} %get-tuple-element.81) | copy-start | bytes 2359300
  160.0 10.0 %collective-permute-start.18 = (bf16[72,768]{1,0:T(8,128)(2,1)S(1)}, bf16[72,768]{1,0:T(8,128)(2,1)S(1)}, u32[]{:S(2)}, u32[]{:S(2)}) collective-permute-start(bf16[72,768]{1,0:T(8,128)(2,1)S(1)} %get-tuple-element.110), channel_id=1, source_target_pairs={{0,6},{1,7},{2,4},{3,5},{4,2},{5,3},{6,0},{7,1},{8,14},{9,15},{10,... | collective-permute-start | bytes 331784 | tf_op jit(solution)/shard_map/ppermute | solution.py:398
  162.9 19.8 %collective-permute-start.17 = (bf16[72,768]{1,0:T(8,128)(2,1)S(1)}, bf16[72,768]{1,0:T(8,128)(2,1)S(1)}, u32[]{:S(2)}, u32[]{:S(2)}) collective-permute-start(bf16[72,768]{1,0:T(8,128)(2,1)S(1)} %get-tuple-element.109), channel_id=1, source_target_pairs={{0,4},{1,5},{2,6},{3,7},{4,0},{5,1},{6,2},{7,3},{8,12},{9,13},{10,... | collective-permute-start | bytes 331784 | tf_op jit(solution)/shard_map/ppermute | solution.py:398
  162.9 19.8 %collective-permute-start.16 = (bf16[72,768]{1,0:T(8,128)(2,1)S(1)}, bf16[72,768]{1,0:T(8,128)(2,1)S(1)}, u32[]{:S(2)}, u32[]{:S(2)}) collective-permute-start(bf16[72,768]{1,0:T(8,128)(2,1)S(1)} %get-tuple-element.108), channel_id=1, source_target_pairs={{0,2},{1,3},{2,0},{3,1},{4,6},{5,7},{6,4},{7,5},{8,10},{9,11},{10,... | collective-permute-start | bytes 331784 | tf_op jit(solution)/shard_map/ppermute | solution.py:398
  164.4 109.7 %copy-start.12 = (bf16[64,768]{1,0:T(8,128)(2,1)}, bf16[64,768]{1,0:T(8,128)(2,1)S(1)}, u32[]{:S(2)}) copy-start(bf16[64,768]{1,0:T(8,128)(2,1)S(1)} %pad_maximum_fusion.4.refs_6_) | copy-start | bytes 294916
  169.9 35.3 %collective-permute-start.13 = (bf16[1024,768]{1,0:T(8,128)(2,1)S(1)}, bf16[1024,768]{1,0:T(8,128)(2,1)S(1)}, u32[]{:S(2)}, u32[]{:S(2)}) collective-permute-start(bf16[1024,768]{1,0:T(8,128)(2,1)S(1)} %copy-done.21), channel_id=1, source_target_pairs={{0,8},{8,0},{16,24},{24,16},{1,9},{9,1},{17,25},{25,17},{2,10},{10... | collective-permute-start | bytes 4718600 | tf_op jit(solution)/shard_map/ppermute | solution.py:398
  182.8 22.4 %copy-start.3 = (bf16[64,768]{1,0:T(8,128)(2,1)}, bf16[64,768]{1,0:T(8,128)(2,1)S(1)}, u32[]{:S(2)}) copy-start(bf16[64,768]{1,0:T(8,128)(2,1)S(1)} %add_convert_fusion.3.refs_1_) | copy-start | bytes 294916
  182.8 9.5 %collective-permute-start.21 = (bf16[64,768]{1,0:T(8,128)(2,1)S(1)}, bf16[64,768]{1,0:T(8,128)(2,1)S(1)}, u32[]{:S(2)}, u32[]{:S(2)}) collective-permute-start(bf16[64,768]{1,0:T(8,128)(2,1)S(1)} %add_convert_fusion.3.refs_1_), channel_id=1, source_target_pairs={{0,2},{1,3},{2,0},{3,1},{4,6},{5,7},{6,4},{7,5},{8,10},{9,11},{10,... | collective-permute-start | bytes 294920 | tf_op jit(solution)/shard_map/ppermute | solution.py:398
  182.9 14.0 %collective-permute-start.22 = (bf16[64,768]{1,0:T(8,128)(2,1)S(1)}, bf16[64,768]{1,0:T(8,128)(2,1)S(1)}, u32[]{:S(2)}, u32[]{:S(2)}) collective-permute-start(bf16[64,768]{1,0:T(8,128)(2,1)S(1)} %add_convert_fusion.3.refs_1_), channel_id=1, source_target_pairs={{0,4},{1,5},{2,6},{3,7},{4,0},{5,1},{6,2},{7,3},{8,12},{9,13},{10,... | collective-permute-start | bytes 294920 | tf_op jit(solution)/shard_map/ppermute | solution.py:398
  192.4 12.8 %copy-start.9 = (bf16[64,768]{1,0:T(8,128)(2,1)}, bf16[64,768]{1,0:T(8,128)(2,1)S(1)}, u32[]{:S(2)}) copy-start(bf16[64,768]{1,0:T(8,128)(2,1)S(1)} %collective-permute-done.21.refs_2_) | copy-start | bytes 294916
  192.4 8.6 %collective-permute-start.23 = (bf16[64,768]{1,0:T(8,128)(2,1)S(1)}, bf16[64,768]{1,0:T(8,128)(2,1)S(1)}, u32[]{:S(2)}, u32[]{:S(2)}) collective-permute-start(bf16[64,768]{1,0:T(8,128)(2,1)S(1)} %add_convert_fusion.3.refs_1_), channel_id=1, source_target_pairs={{0,6},{1,7},{2,4},{3,5},{4,2},{5,3},{6,0},{7,1},{8,14},{9,15},{10,... | collective-permute-start | bytes 294920 | tf_op jit(solution)/shard_map/ppermute | solution.py:398
  194.6 12.6 %copy-start.7 = (bf16[512,768]{1,0:T(8,128)(2,1)S(1)}, bf16[512,768]{1,0:T(8,128)(2,1)}, u32[]{:S(2)}) copy-start(bf16[512,768]{1,0:T(8,128)(2,1)} %get-tuple-element.84) | copy-start | bytes 2359300
  196.9 14.7 %collective-permute-start.30 = (bf16[64,768]{1,0:T(8,128)(2,1)S(1)}, bf16[64,768]{1,0:T(8,128)(2,1)S(1)}, u32[]{:S(2)}, u32[]{:S(2)}) collective-permute-start(bf16[64,768]{1,0:T(8,128)(2,1)S(1)} %pad_maximum_fusion.4.refs_6_), channel_id=1, source_target_pairs={{0,2},{1,3},{2,0},{3,1},{4,6},{5,7},{6,4},{7,5},{8,10},{9,11},{10,... | collective-permute-start | bytes 294920 | tf_op jit(solution)/shard_map/ppermute | solution.py:398
  201.0 8.9 %collective-permute-start.19 = (f32[2,768]{1,0:T(2,128)S(1)}, f32[2,768]{1,0:T(2,128)S(1)}, u32[]{:S(2)}, u32[]{:S(2)}) collective-permute-start(f32[2,768]{1,0:T(2,128)S(1)} %slice_bitcast_fusion.3), channel_id=1, source_target_pairs={{0,8},{8,0},{16,24},{24,16},{1,9},{9,1},{17,25},{25,17},{2,10},{10... | collective-permute-start | bytes 18440 | tf_op jit(solution)/shard_map/ppermute | solution.py:398
  201.8 81.3 %collective-permute-start.24 = (bf16[256,768]{1,0:T(8,128)(2,1)}, bf16[256,768]{1,0:T(8,128)(2,1)}, u32[]{:S(2)}, u32[]{:S(2)}) collective-permute-start(bf16[256,768]{1,0:T(8,128)(2,1)} %pad_maximum_fusion), channel_id=1, source_target_pairs={{0,1},{1,0},{2,3},{3,2},{4,5},{5,4},{6,7},{7,6},{8,9},{9,8},{10,11... | collective-permute-start | bytes 1179656 | tf_op jit(solution)/shard_map/ppermute | solution.py:398
  205.2 81.5 %collective-permute-start.12 = (bf16[512,768]{1,0:T(8,128)(2,1)}, bf16[512,768]{1,0:T(8,128)(2,1)}, u32[]{:S(2)}, u32[]{:S(2)}) collective-permute-start(bf16[512,768]{1,0:T(8,128)(2,1)} %add_convert_fusion.1), channel_id=1, source_target_pairs={{0,16},{8,24},{16,0},{24,8},{1,17},{9,25},{17,1},{25,9},{2,18},{10... | collective-permute-start | bytes 2359304 | tf_op jit(solution)/shard_map/ppermute | solution.py:398
  208.3 67.3 %copy-start.16 = (f32[768]{0:T(1024)S(1)}, f32[768]{0:T(1024)}, u32[]{:S(2)}) copy-start(f32[768]{0:T(1024)} %refs_2_.3) | copy-start | bytes 9220
  208.4 78.3 %copy-start = (bf16[1024,768]{1,0:T(8,128)(2,1)}, bf16[1024,768]{1,0:T(8,128)(2,1)S(1)}, u32[]{:S(2)}) copy-start(bf16[1024,768]{1,0:T(8,128)(2,1)S(1)} %collective-permute-done.9.refs_5_) | copy-start | bytes 4718596
  208.4 78.3 %collective-permute-start.14 = (bf16[512,768]{1,0:T(8,128)(2,1)}, bf16[512,768]{1,0:T(8,128)(2,1)S(1)}, u32[]{:S(2)}, u32[]{:S(2)}) collective-permute-start(bf16[512,768]{1,0:T(8,128)(2,1)} %add_convert_fusion), channel_id=1, source_target_pairs={{0,16},{8,24},{16,0},{24,8},{1,17},{9,25},{17,1},{25,9},{2,18},{10... | collective-permute-start | bytes 2359304 | tf_op jit(solution)/shard_map/ppermute | solution.py:398
  209.8 87.2 %collective-permute-start.10 = (bf16[512,768]{1,0:T(8,128)(2,1)}, bf16[512,768]{1,0:T(8,128)(2,1)S(1)}, u32[]{:S(2)}, u32[]{:S(2)}) collective-permute-start(bf16[512,768]{1,0:T(8,128)(2,1)} %add_convert_fusion.2), channel_id=1, source_target_pairs={{0,16},{8,24},{16,0},{24,8},{1,17},{9,25},{17,1},{25,9},{2,18},{10... | collective-permute-start | bytes 2359304 | tf_op jit(solution)/shard_map/ppermute | solution.py:398
  212.2 46.9 %collective-permute-start.20 = (f32[2,768]{1,0:T(2,128)S(1)}, f32[2,768]{1,0:T(2,128)S(1)}, u32[]{:S(2)}, u32[]{:S(2)}) collective-permute-start(f32[2,768]{1,0:T(2,128)S(1)} %fusion), channel_id=1, source_target_pairs={{0,16},{8,24},{16,0},{24,8},{1,17},{9,25},{17,1},{25,9},{2,18},{10... | collective-permute-start | bytes 18440 | tf_op jit(solution)/shard_map/ppermute | solution.py:398
  259.1 15.0 %collective-permute-start.31 = (bf16[64,768]{1,0:T(8,128)(2,1)S(1)}, bf16[64,768]{1,0:T(8,128)(2,1)S(1)}, u32[]{:S(2)}, u32[]{:S(2)}) collective-permute-start(bf16[64,768]{1,0:T(8,128)(2,1)S(1)} %pad_maximum_fusion.4.refs_6_), channel_id=1, source_target_pairs={{0,4},{1,5},{2,6},{3,7},{4,0},{5,1},{6,2},{7,3},{8,12},{9,13},{10,... | collective-permute-start | bytes 294920 | tf_op jit(solution)/shard_map/ppermute | solution.py:398
  274.1 8.9 %copy-start.14 = (bf16[64,768]{1,0:T(8,128)(2,1)}, bf16[64,768]{1,0:T(8,128)(2,1)S(1)}, u32[]{:S(2)}) copy-start(bf16[64,768]{1,0:T(8,128)(2,1)S(1)} %collective-permute-done.31.refs_8_) | copy-start | bytes 294916
  274.1 8.9 %collective-permute-start.32 = (bf16[64,768]{1,0:T(8,128)(2,1)S(1)}, bf16[64,768]{1,0:T(8,128)(2,1)S(1)}, u32[]{:S(2)}, u32[]{:S(2)}) collective-permute-start(bf16[64,768]{1,0:T(8,128)(2,1)S(1)} %pad_maximum_fusion.4.refs_6_), channel_id=1, source_target_pairs={{0,6},{1,7},{2,4},{3,5},{4,2},{5,3},{6,0},{7,1},{8,14},{9,15},{10,... | collective-permute-start | bytes 294920 | tf_op jit(solution)/shard_map/ppermute | solution.py:398
  (16 other events, 49.7 us)
Sparse Core Ops, SparseCore 0:
  154.7 136.2 all-reduce.1

commit v2 on v1

--- a/solution.py
+++ b/solution.py
@@ -63,29 +63,24 @@
     return jnp.broadcast_to(column, (column.shape[0], 128)).T[0:1]
 
 
-def emit_pieces(acc, pos, keep_a, send_a, keep_b, *send_b):
-    third = acc.shape[0] // 3
-    half, step = third, keep_b.shape[0]
-    keep_a[...] = acc[pl.ds(pl.multiple_of(pos[0] * half, half), half), :]
-    send_a[0:half] = acc[pl.ds(pl.multiple_of((1 - pos[0]) * half, half), half), :].astype(BF16)
-    for k, out in enumerate((keep_b,) + send_b):
-        at = pl.multiple_of(2 * third + (pos[1] ^ k) * step, step)
-        out[...] = acc[pl.ds(at, step), :].astype(out.dtype)
+def emit_halves(acc, pos, keep, send):
+    half = acc.shape[0] // 2
+    keep[...] = acc[pl.ds(pl.multiple_of(pos[0] * half, half), half), :]
+    send[0:half] = acc[pl.ds(pl.multiple_of((1 - pos[0]) * half, half), half), :].astype(BF16)
 
 
 def ff_kernel(first, last, blocks, owned, *refs):
     refs = list(refs)
     take = lambda n: [refs.pop(0) for _ in range(n)]
     packs = take(blocks)
-    prior = [] if first else take(1)
-    w1, w2, b1 = take(3)
-    prior_bias = [] if first else take(1)
+    weights = take(3)
+    prior = [] if first else take(2)
     o_ff, n_ff = take(2)
     if last:
         summed, accb = take(2)
     else:
         acc, accb = take(2)
-    buf, sem, prior_sem = take(3)
+    buf, w1, w2, b1, o_s, n_s, sem, weight_sem, prior_sem, o_sem, n_sem = take(11)
     if last:
         (acc,) = take(1)
     rows = packs[0].shape[0] // 2
@@ -95,14 +90,25 @@
     def fetch(j, slot):
         return pltpu.make_async_copy(packs[j], buf.at[slot], sem.at[slot])
 
+    def writes(k, slot):
+        at = pl.ds(pl.multiple_of(k * rows, rows), rows)
+        return (
+            pltpu.make_async_copy(o_s.at[slot], o_ff.at[at], o_sem.at[slot]),
+            pltpu.make_async_copy(n_s.at[slot], n_ff.at[at], n_sem.at[slot]),
+        )
+
     fetch(0, 0).start()
-    if prior:
-        held = pltpu.make_async_copy(prior[0], acc, prior_sem)
-        held.start()
-        accb[...] = prior_bias[0][...]
-    else:
+    loads = [pltpu.make_async_copy(weights[j], to, weight_sem.at[j]) for j, to in enumerate((w1, w2, b1))]
+    for load in loads:
+        load.start()
+    held = [pltpu.make_async_copy(prior[j], to, prior_sem.at[j]) for j, to in enumerate((acc, accb))] if prior else []
+    for copy in held:
+        copy.start()
+    if not prior:
         acc[...] = jnp.zeros(acc.shape, F32)
         accb[...] = jnp.zeros(accb.shape, F32)
+    for load in loads:
+        load.wait()
 
     def step(k, carry):
         slot = k & 1
@@ -113,7 +119,11 @@
             def _(j=j):
                 fetch(j, 1 - slot).start()
 
-        sl = pl.ds(pl.multiple_of(k * rows, rows), rows)
+        @pl.when(k >= 2)
+        def _():
+            for write in writes(k - 2, slot):
+                write.wait()
+
         x = buf[slot, 0:rows]
         g = buf[slot, rows : 2 * rows]
         h = mm(x, w1[...]) + b1[...].reshape(1, -1)
@@ -122,20 +132,23 @@
         pdf = jnp.exp(-0.5 * h * h) * (1.0 / math.sqrt(2.0 * math.pi))
         act = (h * cdf).astype(BF16)
         dh = (da * (cdf + h * pdf)).astype(BF16)
-        o_ff[sl, :] = mm(act, w2[...]).astype(BF16)
-        n_ff[sl, :] = mm(dh, w1[...], NT).astype(BF16)
+        o_s[slot] = mm(act, w2[...]).astype(BF16)
+        n_s[slot] = mm(dh, w1[...], NT).astype(BF16)
+        for write in writes(k, slot):
+            write.start()
+        if prior:
+
+            @pl.when(k == 0)
+            def _():
+                for copy in held:
+                    copy.wait()
+
         accb[0:1] += jnp.sum(dh.astype(F32), axis=0, keepdims=True)
         if owned:
 
             @pl.when(k % 2 == 0)
             def _():
                 accb[1:2] += jnp.sum(g.astype(F32), axis=0, keepdims=True)
-
-        if prior:
-
-            @pl.when(k == 0)
-            def _():
-                held.wait()
 
         acc[0:width] += mm(x, dh, TN)
         acc[width:] += mm(act, g, TN)
@@ -145,26 +158,30 @@
     if last:
         accb[2:3] = as_row(jnp.sum(w1[...].astype(F32) * acc[0:width], axis=1, keepdims=True))
         summed[...] = acc[...].astype(BF16)
+    for k in range(blocks - 2, blocks):
+        for write in writes(k, k & 1):
+            write.wait()
 
 
 def att_kernel(first, last, blocks, heads, size, starts, *refs):
     refs = list(refs)
     take = lambda n: [refs.pop(0) for _ in range(n)]
-    length, pos = take(2)
+    length, pos, x_bit = take(3)
     parts = take(blocks)
     ff_parts = take(4)
     prior = [] if first else take(1)
-    wqkv, wproj, qg, kg = take(4)
+    weights = take(4)
     prior_gain = [] if first else take(1)
-    ff_small = take(1) if last else []
+    ff_small_in = take(1) if last else []
     keep_near, keep_far, send = take(3)
     if last:
-        pieces = take(len(refs) - 26)
+        pieces = take(len(refs) - 34)
         (small,) = take(1)
     else:
         acc, accg = take(2)
     jt, dot_s, qs_t, qt_s, k_s, kt_s, v_s, vt_s, es, dqt, dk, dv, ot, djt = take(14)
     ff_s, ff_sem, prior_sem, out_s, out_sem, dot_bs, r_s, pack_s, pack_sem = take(9)
+    wqkv, wproj, qg, kg, gain_s, small_s, weight_sem, tail_sem = take(8)
     if last:
         acc, accg = take(2)
     rows = parts[0].shape[0] // 2
@@ -172,8 +189,15 @@
     total = rows * blocks
     scale = size**-0.5
     up = scale * math.log2(math.e)
+    loads = [pltpu.make_async_copy(weights[j], to, weight_sem.at[j]) for j, to in enumerate((wqkv, wproj, qg, kg))]
+    for load in loads[:2]:
+        load.start()
     for k in range(blocks):
         pltpu.make_async_copy(parts[k], pack_s.at[k], pack_sem.at[k]).start()
+    for load in loads[2:]:
+        load.start()
+    for load in loads[:2]:
+        load.wait()
 
     def project(k, carry):
         pltpu.make_async_copy(parts[0], pack_s.at[k], pack_sem.at[k]).wait()
@@ -183,7 +207,12 @@
         return carry
 
     lax.fori_loop(0, blocks, project, 0)
-    later = []
+    for load in loads[2:]:
+        load.wait()
+    later = [pltpu.make_async_copy(source, gain_s, tail_sem.at[0]) for source in prior_gain]
+    later += [pltpu.make_async_copy(source, small_s, tail_sem.at[1]) for source in ff_small_in]
+    for copy in later:
+        copy.start()
     for k in range(4):
         rows_of = pl.ds(starts[k // 2], 2 * rows)
         later.append(pltpu.make_async_copy(ff_parts[k].at[rows_of], ff_s.at[k % 2, k // 2], ff_sem.at[k]))
@@ -291,11 +320,10 @@
         return carry
 
     lax.fori_loop(0, heads, undo, 0)
-    if prior:
-        accg[...] += prior_gain[0][...]
-
     for copy in later:
         copy.wait()
+    if prior:
+        accg[...] += gain_s[...]
 
     targets = [keep_near, send.at[pl.ds(0, 2 * rows)], keep_far, send.at[pl.ds(2 * rows, 2 * rows)]]
     writes = [pltpu.make_async_copy(out_s.at[k], targets[k], out_sem.at[k]) for k in range(blocks)]
@@ -319,14 +347,14 @@
 
     lax.fori_loop(0, blocks, give, 0)
     if last:
-        ln = jnp.sum(wqkv[...].astype(F32) * acc[0:joined], axis=0, keepdims=True) + ff_small[0][2:3]
+        ln = jnp.sum(wqkv[...].astype(F32) * acc[0:joined], axis=0, keepdims=True) + small_s[2:3]
         gain_row = as_row(accg[...])
         pad = jnp.zeros((1, ln.shape[1] - gain_row.shape[1]), F32)
-        lines = [jnp.concatenate([gain_row, pad], axis=1), ff_small[0][0:2], ln, jnp.zeros((4, ln.shape[1]), F32)]
+        lines = [jnp.concatenate([gain_row, pad], axis=1), small_s[0:2], ln, jnp.zeros((4, ln.shape[1]), F32)]
         small[...] = jnp.concatenate(lines, axis=0).astype(BF16)
-        emit_pieces(acc, pos.at[1:3], *pieces)
-        third = pieces[0].shape[0]
-        pieces[1][third : third + 8] = small[...]
+        emit_halves(acc, x_bit, *pieces)
+        half = pieces[0].shape[0]
+        pieces[1][half : half + 8] = small[...]
     for write in writes:
         write.wait()
 
@@ -360,20 +388,17 @@
 
 
 def join_kernel(n, *refs):
-    pos, own, far, pairs = refs[0], refs[1 : 1 + n], refs[1 + n], refs[2 + n : 2 + 2 * n]
-    one, two, whole = refs[2 + 2 * n :]
+    pos, own, across, rest = refs[0], refs[1 : 1 + n], refs[1 + n], refs[2 + n]
+    one, two, whole = refs[3 + n :]
     step = own[0].shape[0]
-    third = step * n
+    half = step * n
     for k in range(n):
         z = pos[1] ^ k
-        at = pl.multiple_of(pos[0] * third + z * step, step)
+        at = pl.multiple_of(pos[0] * half + z * step, step)
         whole[pl.ds(at, step), :] = own[k][...].astype(F32)
-        at = pl.multiple_of((1 - pos[0]) * third + z * step, step)
-        whole[pl.ds(at, step), :] = far[k * step : (k + 1) * step].astype(F32)
-        half = step // 2
-        for s in range(2):
-            at = pl.multiple_of(2 * third + z * step + (pos[0] ^ s) * half, half)
-            whole[pl.ds(at, half), :] = pairs[k][s * half : (s + 1) * half].astype(F32)
+        at = pl.multiple_of((1 - pos[0]) * half + z * step, step)
+        far = across[...] if k == 0 else rest[(k - 1) * step : k * step]
+        whole[pl.ds(at, step), :] = far.astype(F32)
     cut = one.shape[0]
     one[...] = whole[0:cut]
     two[...] = whole[cut:]
@@ -423,21 +448,24 @@
     b1 = b_fc1
     pos = jnp.stack([x, z])
 
-    def pieces_of(third, columns):
-        step = third // n
-        return [((third, columns), F32), ((third + 8, columns), BF16), ((step, columns), F32)] + [
-            ((step, columns), BF16)
-        ] * (n - 1)
-
-    qp_pieces = pieces_of((joined + inner) // 3, width)
+    half = (joined + inner) // 2
+    qp_pieces = [((half, width), F32), ((half + 8, width), BF16)]
 
     def ff(first, last, packs, state):
         count = len(packs)
         outs = [((count * rows, width), BF16)] * 2
         scratch = [
             pltpu.VMEM((2, 2 * rows, width), BF16),
+            pltpu.VMEM((width, hidden), BF16),
+            pltpu.VMEM((hidden, width), BF16),
+            pltpu.VMEM((hidden,), F32),
+            pltpu.VMEM((2, rows, width), BF16),
+            pltpu.VMEM((2, rows, width), BF16),
             pltpu.SemaphoreType.DMA((2,)),
-            pltpu.SemaphoreType.DMA,
+            pltpu.SemaphoreType.DMA((3,)),
+            pltpu.SemaphoreType.DMA((2,)),
+            pltpu.SemaphoreType.DMA((2,)),
+            pltpu.SemaphoreType.DMA((2,)),
         ]
         if last:
             outs += [((width + hidden, width), BF16), ((8, width), F32)]
@@ -446,7 +474,7 @@
             outs += [((width + hidden, width), F32), ((8, width), F32)]
         res = call(
             functools.partial(ff_kernel, first, last, count, first), outs, 0,
-            *packs, *state[:1], w_fc1, w_fc2, b1, *state[1:], n_any=count + len(state[:1]),
+            *packs, w_fc1, w_fc2, b1, *state, n_any=count + 3 + len(state), any_outs=2,
             scratch=scratch, flops=12 * count * rows * width * hidden,
         )
         return res[0], res[1], res[2:]
@@ -454,7 +482,6 @@
     qg = q_gain.reshape(-1, 1)
     kg = k_gain.reshape(-1, 1)
     w_t = w_qkv.T
-    att_pos = jnp.stack([t, x, z])
     keeps = []
 
     def att(i, ff_parts, starts, state, ff_small=()):
@@ -484,6 +511,14 @@
             pltpu.VMEM((8, total), F32),
             pltpu.VMEM((blocks, 2 * rows, width), BF16),
             pltpu.SemaphoreType.DMA((blocks,)),
+            pltpu.VMEM((joined, width), BF16),
+            pltpu.VMEM((inner, width), BF16),
+            pltpu.VMEM((inner, 1), F32),
+            pltpu.VMEM((inner, 1), F32),
+            pltpu.VMEM((2 * inner, 1), F32),
+            pltpu.VMEM((8, width), F32),
+            pltpu.SemaphoreType.DMA((4,)),
+            pltpu.SemaphoreType.DMA((2,)),
         ]
         if last:
             outs += qp_pieces + [((8, width), BF16)]
@@ -491,9 +526,9 @@
         else:
             outs += [((joined + inner, width), F32), ((2 * inner, 1), F32)]
         res = call(
-            functools.partial(att_kernel, first, last, blocks, heads, size, starts), outs, 2,
-            lengths[i : i + 1], att_pos, own[i], near[i], far[i], cross[i], *ff_parts, *state[:1],
-            w_t, w_proj, qg, kg, *state[1:], *ff_small, n_any=blocks + 4 + len(state[:1]), any_outs=3,
+            functools.partial(att_kernel, first, last, blocks, heads, size, starts), outs, 3,
+            lengths[i : i + 1], t[None], x[None], own[i], near[i], far[i], cross[i], *ff_parts, *state[:1],
+            w_t, w_proj, qg, kg, *state[1:], *ff_small, n_any=blocks + 8 + len(state) + len(ff_small), any_outs=3,
             scratch=scratch,
             flops=6 * 8 * heads * total * total * size + 8 * total * width * (joined + inner),
         )
@@ -503,39 +538,31 @@
         keeps.extend([keep_near, got, swap(summed, "tp", 2)])
         return res[3:]
 
-    def reduce_weight(small, keep_a, send_a, keep_b, *send_b):
+    def reduce_weight(small, keep, send):
         extra = small.shape[0]
-        got = swap(send_a, "dp", 1)
-        half = keep_a + got[:-extra].astype(F32)
+        got = swap(send, "dp", 1)
+        half = keep + got[:-extra].astype(F32)
         small = (small.astype(F32) + got[-extra:].astype(F32)).astype(BF16)
-        done_b = keep_b
-        for k in range(1, n):
-            done_b = done_b + swap(send_b[k - 1], "dp", 2 * k).astype(F32)
-        step = keep_b.shape[0]
+        step = keep.shape[0] // n
         piece = lambda k: lax.dynamic_slice_in_dim(half, (z ^ k) * step, step, 0)
-        cut = step // 2
-        sent = lax.dynamic_slice_in_dim(done_b, (1 - x) * cut, cut, 0).astype(BF16)
-        done_b = lax.dynamic_slice_in_dim(done_b, x * cut, cut, 0) + swap(sent, "dp", 1).astype(F32)
-        done_b = done_b.astype(BF16)
-        done_a = piece(0)
+        done = piece(0)
         smalls = [small]
         for k in range(1, n):
             got = swap(jnp.concatenate([piece(k).astype(BF16), small], axis=0), "dp", 2 * k)
-            done_a = done_a + got[:-extra].astype(F32)
+            done = done + got[:-extra].astype(F32)
             smalls.append(got[-extra:])
-        done_a = done_a.astype(BF16)
+        done = done.astype(BF16)
         smalls = jnp.stack(smalls).astype(F32)
         small = sum(lax.dynamic_index_in_dim(smalls, z ^ k, 0, keepdims=False) for k in range(n))
-        pair = jnp.concatenate([done_b, swap(done_b, "dp", 1)], axis=0)
-        near_a = [done_a] + [swap(done_a, "dp", 2 * k) for k in range(1, n)]
-        pairs = [pair] + [swap(pair, "dp", 2 * k) for k in range(1, n)]
-        far_a = swap(jnp.concatenate(near_a, axis=0), "dp", 1)
-        return near_a + [far_a] + pairs, small
+        near = [swap(done, "dp", 2 * k) for k in range(1, n)]
+        across = swap(done, "dp", 1)
+        rest = swap(jnp.concatenate(near, axis=0), "dp", 1)
+        return [done] + near + [across, rest], small
 
     def join(parts, shapes):
         return call(
             functools.partial(join_kernel, n), [(s, F32) for s in shapes], 1, pos, *parts,
-            scratch=[pltpu.VMEM((3 * n * parts[0].shape[0], width), F32)],
+            scratch=[pltpu.VMEM((joined + inner, width), F32)],
         )
 
     a_parts = ff(True, False, [b for i in range(images) for b in (own[i], near[i])], [])

time: 309 us -> 304 us (0.984)
  starting transfers between devices: 32.2 us -> 23.8 us
  Pallas kernels: 124 us -> 120 us
  waiting for transfers between devices: 115 us -> 119 us
    psum x1, waiting for transfers between devices: 0.01 us -> 17.8 us  [block(): fc = lax.psum(ff_out, 'dp')]
    ppermute x33 -> x26, waiting for transfers between devices: 115 us -> 101 us  [swap(): return lax.ppermute(v, axis, [(i, i ^ mask) for i in range(count)])]
    ppermute x33 -> x26, starting transfers between devices: 32.2 us -> 23.8 us  [swap(): return lax.ppermute(v, axis, [(i, i ^ mask) for i in range(count)])]
  transfers between devices with their start and end apart: 34 -> 27, of which waited for: 15 -> 12; matrix products, arithmetic and copies ran while one was open for 6% -> 6% of each run, Pallas kernels for 18% -> 17%
where the time goes in v2:
time: 304 us
  Pallas kernels  120 us (39%)
  waiting for transfers between devices  119 us (39%)
  starting transfers between devices  23.8 us (8%)
  between operations  14.3 us (5%)
  other arithmetic  14.1 us (5%)
  local copies, waits for them, and re-layouts  12.3 us (4%)
    pallas_call x8, Pallas kernels, call(): pl.pallas_call(kernel, out_shape=[jax.ShapeDtypeStruct(s, d) for s, d in...  112 us
    ppermute x26, waiting for transfers between devices, swap(): return lax.ppermute(v, axis, [(i, i ^ mask) for i in range(count)])  101 us
    ppermute x26, starting transfers between devices, swap(): return lax.ppermute(v, axis, [(i, i ^ mask) for i in range(count)])  23.8 us
    psum x1, waiting for transfers between devices, block(): fc = lax.psum(ff_out, 'dp')  17.8 us
    pallas_call x2, Pallas kernels, finish(): pl.pallas_call(functools.partial(final_kernel, end - begin), grid=(end -...  8.81 us
  transfers between devices with their start and end apart: 27, of which 12 were waited for; matrix products, arithmetic and copies ran while one was open for 6% of the time, Pallas kernels for 17%

profile of v2, /device:TPU:0, one launch (start us, length us, event | category | flops | bytes accessed | tf_op | source)
XLA Modules:
  0.0 303.6 jit_solution(5770759248152744371)
XLA Ops:
  7.2 4.0 %shard_map.203 = (bf16[512,768]{1,0:T(8,128)(2,1)}, bf16[512,768]{1,0:T(8,128)(2,1)}, bf16[512,768]{1,0:T(8,128)(2,1)}) custom-call(bf16[3,256,768]{2,1,0:T(8,128)(2,1)} %refs_0_.3, bf16[3,256,768]{2,1,0:T(8,128)(2,1)} %refs_1_.3, f32[768]{0:T(1024)} %refs_2_.5), custom_call_target="tpu_custom_call" | custom-call | bytes 4721664 | tf_op jit(solution)/shard_map/pallas_call | solution.py:31
  12.3 2.6 collective-permute-start.3
  15.1 1.0 collective-permute-done.4.refs_3_.refs_4_
  16.1 0.9 copy-done.21
  17.0 17.8 %shard_map.204 = (bf16[1536,768]{1,0:T(8,128)(2,1)}, bf16[1536,768]{1,0:T(8,128)(2,1)}, f32[1536,768]{1,0:T(8,128)}, f32[8,768]{1,0:T(8,128)}) custom-call(bf16[512,768]{1,0:T(8,128)(2,1)} %get-tuple-element.52.refs_0_.refs_3_, bf16[512,768]{1,0:T(8,128)(2,1)} %collective-permute-done.2.refs_1_.refs_4_, bf16[512,768]{1,0:T(8,128)(2,1)} %get-tuple-element.53.refs_2_.refs_3_, ...), custom_call_target="tpu_custom_call" | custom-call | flops 10871635968 | bytes 16542720 | tf_op jit(solution)/shard_map/pallas_call | solution.py:31
  35.3 2.6 collective-permute-start.1
  38.0 0.8 reshape.36.refs_13_.refs_14_
  38.8 0.8 reshape.37.refs_14_.refs_15_
  40.1 9.9 %shard_map.205 = (bf16[512,768]{1,0:T(8,128)(2,1)}, bf16[512,768]{1,0:T(8,128)(2,1)}, f32[1536,768]{1,0:T(8,128)}, f32[8,768]{1,0:T(8,128)}) custom-call(bf16[512,768]{1,0:T(8,128)(2,1)} %collective-permute-done.3.refs_0_.refs_5_, bf16[512,768]{1,0:T(8,128)(2,1)} %collective-permute-done.5.refs_1_.refs_6_, bf16[768,768]{1,0:T(8,128)(2,1)} %refs_4_.3, ...), custom_call_target="tpu_custom_call" | custom-call | flops 3623878656 | bytes 14994432 | tf_op jit(solution)/shard_map/pallas_call | solution.py:31
  50.1 16.5 %shard_map.206 = (bf16[512,768]{1,0:T(8,128)(2,1)}, bf16[512,768]{1,0:T(8,128)(2,1)}, bf16[1024,768]{1,0:T(8,128)(2,1)}, f32[768,768]{1,0:T(8,128)}, f32[384,1]{1,0:T(8,128)}) custom-call(s32[1]{0:T(128)} %get-tuple-element.105.refs_0_, s32[1]{0:T(128)} %bitcast.refs_1_, s32[1]{0:T(128)} %bitcast.1.refs_2_, ...), custom_call_target="tpu_custom_call" | custom-call | flops 14495514624 | bytes 16124940 | tf_op jit(solution)/shard_map/pallas_call | solution.py:31
  66.8 6.1 %collective-permute-done.7.refs_0_.refs_5_ = bf16[512,768]{1,0:T(8,128)(2,1)S(1)} collective-permute-done((bf16[512,768]{1,0:T(8,128)(2,1)S(1)}, bf16[512,768]{1,0:T(8,128)(2,1)S(1)}, u32[]{:S(2)}, u32[]{:S(2)}) %collective-permute-start.7) | collective-permute-done | bytes 786464 | tf_op jit(solution)/shard_map/ppermute | solution.py:423
  72.9 2.3 collective-permute-done.8.refs_1_.refs_6_
  75.2 0.9 copy-done.25
  76.0 14.2 %shard_map.207 = (bf16[1024,768]{1,0:T(8,128)(2,1)}, bf16[1024,768]{1,0:T(8,128)(2,1)}, bf16[1536,768]{1,0:T(8,128)(2,1)}, f32[8,768]{1,0:T(8,128)}) custom-call(bf16[512,768]{1,0:T(8,128)(2,1)} %copy-done.23, bf16[512,768]{1,0:T(8,128)(2,1)} %copy-done.25, bf16[512,768]{1,0:T(8,128)(2,1)} %copy-done.22, bf16[512,768]{1,0:T(8,128)(2,1)} %copy-done.24, ...), custom_call_target="tpu_custom_call" | custom-call | flops 7247757312 | bytes 15780864 | tf_op jit(solution)/shard_map/pallas_call | solution.py:31
  90.3 21.8 %shard_map.208 = (bf16[512,768]{1,0:T(8,128)(2,1)}, bf16[512,768]{1,0:T(8,128)(2,1)}, bf16[1024,768]{1,0:T(8,128)(2,1)}, f32[768,768]{1,0:T(8,128)}, f32[384,1]{1,0:T(8,128)}) custom-call(s32[1]{0:T(128)} %get-tuple-element.103.refs_0_, s32[1]{0:T(128)} %bitcast.refs_1_, s32[1]{0:T(128)} %bitcast.1.refs_2_, ...), custom_call_target="tpu_custom_call" | custom-call | flops 14495514624 | bytes 20058636 | tf_op jit(solution)/shard_map/pallas_call | solution.py:31
  112.0 24.4 %shard_map.209 = (bf16[512,768]{1,0:T(8,128)(2,1)}, bf16[512,768]{1,0:T(8,128)(2,1)}, bf16[1024,768]{1,0:T(8,128)(2,1)}, f32[384,768]{1,0:T(8,128)}, bf16[392,768]{1,0:T(8,128)(2,1)}, /*index=5*/bf16[8,768]{1,0:T(8,128)(2,1)}) custom-call(s32[1]{0:T(128)} %get-tuple-element.104.refs_0_, s32[1]{0:T(128)} %bitcast.refs_1_, s32[1]{0:T(128)} %bitcast.1.refs_2_, ...), custom_call_target="tpu_custom_call" | custom-call | flops 14495514624 | bytes 19516428 | tf_op jit(solution)/shard_map/pallas_call | solution.py:31
  136.6 15.8 %collective-permute-done.15 = bf16[392,768]{1,0:T(8,128)(2,1)S(1)} collective-permute-done((bf16[392,768]{1,0:T(8,128)(2,1)}, bf16[392,768]{1,0:T(8,128)(2,1)S(1)}, u32[]{:S(2)}, u32[]{:S(2)}) %collective-permute-start.15) | collective-permute-done | bytes 602144 | tf_op jit(solution)/shard_map/ppermute | solution.py:423
  152.4 1.4 convert_add_fusion
  153.8 1.0 copy-done.3
  155.5 1.7 collective-permute-start.18
  157.2 1.8 collective-permute-start.17
  159.0 0.9 collective-permute-start.16
  161.1 3.3 %collective-permute-done.18 = bf16[104,768]{1,0:T(8,128)(2,1)} collective-permute-done((bf16[104,768]{1,0:T(8,128)(2,1)}, bf16[104,768]{1,0:T(8,128)(2,1)}, u32[]{:S(2)}, u32[]{:S(2)}) %collective-permute-start.18) | collective-permute-done | bytes 159776 | tf_op jit(solution)/shard_map/ppermute | solution.py:423
  164.4 19.2 %collective-permute-done.17 = bf16[104,768]{1,0:T(8,128)(2,1)} collective-permute-done((bf16[104,768]{1,0:T(8,128)(2,1)S(1)}, bf16[104,768]{1,0:T(8,128)(2,1)}, u32[]{:S(2)}, u32[]{:S(2)}) %collective-permute-start.17) | collective-permute-done | bytes 159776 | tf_op jit(solution)/shard_map/ppermute | solution.py:423
  183.6 1.9 add_convert_fusion.3.refs_1_
  185.5 2.8 collective-permute-start.22
  188.3 0.7 slice_bitcast_fusion
  191.1 1.6 collective-permute-start.23
  192.7 1.1 add_convert_fusion.1
  193.8 7.2 %collective-permute-done.21.refs_2_ = bf16[96,768]{1,0:T(8,128)(2,1)S(1)} collective-permute-done((bf16[96,768]{1,0:T(8,128)(2,1)}, bf16[96,768]{1,0:T(8,128)(2,1)S(1)}, u32[]{:S(2)}, u32[]{:S(2)}) %collective-permute-start.21) | collective-permute-done | bytes 147488 | tf_op jit(solution)/shard_map/ppermute | solution.py:423
  201.0 4.1 %collective-permute-done.22.refs_3_ = bf16[96,768]{1,0:T(8,128)(2,1)S(1)} collective-permute-done((bf16[96,768]{1,0:T(8,128)(2,1)}, bf16[96,768]{1,0:T(8,128)(2,1)S(1)}, u32[]{:S(2)}, u32[]{:S(2)}) %collective-permute-start.22) | collective-permute-done | bytes 147488 | tf_op jit(solution)/shard_map/ppermute | solution.py:423
  205.2 3.5 %collective-permute-start.12 = (bf16[512,768]{1,0:T(8,128)(2,1)}, bf16[512,768]{1,0:T(8,128)(2,1)}, u32[]{:S(2)}, u32[]{:S(2)}) collective-permute-start(bf16[512,768]{1,0:T(8,128)(2,1)} %add_convert_fusion.1), channel_id=1, source_target_pairs={{0,16},{8,24},{16,0},{24,8},{1,17},{9,25},{17,1},{25,9},{2,18},{10... | collective-permute-start | bytes 2359304 | tf_op jit(solution)/shard_map/ppermute | solution.py:423
  208.7 0.8 pad_maximum_fusion
  209.5 1.3 add_convert_fusion
  210.9 0.9 collective-permute-start.14
  211.8 1.4 add_convert_fusion.2
  213.1 1.2 collective-permute-start.10
  214.4 0.9 collective-permute-start.20
  215.3 39.8 %collective-permute-done.20 = f32[2,768]{1,0:T(2,128)S(1)} collective-permute-done((f32[2,768]{1,0:T(2,128)S(1)}, f32[2,768]{1,0:T(2,128)S(1)}, u32[]{:S(2)}, u32[]{:S(2)}) %collective-permute-start.20) | collective-permute-done | bytes 6176 | tf_op jit(solution)/shard_map/ppermute | solution.py:423
  255.0 0.8 collective-permute-start.24
  258.5 1.9 collective-permute-done.24.refs_5_
  261.0 3.1 %shard_map.212 = (f32[576,768]{1,0:T(8,128)}, f32[192,768]{1,0:T(8,128)}) custom-call(s32[2]{0:T(128)} %pad_add_fusion.refs_0_, bf16[96,768]{1,0:T(8,128)(2,1)} %add_convert_fusion.3.refs_1_, bf16[96,768]{1,0:T(8,128)(2,1)} %copy-done.9, bf16[96,768]{1,0:T(8,128)(2,1)} %copy-done.10, bf16[96,768]{1,0:T(8,128)(2,1)} %copy-done.11, ...), custom_call_target="tpu_custom_call" | custom-call | bytes 3538952 | tf_op jit(solution)/shard_map/pallas_call | solution.py:31
  264.1 1.0 copy-done.5
  265.1 5.3 %shard_map.210 = (bf16[3,256,768]{2,1,0:T(8,128)(2,1)}, f32[3,256,768]{2,1,0:T(8,128)}) custom-call(bf16[3,256,768]{2,1,0:T(8,128)(2,1)} %refs_0_.3, bf16[3,256,768]{2,1,0:T(8,128)(2,1)} %refs_1_.3, f32[768]{0:T(1024)} %refs_2_.5, f32[768]{0:T(1024)} %refs_3_.5, bf16[512,768]{1,0:T(8,128)(2,1)} %get-tuple-element.75.refs_4_, bf16[1024,768]{1,0:T(8,128)(2,1)} %copy-done.1, ...), custom_call_target="tpu_custom_call" | custom-call | tf_op jit(solution)/shard_map/pallas_call | solution.py:602
  270.3 17.8 %all-reduce.2.cloned.1.call-done = bf16[1536,768]{1,0:T(8,128)(2,1)} async-done(((bf16[1536,768]{1,0:T(8,128)(2,1)}), bf16[1536,768]{1,0:T(8,128)(2,1)}) %all-reduce.2.cloned.1.call-update) | async-done | bytes 2359312 | tf_op jit(solution)/shard_map/psum | solution.py:578
  288.1 4.2 %slice_convert_fusion = (f32[768,768]{1,0:T(8,128)}, f32[768,768]{1,0:T(8,128)}) fusion(bf16[1536,768]{1,0:T(8,128)(2,1)} %all-reduce.2.cloned.1.call-done), kind=kLoop, calls=%fused_computation.3 | loop fusion | flops 1179648 | bytes 7077888 | tf_op jit(solution)/shard_map/convert_element_type | solution.py:593
  292.3 0.9 copy-done.4
  293.2 3.5 %shard_map.211 = (bf16[3,256,768]{2,1,0:T(8,128)(2,1)}, f32[3,256,768]{2,1,0:T(8,128)}) custom-call(bf16[3,256,768]{2,1,0:T(8,128)(2,1)} %refs_0_.3, bf16[3,256,768]{2,1,0:T(8,128)(2,1)} %refs_1_.3, f32[768]{0:T(1024)} %refs_2_.5, f32[768]{0:T(1024)} %refs_3_.5, ...), custom_call_target="tpu_custom_call", output_to_operand_aliasing={{0}: (7, {}), {1}: (8, {})} | custom-call | tf_op jit(solution)/shard_map/pallas_call | solution.py:602
  (98 shorter events, 10.1 us)
Async XLA Ops:
  7.2 280.9 %all-reduce.2.cloned.1.call-start = ((), (), s32[]{:S(2)}) async-start(), calls=%async_computation | async-start | bytes 4718592 | tf_op jit(solution)/shard_map/psum | solution.py:578
  11.2 3.7 %collective-permute-start = (bf16[512,768]{1,0:T(8,128)(2,1)}, bf16[512,768]{1,0:T(8,128)(2,1)S(1)}, u32[]{:S(2)}, u32[]{:S(2)}) collective-permute-start(bf16[512,768]{1,0:T(8,128)(2,1)} %get-tuple-element.51.refs_4_.refs_3_), channel_id=1, source_target_pairs={{0,8},{8,0},{16,24},{24,16},{1,9},{9,1},{17,25},{25,17},{2,10},{10... | collective-permute-start | bytes 2359304 | tf_op jit(solution)/shard_map/ppermute | solution.py:423
  11.7 3.4 %collective-permute-start.2 = (bf16[512,768]{1,0:T(8,128)(2,1)}, bf16[512,768]{1,0:T(8,128)(2,1)}, u32[]{:S(2)}, u32[]{:S(2)}) collective-permute-start(bf16[512,768]{1,0:T(8,128)(2,1)} %get-tuple-element.52.refs_0_.refs_3_), channel_id=1, source_target_pairs={{0,8},{8,0},{16,24},{24,16},{1,9},{9,1},{17,25},{25,17},{2,10},{10... | collective-permute-start | bytes 2359304 | tf_op jit(solution)/shard_map/ppermute | solution.py:423
  11.8 23.5 %copy-start.18 = (bf16[512,768]{1,0:T(8,128)(2,1)S(1)}, bf16[512,768]{1,0:T(8,128)(2,1)}, u32[]{:S(2)}) copy-start(bf16[512,768]{1,0:T(8,128)(2,1)} %get-tuple-element.51.refs_4_.refs_3_) | copy-start | bytes 2359300
  11.8 26.1 %copy-start.20 = (bf16[512,768]{1,0:T(8,128)(2,1)S(1)}, bf16[512,768]{1,0:T(8,128)(2,1)}, u32[]{:S(2)}) copy-start(bf16[512,768]{1,0:T(8,128)(2,1)} %get-tuple-element.53.refs_2_.refs_3_) | copy-start | bytes 2359300
  11.8 26.2 %copy-start.16 = (f32[3,64]{1,0:T(4,128)S(1)}, f32[3,64]{1,0:T(4,128)}, u32[]{:S(2)}) copy-start(f32[3,64]{1,0:T(4,128)} %param.16) | copy-start | bytes 2308
  11.8 26.9 %copy-start.17 = (f32[3,64]{1,0:T(4,128)S(1)}, f32[3,64]{1,0:T(4,128)}, u32[]{:S(2)}) copy-start(f32[3,64]{1,0:T(4,128)} %param.17) | copy-start | bytes 2308
  11.8 27.7 %copy-start.15 = (s32[3]{0:T(128)S(1)}, s32[3]{0:T(128)}, u32[]{:S(2)}) copy-start(s32[3]{0:T(128)} %param.13) | copy-start | bytes 40
  11.8 4.3 %collective-permute-start.4 = (bf16[512,768]{1,0:T(8,128)(2,1)}, bf16[512,768]{1,0:T(8,128)(2,1)S(1)}, u32[]{:S(2)}, u32[]{:S(2)}) collective-permute-start(bf16[512,768]{1,0:T(8,128)(2,1)} %get-tuple-element.53.refs_2_.refs_3_), channel_id=1, source_target_pairs={{0,8},{8,0},{16,24},{24,16},{1,9},{9,1},{17,25},{25,17},{2,10},{10... | collective-permute-start | bytes 2359304 | tf_op jit(solution)/shard_map/ppermute | solution.py:423
  12.3 22.5 %collective-permute-start.3 = (bf16[512,768]{1,0:T(8,128)(2,1)}, bf16[512,768]{1,0:T(8,128)(2,1)}, u32[]{:S(2)}, u32[]{:S(2)}) collective-permute-start(bf16[512,768]{1,0:T(8,128)(2,1)} %get-tuple-element.52.refs_0_.refs_3_), channel_id=1, source_target_pairs={{0,16},{8,24},{16,0},{24,8},{1,17},{9,25},{17,1},{25,9},{2,18},{10... | collective-permute-start | bytes 2359304 | tf_op jit(solution)/shard_map/ppermute | solution.py:423
  14.9 1.2 copy-start.19
  34.8 5.3 %collective-permute-start.5 = (bf16[512,768]{1,0:T(8,128)(2,1)}, bf16[512,768]{1,0:T(8,128)(2,1)}, u32[]{:S(2)}, u32[]{:S(2)}) collective-permute-start(bf16[512,768]{1,0:T(8,128)(2,1)} %collective-permute-done.3.refs_0_.refs_5_), channel_id=1, source_target_pairs={{0,8},{8,0},{16,24},{24,16},{1,9},{9,1},{17,25},{25,17},{2,10},{10... | collective-permute-start | bytes 2359304 | tf_op jit(solution)/shard_map/ppermute | solution.py:423
  35.3 31.3 %collective-permute-start.1 = (bf16[512,768]{1,0:T(8,128)(2,1)S(1)}, bf16[512,768]{1,0:T(8,128)(2,1)S(1)}, u32[]{:S(2)}, u32[]{:S(2)}) collective-permute-start(bf16[512,768]{1,0:T(8,128)(2,1)S(1)} %copy-done.18), channel_id=1, source_target_pairs={{0,16},{8,24},{16,0},{24,8},{1,17},{9,25},{17,1},{25,9},{2,18},{10... | collective-permute-start | bytes 2359304 | tf_op jit(solution)/shard_map/ppermute | solution.py:423
  37.9 34.9 %collective-permute-start.7 = (bf16[512,768]{1,0:T(8,128)(2,1)S(1)}, bf16[512,768]{1,0:T(8,128)(2,1)S(1)}, u32[]{:S(2)}, u32[]{:S(2)}) collective-permute-start(bf16[512,768]{1,0:T(8,128)(2,1)S(1)} %copy-done.20), channel_id=1, source_target_pairs={{0,16},{8,24},{16,0},{24,8},{1,17},{9,25},{17,1},{25,9},{2,18},{10... | collective-permute-start | bytes 2359304 | tf_op jit(solution)/shard_map/ppermute | solution.py:423
  66.6 8.5 %copy-start.22 = (bf16[512,768]{1,0:T(8,128)(2,1)}, bf16[512,768]{1,0:T(8,128)(2,1)S(1)}, u32[]{:S(2)}) copy-start(bf16[512,768]{1,0:T(8,128)(2,1)S(1)} %collective-permute-done.1.refs_2_.refs_5_) | copy-start | bytes 2359300
  66.6 6.2 %collective-permute-start.6 = (bf16[512,768]{1,0:T(8,128)(2,1)S(1)}, bf16[512,768]{1,0:T(8,128)(2,1)S(1)}, u32[]{:S(2)}, u32[]{:S(2)}) collective-permute-start(bf16[512,768]{1,0:T(8,128)(2,1)S(1)} %collective-permute-done.1.refs_2_.refs_5_), channel_id=1, source_target_pairs={{0,8},{8,0},{16,24},{24,16},{1,9},{9,1},{17,25},{25,17},{2,10},{10... | collective-permute-start | bytes 2359304 | tf_op jit(solution)/shard_map/ppermute | solution.py:423
  72.9 2.3 copy-start.23
  72.9 2.3 collective-permute-start.8
  72.9 2.3 copy-start.24
  136.5 15.9 %collective-permute-start.15 = (bf16[392,768]{1,0:T(8,128)(2,1)}, bf16[392,768]{1,0:T(8,128)(2,1)S(1)}, u32[]{:S(2)}, u32[]{:S(2)}) collective-permute-start(bf16[392,768]{1,0:T(8,128)(2,1)} %get-tuple-element.86), channel_id=1, source_target_pairs={{0,1},{1,0},{2,3},{3,2},{4,5},{5,4},{6,7},{7,6},{8,9},{9,8},{10,11... | collective-permute-start | bytes 1806344 | tf_op jit(solution)/shard_map/ppermute | solution.py:423
  152.3 2.5 copy-start.14
  153.7 1.0 copy-start.3
  155.5 8.9 %collective-permute-start.18 = (bf16[104,768]{1,0:T(8,128)(2,1)}, bf16[104,768]{1,0:T(8,128)(2,1)}, u32[]{:S(2)}, u32[]{:S(2)}) collective-permute-start(bf16[104,768]{1,0:T(8,128)(2,1)} %get-tuple-element.102), channel_id=1, source_target_pairs={{0,6},{1,7},{2,4},{3,5},{4,2},{5,3},{6,0},{7,1},{8,14},{9,15},{10,... | collective-permute-start | bytes 479240 | tf_op jit(solution)/shard_map/ppermute | solution.py:423
  157.2 26.4 %collective-permute-start.17 = (bf16[104,768]{1,0:T(8,128)(2,1)S(1)}, bf16[104,768]{1,0:T(8,128)(2,1)}, u32[]{:S(2)}, u32[]{:S(2)}) collective-permute-start(bf16[104,768]{1,0:T(8,128)(2,1)S(1)} %get-tuple-element.101), channel_id=1, source_target_pairs={{0,4},{1,5},{2,6},{3,7},{4,0},{5,1},{6,2},{7,3},{8,12},{9,13},{10,... | collective-permute-start | bytes 479240 | tf_op jit(solution)/shard_map/ppermute | solution.py:423
  159.0 24.6 %collective-permute-start.16 = (bf16[104,768]{1,0:T(8,128)(2,1)S(1)}, bf16[104,768]{1,0:T(8,128)(2,1)}, u32[]{:S(2)}, u32[]{:S(2)}) collective-permute-start(bf16[104,768]{1,0:T(8,128)(2,1)S(1)} %get-tuple-element.100), channel_id=1, source_target_pairs={{0,2},{1,3},{2,0},{3,1},{4,6},{5,7},{6,4},{7,5},{8,10},{9,11},{10,... | collective-permute-start | bytes 479240 | tf_op jit(solution)/shard_map/ppermute | solution.py:423
  159.9 31.2 %collective-permute-start.11 = (bf16[1024,768]{1,0:T(8,128)(2,1)}, bf16[1024,768]{1,0:T(8,128)(2,1)S(1)}, u32[]{:S(2)}, u32[]{:S(2)}) collective-permute-start(bf16[1024,768]{1,0:T(8,128)(2,1)} %get-tuple-element.76), channel_id=1, source_target_pairs={{0,8},{8,0},{16,24},{24,16},{1,9},{9,1},{17,25},{25,17},{2,10},{10... | collective-permute-start | bytes 4718600 | tf_op jit(solution)/shard_map/ppermute | solution.py:423
  160.6 51.2 %collective-permute-start.9 = (bf16[1024,768]{1,0:T(8,128)(2,1)}, bf16[1024,768]{1,0:T(8,128)(2,1)S(1)}, u32[]{:S(2)}, u32[]{:S(2)}) collective-permute-start(bf16[1024,768]{1,0:T(8,128)(2,1)} %get-tuple-element.73), channel_id=1, source_target_pairs={{0,8},{8,0},{16,24},{24,16},{1,9},{9,1},{17,25},{25,17},{2,10},{10... | collective-permute-start | bytes 4718600 | tf_op jit(solution)/shard_map/ppermute | solution.py:423
  161.1 31.6 %copy-start.6 = (bf16[512,768]{1,0:T(8,128)(2,1)S(1)}, bf16[512,768]{1,0:T(8,128)(2,1)}, u32[]{:S(2)}) copy-start(bf16[512,768]{1,0:T(8,128)(2,1)} %get-tuple-element.77) | copy-start | bytes 2359300
  164.4 45.1 %collective-permute-start.13 = (bf16[1024,768]{1,0:T(8,128)(2,1)}, bf16[1024,768]{1,0:T(8,128)(2,1)S(1)}, u32[]{:S(2)}, u32[]{:S(2)}) collective-permute-start(bf16[1024,768]{1,0:T(8,128)(2,1)} %get-tuple-element.79), channel_id=1, source_target_pairs={{0,8},{8,0},{16,24},{24,16},{1,9},{9,1},{17,25},{25,17},{2,10},{10... | collective-permute-start | bytes 4718600 | tf_op jit(solution)/shard_map/ppermute | solution.py:423
  185.5 15.5 %collective-permute-start.21 = (bf16[96,768]{1,0:T(8,128)(2,1)}, bf16[96,768]{1,0:T(8,128)(2,1)S(1)}, u32[]{:S(2)}, u32[]{:S(2)}) collective-permute-start(bf16[96,768]{1,0:T(8,128)(2,1)} %add_convert_fusion.3.refs_1_), channel_id=1, source_target_pairs={{0,2},{1,3},{2,0},{3,1},{4,6},{5,7},{6,4},{7,5},{8,10},{9,11},{10,... | collective-permute-start | bytes 442376 | tf_op jit(solution)/shard_map/ppermute | solution.py:423
  185.5 19.7 %collective-permute-start.22 = (bf16[96,768]{1,0:T(8,128)(2,1)}, bf16[96,768]{1,0:T(8,128)(2,1)S(1)}, u32[]{:S(2)}, u32[]{:S(2)}) collective-permute-start(bf16[96,768]{1,0:T(8,128)(2,1)} %add_convert_fusion.3.refs_1_), channel_id=1, source_target_pairs={{0,4},{1,5},{2,6},{3,7},{4,0},{5,1},{6,2},{7,3},{8,12},{9,13},{10,... | collective-permute-start | bytes 442376 | tf_op jit(solution)/shard_map/ppermute | solution.py:423
  191.1 18.4 %copy-start.1 = (bf16[1024,768]{1,0:T(8,128)(2,1)}, bf16[1024,768]{1,0:T(8,128)(2,1)S(1)}, u32[]{:S(2)}) copy-start(bf16[1024,768]{1,0:T(8,128)(2,1)S(1)} %collective-permute-done.11.refs_5_) | copy-start | bytes 4718596
  191.1 17.6 %collective-permute-start.23 = (bf16[96,768]{1,0:T(8,128)(2,1)}, bf16[96,768]{1,0:T(8,128)(2,1)S(1)}, u32[]{:S(2)}, u32[]{:S(2)}) collective-permute-start(bf16[96,768]{1,0:T(8,128)(2,1)} %add_convert_fusion.3.refs_1_), channel_id=1, source_target_pairs={{0,6},{1,7},{2,4},{3,5},{4,2},{5,3},{6,0},{7,1},{8,14},{9,15},{10,... | collective-permute-start | bytes 442376 | tf_op jit(solution)/shard_map/ppermute | solution.py:423
  192.7 16.8 %copy-start.7 = (bf16[512,768]{1,0:T(8,128)(2,1)S(1)}, bf16[512,768]{1,0:T(8,128)(2,1)}, u32[]{:S(2)}) copy-start(bf16[512,768]{1,0:T(8,128)(2,1)} %get-tuple-element.80) | copy-start | bytes 2359300
  193.8 18.0 %copy-start.8 = (bf16[512,768]{1,0:T(8,128)(2,1)S(1)}, bf16[512,768]{1,0:T(8,128)(2,1)}, u32[]{:S(2)}) copy-start(bf16[512,768]{1,0:T(8,128)(2,1)} %get-tuple-element.74) | copy-start | bytes 2359300
  201.0 9.9 %copy-start.9 = (bf16[96,768]{1,0:T(8,128)(2,1)}, bf16[96,768]{1,0:T(8,128)(2,1)S(1)}, u32[]{:S(2)}) copy-start(bf16[96,768]{1,0:T(8,128)(2,1)S(1)} %collective-permute-done.21.refs_2_) | copy-start | bytes 442372
  201.0 13.4 %collective-permute-start.19 = (f32[2,768]{1,0:T(2,128)S(1)}, f32[2,768]{1,0:T(2,128)S(1)}, u32[]{:S(2)}, u32[]{:S(2)}) collective-permute-start(f32[2,768]{1,0:T(2,128)S(1)} %slice_bitcast_fusion.3), channel_id=1, source_target_pairs={{0,8},{8,0},{16,24},{24,16},{1,9},{9,1},{17,25},{25,17},{2,10},{10... | collective-permute-start | bytes 18440 | tf_op jit(solution)/shard_map/ppermute | solution.py:423
  205.1 5.7 %copy-start.10 = (bf16[96,768]{1,0:T(8,128)(2,1)}, bf16[96,768]{1,0:T(8,128)(2,1)S(1)}, u32[]{:S(2)}) copy-start(bf16[96,768]{1,0:T(8,128)(2,1)S(1)} %collective-permute-done.22.refs_3_) | copy-start | bytes 442372
  205.2 58.9 %collective-permute-start.12 = (bf16[512,768]{1,0:T(8,128)(2,1)}, bf16[512,768]{1,0:T(8,128)(2,1)}, u32[]{:S(2)}, u32[]{:S(2)}) collective-permute-start(bf16[512,768]{1,0:T(8,128)(2,1)} %add_convert_fusion.1), channel_id=1, source_target_pairs={{0,16},{8,24},{16,0},{24,8},{1,17},{9,25},{17,1},{25,9},{2,18},{10... | collective-permute-start | bytes 2359304 | tf_op jit(solution)/shard_map/ppermute | solution.py:423
  208.7 2.2 copy-start.11
  209.5 50.9 %collective-permute-start.25 = (bf16[288,768]{1,0:T(8,128)(2,1)}, bf16[288,768]{1,0:T(8,128)(2,1)}, u32[]{:S(2)}, u32[]{:S(2)}) collective-permute-start(bf16[288,768]{1,0:T(8,128)(2,1)} %pad_maximum_fusion), channel_id=1, source_target_pairs={{0,1},{1,0},{2,3},{3,2},{4,5},{5,4},{6,7},{7,6},{8,9},{9,8},{10,11... | collective-permute-start | bytes 1327112 | tf_op jit(solution)/shard_map/ppermute | solution.py:423
  209.5 3.6 %copy-start.2 = (bf16[1024,768]{1,0:T(8,128)(2,1)}, bf16[1024,768]{1,0:T(8,128)(2,1)S(1)}, u32[]{:S(2)}) copy-start(bf16[1024,768]{1,0:T(8,128)(2,1)S(1)} %collective-permute-done.13.refs_8_) | copy-start | bytes 4718596
  210.9 47.0 %copy-start.13 = (f32[768]{0:T(1024)S(1)}, f32[768]{0:T(1024)}, u32[]{:S(2)}) copy-start(f32[768]{0:T(1024)} %refs_2_.5) | copy-start | bytes 9220
  210.9 53.2 %collective-permute-start.14 = (bf16[512,768]{1,0:T(8,128)(2,1)}, bf16[512,768]{1,0:T(8,128)(2,1)S(1)}, u32[]{:S(2)}, u32[]{:S(2)}) collective-permute-start(bf16[512,768]{1,0:T(8,128)(2,1)} %add_convert_fusion), channel_id=1, source_target_pairs={{0,16},{8,24},{16,0},{24,8},{1,17},{9,25},{17,1},{25,9},{2,18},{10... | collective-permute-start | bytes 2359304 | tf_op jit(solution)/shard_map/ppermute | solution.py:423
  211.8 52.3 %copy-start = (bf16[1024,768]{1,0:T(8,128)(2,1)}, bf16[1024,768]{1,0:T(8,128)(2,1)S(1)}, u32[]{:S(2)}) copy-start(bf16[1024,768]{1,0:T(8,128)(2,1)S(1)} %collective-permute-done.9.refs_5_) | copy-start | bytes 4718596
  213.1 79.1 %collective-permute-start.10 = (bf16[512,768]{1,0:T(8,128)(2,1)}, bf16[512,768]{1,0:T(8,128)(2,1)S(1)}, u32[]{:S(2)}, u32[]{:S(2)}) collective-permute-start(bf16[512,768]{1,0:T(8,128)(2,1)} %add_convert_fusion.2), channel_id=1, source_target_pairs={{0,16},{8,24},{16,0},{24,8},{1,17},{9,25},{17,1},{25,9},{2,18},{10... | collective-permute-start | bytes 2359304 | tf_op jit(solution)/shard_map/ppermute | solution.py:423
  214.4 40.6 %collective-permute-start.20 = (f32[2,768]{1,0:T(2,128)S(1)}, f32[2,768]{1,0:T(2,128)S(1)}, u32[]{:S(2)}, u32[]{:S(2)}) collective-permute-start(f32[2,768]{1,0:T(2,128)S(1)} %fusion), channel_id=1, source_target_pairs={{0,16},{8,24},{16,0},{24,8},{1,17},{9,25},{17,1},{25,9},{2,18},{10... | collective-permute-start | bytes 18440 | tf_op jit(solution)/shard_map/ppermute | solution.py:423
  255.0 5.4 %collective-permute-start.24 = (bf16[96,768]{1,0:T(8,128)(2,1)}, bf16[96,768]{1,0:T(8,128)(2,1)S(1)}, u32[]{:S(2)}, u32[]{:S(2)}) collective-permute-start(bf16[96,768]{1,0:T(8,128)(2,1)} %add_convert_fusion.3.refs_1_), channel_id=1, source_target_pairs={{0,1},{1,0},{2,3},{3,2},{4,5},{5,4},{6,7},{7,6},{8,9},{9,8},{10,11... | collective-permute-start | bytes 442376 | tf_op jit(solution)/shard_map/ppermute | solution.py:423
  (5 other events, 4.3 us)
Sparse Core Ops, SparseCore 0:
  161.2 126.8 all-reduce.1

commit v3 on v2

--- a/solution.py
+++ b/solution.py
@@ -82,7 +82,7 @@
         acc, accb = take(2)
     buf, w1, w2, b1, o_s, n_s, sem, weight_sem, prior_sem, o_sem, n_sem = take(11)
     if last:
-        (acc,) = take(1)
+        acc, sum_s, sum_sem = take(3)
     rows = packs[0].shape[0] // 2
     width = w1.shape[0]
     inv_sqrt2 = 2.0**-0.5
@@ -156,8 +156,11 @@
 
     lax.fori_loop(0, blocks, step, 0)
     if last:
+        sum_s[...] = acc[...].astype(BF16)
+        out = pltpu.make_async_copy(sum_s, summed, sum_sem)
+        out.start()
         accb[2:3] = as_row(jnp.sum(w1[...].astype(F32) * acc[0:width], axis=1, keepdims=True))
-        summed[...] = acc[...].astype(BF16)
+        out.wait()
     for k in range(blocks - 2, blocks):
         for write in writes(k, k & 1):
             write.wait()
@@ -175,18 +178,17 @@
     ff_small_in = take(1) if last else []
     keep_near, keep_far, send = take(3)
     if last:
-        pieces = take(len(refs) - 34)
+        pieces = take(len(refs) - 36)
         (small,) = take(1)
     else:
         acc, accg = take(2)
     jt, dot_s, qs_t, qt_s, k_s, kt_s, v_s, vt_s, es, dqt, dk, dv, ot, djt = take(14)
     ff_s, ff_sem, prior_sem, out_s, out_sem, dot_bs, r_s, pack_s, pack_sem = take(9)
-    wqkv, wproj, qg, kg, gain_s, small_s, weight_sem, tail_sem = take(8)
+    wqkv, wproj, qg, kg, gain_s, small_s, weight_sem, tail_sem, o_acc, inv_s = take(10)
     if last:
         acc, accg = take(2)
     rows = parts[0].shape[0] // 2
     joined = wqkv.shape[0]
-    total = rows * blocks
     scale = size**-0.5
     up = scale * math.log2(math.e)
     loads = [pltpu.make_async_copy(weights[j], to, weight_sem.at[j]) for j, to in enumerate((wqkv, wproj, qg, kg))]
@@ -235,10 +237,15 @@
     def prepare(h, carry):
         base = pl.multiple_of(h * 3 * size, size)
         gh = pl.ds(pl.multiple_of(h * size, size), size)
-        part = lambda c: jt[pl.ds(pl.multiple_of(base + c * size, size), size), :]
-        qt = normed(part(0))[0] * qg[gh, :]
-        kt = normed(part(1))[0] * kg[gh, :]
-        vt = part(2)
+        at = lambda c: pl.ds(pl.multiple_of(base + c * size, size), size)
+        scaled = []
+        for c, gain in ((0, qg), (1, kg)):
+            unit, r = normed(jt[at(c), :])
+            jt[at(c), :] = unit
+            inv_s[pl.ds(2 * h + c, 1), :] = r
+            scaled.append(unit * gain[gh, :])
+        qt, kt = scaled
+        vt = jt[at(2), :]
         qs_t[h] = (qt * up).astype(BF16)
         qt_s[h] = qt.astype(BF16)
         k_s[h] = kt.T.astype(BF16)
@@ -258,33 +265,32 @@
     dk[...] = jnp.zeros(dk.shape, F32)
     dv[...] = jnp.zeros(dv.shape, F32)
 
-    def forward(j, accs):
+    def forward(j, carry):
         b = j ^ pos[0]
         start = pl.multiple_of(b * rows, rows)
         slot = lax.broadcasted_iota(jnp.int32, (rows, 1), 0) + j * rows
-        out = []
         for h in range(heads):
             s = mm(k_s[h, pl.ds(start, rows), :], qs_t[h])
             e = jnp.where(slot < live, jnp.exp2(s), 0.0).astype(BF16)
             es[h, b] = e
-            out.append(accs[h] + mm(vt_s[h, b], e))
-        return tuple(out)
-
-    zero = jnp.zeros((size + 16, total), F32)
-    accs = lax.fori_loop(0, count, forward, (zero,) * heads)
+            o_acc[h] += mm(vt_s[h, b], e)
+        return carry
+
+    o_acc[...] = jnp.zeros(o_acc.shape, F32)
+    dqt[...] = jnp.zeros(dqt.shape, F32)
+    lax.fori_loop(0, count, forward, 0)
     for h in range(heads):
-        inv = 1.0 / accs[h][size : size + 1]
-        o = accs[h][0:size] * inv
+        inv = 1.0 / o_acc[h, size : size + 1]
+        o = o_acc[h, 0:size] * inv
         hs = slice(h * size, (h + 1) * size)
         ot[hs] = o.astype(BF16)
         dot_b = (dot_s[hs] * inv).astype(BF16)
         dot_bs[hs] = dot_b
         r_s[h : h + 1] = jnp.sum(dot_b.astype(F32) * o, axis=0, keepdims=True)
 
-    def backward(j, accs):
+    def backward(j, carry):
         b = j ^ pos[0]
         start = pl.multiple_of(b * rows, rows)
-        out = []
         for h in range(heads):
             dot_b = dot_bs[h * size : (h + 1) * size]
             dp = mm(v_s[h, pl.ds(start, rows), :], dot_b)
@@ -292,20 +298,17 @@
             ds = (e.astype(F32) * (dp - r_s[h : h + 1])).astype(BF16)
             dv[h, b] = mm(dot_b, e, NT)
             dk[h, b] = mm(qt_s[h], ds, NT)
-            out.append(accs[h] + mm(kt_s[h, b], ds))
-        return tuple(out)
-
-    zero = jnp.zeros((size, total), F32)
-    accs = lax.fori_loop(0, count, backward, (zero,) * heads)
-    for h in range(heads):
-        dqt[h] = accs[h]
+            dqt[h] += mm(kt_s[h, b], ds)
+        return carry
+
+    lax.fori_loop(0, count, backward, 0)
 
     def undo(h, carry):
         base = pl.multiple_of(h * 3 * size, size)
         gh = pl.multiple_of(h * size, size)
         for c, gain, grad in ((0, qg, dqt[h]), (1, kg, jnp.concatenate([dk[h, k] for k in range(blocks)], axis=1))):
             at = pl.ds(pl.multiple_of(base + c * size, size), size)
-            n, r = normed(jt[at, :])
+            n, r = jt[at, :], inv_s[pl.ds(2 * h + c, 1), :]
             grad = grad * scale
             y = grad * gain[pl.ds(gh, size), :]
             back = r * (
@@ -469,12 +472,16 @@
         ]
         if last:
             outs += [((width + hidden, width), BF16), ((8, width), F32)]
-            scratch += [pltpu.VMEM((width + hidden, width), F32)]
+            scratch += [
+                pltpu.VMEM((width + hidden, width), F32),
+                pltpu.VMEM((width + hidden, width), BF16),
+                pltpu.SemaphoreType.DMA,
+            ]
         else:
             outs += [((width + hidden, width), F32), ((8, width), F32)]
         res = call(
             functools.partial(ff_kernel, first, last, count, first), outs, 0,
-            *packs, w_fc1, w_fc2, b1, *state, n_any=count + 3 + len(state), any_outs=2,
+            *packs, w_fc1, w_fc2, b1, *state, n_any=count + 3 + len(state), any_outs=3 if last else 2,
             scratch=scratch, flops=12 * count * rows * width * hidden,
         )
         return res[0], res[1], res[2:]
@@ -519,6 +526,8 @@
             pltpu.VMEM((8, width), F32),
             pltpu.SemaphoreType.DMA((4,)),
             pltpu.SemaphoreType.DMA((2,)),
+            pltpu.VMEM((heads, size + 16, total), F32),
+            pltpu.VMEM((8, total), F32),
         ]
         if last:
             outs += qp_pieces + [((8, width), BF16)]

time: 304 us -> 301 us (level)
    ppermute x26, waiting for transfers between devices: 101 us -> 104 us  [swap(): return lax.ppermute(v, axis, [(i, i ^ mask) for i in range(count)])]
where the time goes in v3:
time: 301 us
  waiting for transfers between devices  121 us (40%)
  Pallas kernels  118 us (39%)
  starting transfers between devices  21 us (7%)
  between operations  14.3 us (5%)
  other arithmetic  14.1 us (5%)
  local copies, waits for them, and re-layouts  12.3 us (4%)
    pallas_call x8, Pallas kernels, call(): pl.pallas_call(kernel, out_shape=[jax.ShapeDtypeStruct(s, d) for s, d in...  109 us
    ppermute x26, waiting for transfers between devices, swap(): return lax.ppermute(v, axis, [(i, i ^ mask) for i in range(count)])  104 us
    ppermute x26, starting transfers between devices, swap(): return lax.ppermute(v, axis, [(i, i ^ mask) for i in range(count)])  20.9 us
    psum x1, waiting for transfers between devices, block(): fc = lax.psum(ff_out, 'dp')  16.9 us
    pallas_call x2, Pallas kernels, finish(): pl.pallas_call(functools.partial(final_kernel, end - begin), grid=(end -...  8.8 us
  transfers between devices with their start and end apart: 27, of which 12 were waited for; matrix products, arithmetic and copies ran while one was open for 6% of the time, Pallas kernels for 17%

profile of v3, /device:TPU:0, one launch (start us, length us, event | category | flops | bytes accessed | tf_op | source)
XLA Modules:
  0.0 300.6 jit_solution(11223297302170865582)
XLA Ops:
  7.2 4.0 %shard_map.203 = (bf16[512,768]{1,0:T(8,128)(2,1)}, bf16[512,768]{1,0:T(8,128)(2,1)}, bf16[512,768]{1,0:T(8,128)(2,1)}) custom-call(bf16[3,256,768]{2,1,0:T(8,128)(2,1)} %refs_0_.3, bf16[3,256,768]{2,1,0:T(8,128)(2,1)} %refs_1_.3, f32[768]{0:T(1024)} %refs_2_.5), custom_call_target="tpu_custom_call" | custom-call | bytes 4721664 | tf_op jit(solution)/shard_map/pallas_call | solution.py:31
  12.3 2.6 collective-permute-start.3
  15.1 1.0 collective-permute-done.4.refs_3_.refs_4_
  16.1 0.9 copy-done.21
  17.0 17.8 %shard_map.204 = (bf16[1536,768]{1,0:T(8,128)(2,1)}, bf16[1536,768]{1,0:T(8,128)(2,1)}, f32[1536,768]{1,0:T(8,128)}, f32[8,768]{1,0:T(8,128)}) custom-call(bf16[512,768]{1,0:T(8,128)(2,1)} %get-tuple-element.52.refs_0_.refs_3_, bf16[512,768]{1,0:T(8,128)(2,1)} %collective-permute-done.2.refs_1_.refs_4_, bf16[512,768]{1,0:T(8,128)(2,1)} %get-tuple-element.53.refs_2_.refs_3_, ...), custom_call_target="tpu_custom_call" | custom-call | flops 10871635968 | bytes 16542720 | tf_op jit(solution)/shard_map/pallas_call | solution.py:31
  35.3 2.6 collective-permute-start.1
  38.0 0.8 reshape.36.refs_13_.refs_14_
  38.8 0.8 reshape.37.refs_14_.refs_15_
  40.1 9.9 %shard_map.205 = (bf16[512,768]{1,0:T(8,128)(2,1)}, bf16[512,768]{1,0:T(8,128)(2,1)}, f32[1536,768]{1,0:T(8,128)}, f32[8,768]{1,0:T(8,128)}) custom-call(bf16[512,768]{1,0:T(8,128)(2,1)} %collective-permute-done.3.refs_0_.refs_5_, bf16[512,768]{1,0:T(8,128)(2,1)} %collective-permute-done.5.refs_1_.refs_6_, bf16[768,768]{1,0:T(8,128)(2,1)} %refs_4_.3, ...), custom_call_target="tpu_custom_call" | custom-call | flops 3623878656 | bytes 14994432 | tf_op jit(solution)/shard_map/pallas_call | solution.py:31
  50.1 15.7 %shard_map.206 = (bf16[512,768]{1,0:T(8,128)(2,1)}, bf16[512,768]{1,0:T(8,128)(2,1)}, bf16[1024,768]{1,0:T(8,128)(2,1)}, f32[768,768]{1,0:T(8,128)}, f32[384,1]{1,0:T(8,128)}) custom-call(s32[1]{0:T(128)} %get-tuple-element.105.refs_0_, s32[1]{0:T(128)} %bitcast.refs_1_, s32[1]{0:T(128)} %bitcast.1.refs_2_, ...), custom_call_target="tpu_custom_call" | custom-call | flops 14495514624 | bytes 16124940 | tf_op jit(solution)/shard_map/pallas_call | solution.py:31
  66.0 6.9 %collective-permute-done.7.refs_0_.refs_5_ = bf16[512,768]{1,0:T(8,128)(2,1)S(1)} collective-permute-done((bf16[512,768]{1,0:T(8,128)(2,1)S(1)}, bf16[512,768]{1,0:T(8,128)(2,1)S(1)}, u32[]{:S(2)}, u32[]{:S(2)}) %collective-permute-start.7) | collective-permute-done | bytes 786464 | tf_op jit(solution)/shard_map/ppermute | solution.py:426
  72.9 2.3 collective-permute-done.8.refs_1_.refs_6_
  75.2 0.9 copy-done.25
  76.0 14.8 %shard_map.207 = (bf16[1024,768]{1,0:T(8,128)(2,1)}, bf16[1024,768]{1,0:T(8,128)(2,1)}, bf16[1536,768]{1,0:T(8,128)(2,1)}, f32[8,768]{1,0:T(8,128)}) custom-call(bf16[512,768]{1,0:T(8,128)(2,1)} %copy-done.23, bf16[512,768]{1,0:T(8,128)(2,1)} %copy-done.25, bf16[512,768]{1,0:T(8,128)(2,1)} %copy-done.22, bf16[512,768]{1,0:T(8,128)(2,1)} %copy-done.24, ...), custom_call_target="tpu_custom_call" | custom-call | flops 7247757312 | bytes 15780864 | tf_op jit(solution)/shard_map/pallas_call | solution.py:31
  90.9 20.6 %shard_map.208 = (bf16[512,768]{1,0:T(8,128)(2,1)}, bf16[512,768]{1,0:T(8,128)(2,1)}, bf16[1024,768]{1,0:T(8,128)(2,1)}, f32[768,768]{1,0:T(8,128)}, f32[384,1]{1,0:T(8,128)}) custom-call(s32[1]{0:T(128)} %get-tuple-element.103.refs_0_, s32[1]{0:T(128)} %bitcast.refs_1_, s32[1]{0:T(128)} %bitcast.1.refs_2_, ...), custom_call_target="tpu_custom_call" | custom-call | flops 14495514624 | bytes 20058636 | tf_op jit(solution)/shard_map/pallas_call | solution.py:31
  111.5 23.1 %shard_map.209 = (bf16[512,768]{1,0:T(8,128)(2,1)}, bf16[512,768]{1,0:T(8,128)(2,1)}, bf16[1024,768]{1,0:T(8,128)(2,1)}, f32[384,768]{1,0:T(8,128)}, bf16[392,768]{1,0:T(8,128)(2,1)}, /*index=5*/bf16[8,768]{1,0:T(8,128)(2,1)}) custom-call(s32[1]{0:T(128)} %get-tuple-element.104.refs_0_, s32[1]{0:T(128)} %bitcast.refs_1_, s32[1]{0:T(128)} %bitcast.1.refs_2_, ...), custom_call_target="tpu_custom_call" | custom-call | flops 14495514624 | bytes 19516428 | tf_op jit(solution)/shard_map/pallas_call | solution.py:31
  134.7 15.8 %collective-permute-done.15 = bf16[392,768]{1,0:T(8,128)(2,1)S(1)} collective-permute-done((bf16[392,768]{1,0:T(8,128)(2,1)}, bf16[392,768]{1,0:T(8,128)(2,1)S(1)}, u32[]{:S(2)}, u32[]{:S(2)}) %collective-permute-start.15) | collective-permute-done | bytes 602144 | tf_op jit(solution)/shard_map/ppermute | solution.py:426
  150.5 1.4 convert_add_fusion
  151.9 1.0 copy-done.3
  153.0 0.7 pad_maximum_fusion.3
  153.7 0.7 collective-permute-start.18
  154.4 1.6 collective-permute-start.17
  156.0 2.1 collective-permute-start.16
  159.3 3.6 %collective-permute-done.18 = bf16[104,768]{1,0:T(8,128)(2,1)} collective-permute-done((bf16[104,768]{1,0:T(8,128)(2,1)}, bf16[104,768]{1,0:T(8,128)(2,1)}, u32[]{:S(2)}, u32[]{:S(2)}) %collective-permute-start.18) | collective-permute-done | bytes 159776 | tf_op jit(solution)/shard_map/ppermute | solution.py:426
  162.9 19.7 %collective-permute-done.17 = bf16[104,768]{1,0:T(8,128)(2,1)} collective-permute-done((bf16[104,768]{1,0:T(8,128)(2,1)S(1)}, bf16[104,768]{1,0:T(8,128)(2,1)}, u32[]{:S(2)}, u32[]{:S(2)}) %collective-permute-start.17) | collective-permute-done | bytes 159776 | tf_op jit(solution)/shard_map/ppermute | solution.py:426
  182.6 1.9 add_convert_fusion.3.refs_1_
  184.5 1.6 collective-permute-start.22
  186.1 0.7 slice_bitcast_fusion
  186.8 0.7 slice_bitcast_fusion.1
  187.5 0.7 slice_bitcast_fusion.2
  188.9 2.9 collective-permute-start.23
  191.8 1.1 add_convert_fusion.1
  192.9 6.1 %collective-permute-done.21.refs_2_ = bf16[96,768]{1,0:T(8,128)(2,1)S(1)} collective-permute-done((bf16[96,768]{1,0:T(8,128)(2,1)}, bf16[96,768]{1,0:T(8,128)(2,1)S(1)}, u32[]{:S(2)}, u32[]{:S(2)}) %collective-permute-start.21) | collective-permute-done | bytes 147488 | tf_op jit(solution)/shard_map/ppermute | solution.py:426
  198.9 6.1 %collective-permute-done.22.refs_3_ = bf16[96,768]{1,0:T(8,128)(2,1)S(1)} collective-permute-done((bf16[96,768]{1,0:T(8,128)(2,1)}, bf16[96,768]{1,0:T(8,128)(2,1)S(1)}, u32[]{:S(2)}, u32[]{:S(2)}) %collective-permute-start.22) | collective-permute-done | bytes 147488 | tf_op jit(solution)/shard_map/ppermute | solution.py:426
  205.0 1.7 collective-permute-start.12
  206.7 0.8 pad_maximum_fusion
  207.6 1.3 add_convert_fusion
  209.6 1.4 add_convert_fusion.2
  210.9 1.5 collective-permute-start.10
  213.1 39.9 %collective-permute-done.20 = f32[2,768]{1,0:T(2,128)S(1)} collective-permute-done((f32[2,768]{1,0:T(2,128)S(1)}, f32[2,768]{1,0:T(2,128)S(1)}, u32[]{:S(2)}, u32[]{:S(2)}) %collective-permute-start.20) | collective-permute-done | bytes 6176 | tf_op jit(solution)/shard_map/ppermute | solution.py:426
  255.6 2.7 collective-permute-done.24.refs_5_
  258.9 3.0 %shard_map.212 = (f32[576,768]{1,0:T(8,128)}, f32[192,768]{1,0:T(8,128)}) custom-call(s32[2]{0:T(128)} %pad_add_fusion.refs_0_, bf16[96,768]{1,0:T(8,128)(2,1)} %add_convert_fusion.3.refs_1_, bf16[96,768]{1,0:T(8,128)(2,1)} %copy-done.9, bf16[96,768]{1,0:T(8,128)(2,1)} %copy-done.10, bf16[96,768]{1,0:T(8,128)(2,1)} %copy-done.11, ...), custom_call_target="tpu_custom_call" | custom-call | bytes 3538952 | tf_op jit(solution)/shard_map/pallas_call | solution.py:31
  262.0 1.0 copy-done.5
  263.0 5.3 %shard_map.210 = (bf16[3,256,768]{2,1,0:T(8,128)(2,1)}, f32[3,256,768]{2,1,0:T(8,128)}) custom-call(bf16[3,256,768]{2,1,0:T(8,128)(2,1)} %refs_0_.3, bf16[3,256,768]{2,1,0:T(8,128)(2,1)} %refs_1_.3, f32[768]{0:T(1024)} %refs_2_.5, f32[768]{0:T(1024)} %refs_3_.5, bf16[512,768]{1,0:T(8,128)(2,1)} %get-tuple-element.75.refs_4_, bf16[1024,768]{1,0:T(8,128)(2,1)} %copy-done.1, ...), custom_call_target="tpu_custom_call" | custom-call | tf_op jit(solution)/shard_map/pallas_call | solution.py:611
  268.2 16.9 %all-reduce.2.cloned.1.call-done = bf16[1536,768]{1,0:T(8,128)(2,1)} async-done(((bf16[1536,768]{1,0:T(8,128)(2,1)}), bf16[1536,768]{1,0:T(8,128)(2,1)}) %all-reduce.2.cloned.1.call-update) | async-done | bytes 2359312 | tf_op jit(solution)/shard_map/psum | solution.py:587
  285.1 4.2 %slice_convert_fusion = (f32[768,768]{1,0:T(8,128)}, f32[768,768]{1,0:T(8,128)}) fusion(bf16[1536,768]{1,0:T(8,128)(2,1)} %all-reduce.2.cloned.1.call-done), kind=kLoop, calls=%fused_computation.3 | loop fusion | flops 1179648 | bytes 7077888 | tf_op jit(solution)/shard_map/convert_element_type | solution.py:602
  289.3 0.9 copy-done.4
  290.2 3.5 %shard_map.211 = (bf16[3,256,768]{2,1,0:T(8,128)(2,1)}, f32[3,256,768]{2,1,0:T(8,128)}) custom-call(bf16[3,256,768]{2,1,0:T(8,128)(2,1)} %refs_0_.3, bf16[3,256,768]{2,1,0:T(8,128)(2,1)} %refs_1_.3, f32[768]{0:T(1024)} %refs_2_.5, f32[768]{0:T(1024)} %refs_3_.5, ...), custom_call_target="tpu_custom_call", output_to_operand_aliasing={{0}: (7, {}), {1}: (8, {})} | custom-call | tf_op jit(solution)/shard_map/pallas_call | solution.py:611
  (98 shorter events, 9.3 us)
Async XLA Ops:
  7.2 277.9 %all-reduce.2.cloned.1.call-start = ((), (), s32[]{:S(2)}) async-start(), calls=%async_computation | async-start | bytes 4718592 | tf_op jit(solution)/shard_map/psum | solution.py:587
  11.2 3.7 %collective-permute-start = (bf16[512,768]{1,0:T(8,128)(2,1)}, bf16[512,768]{1,0:T(8,128)(2,1)S(1)}, u32[]{:S(2)}, u32[]{:S(2)}) collective-permute-start(bf16[512,768]{1,0:T(8,128)(2,1)} %get-tuple-element.51.refs_4_.refs_3_), channel_id=1, source_target_pairs={{0,8},{8,0},{16,24},{24,16},{1,9},{9,1},{17,25},{25,17},{2,10},{10... | collective-permute-start | bytes 2359304 | tf_op jit(solution)/shard_map/ppermute | solution.py:426
  11.7 3.4 %collective-permute-start.2 = (bf16[512,768]{1,0:T(8,128)(2,1)}, bf16[512,768]{1,0:T(8,128)(2,1)}, u32[]{:S(2)}, u32[]{:S(2)}) collective-permute-start(bf16[512,768]{1,0:T(8,128)(2,1)} %get-tuple-element.52.refs_0_.refs_3_), channel_id=1, source_target_pairs={{0,8},{8,0},{16,24},{24,16},{1,9},{9,1},{17,25},{25,17},{2,10},{10... | collective-permute-start | bytes 2359304 | tf_op jit(solution)/shard_map/ppermute | solution.py:426
  11.8 23.5 %copy-start.18 = (bf16[512,768]{1,0:T(8,128)(2,1)S(1)}, bf16[512,768]{1,0:T(8,128)(2,1)}, u32[]{:S(2)}) copy-start(bf16[512,768]{1,0:T(8,128)(2,1)} %get-tuple-element.51.refs_4_.refs_3_) | copy-start | bytes 2359300
  11.8 26.1 %copy-start.20 = (bf16[512,768]{1,0:T(8,128)(2,1)S(1)}, bf16[512,768]{1,0:T(8,128)(2,1)}, u32[]{:S(2)}) copy-start(bf16[512,768]{1,0:T(8,128)(2,1)} %get-tuple-element.53.refs_2_.refs_3_) | copy-start | bytes 2359300
  11.8 26.2 %copy-start.16 = (f32[3,64]{1,0:T(4,128)S(1)}, f32[3,64]{1,0:T(4,128)}, u32[]{:S(2)}) copy-start(f32[3,64]{1,0:T(4,128)} %param.16) | copy-start | bytes 2308
  11.8 26.9 %copy-start.17 = (f32[3,64]{1,0:T(4,128)S(1)}, f32[3,64]{1,0:T(4,128)}, u32[]{:S(2)}) copy-start(f32[3,64]{1,0:T(4,128)} %param.17) | copy-start | bytes 2308
  11.8 27.7 %copy-start.15 = (s32[3]{0:T(128)S(1)}, s32[3]{0:T(128)}, u32[]{:S(2)}) copy-start(s32[3]{0:T(128)} %param.13) | copy-start | bytes 40
  11.8 4.3 %collective-permute-start.4 = (bf16[512,768]{1,0:T(8,128)(2,1)}, bf16[512,768]{1,0:T(8,128)(2,1)S(1)}, u32[]{:S(2)}, u32[]{:S(2)}) collective-permute-start(bf16[512,768]{1,0:T(8,128)(2,1)} %get-tuple-element.53.refs_2_.refs_3_), channel_id=1, source_target_pairs={{0,8},{8,0},{16,24},{24,16},{1,9},{9,1},{17,25},{25,17},{2,10},{10... | collective-permute-start | bytes 2359304 | tf_op jit(solution)/shard_map/ppermute | solution.py:426
  12.3 22.5 %collective-permute-start.3 = (bf16[512,768]{1,0:T(8,128)(2,1)}, bf16[512,768]{1,0:T(8,128)(2,1)}, u32[]{:S(2)}, u32[]{:S(2)}) collective-permute-start(bf16[512,768]{1,0:T(8,128)(2,1)} %get-tuple-element.52.refs_0_.refs_3_), channel_id=1, source_target_pairs={{0,16},{8,24},{16,0},{24,8},{1,17},{9,25},{17,1},{25,9},{2,18},{10... | collective-permute-start | bytes 2359304 | tf_op jit(solution)/shard_map/ppermute | solution.py:426
  14.9 1.2 copy-start.19
  34.8 5.3 %collective-permute-start.5 = (bf16[512,768]{1,0:T(8,128)(2,1)}, bf16[512,768]{1,0:T(8,128)(2,1)}, u32[]{:S(2)}, u32[]{:S(2)}) collective-permute-start(bf16[512,768]{1,0:T(8,128)(2,1)} %collective-permute-done.3.refs_0_.refs_5_), channel_id=1, source_target_pairs={{0,8},{8,0},{16,24},{24,16},{1,9},{9,1},{17,25},{25,17},{2,10},{10... | collective-permute-start | bytes 2359304 | tf_op jit(solution)/shard_map/ppermute | solution.py:426
  35.3 30.5 %collective-permute-start.1 = (bf16[512,768]{1,0:T(8,128)(2,1)S(1)}, bf16[512,768]{1,0:T(8,128)(2,1)S(1)}, u32[]{:S(2)}, u32[]{:S(2)}) collective-permute-start(bf16[512,768]{1,0:T(8,128)(2,1)S(1)} %copy-done.18), channel_id=1, source_target_pairs={{0,16},{8,24},{16,0},{24,8},{1,17},{9,25},{17,1},{25,9},{2,18},{10... | collective-permute-start | bytes 2359304 | tf_op jit(solution)/shard_map/ppermute | solution.py:426
  37.9 34.9 %collective-permute-start.7 = (bf16[512,768]{1,0:T(8,128)(2,1)S(1)}, bf16[512,768]{1,0:T(8,128)(2,1)S(1)}, u32[]{:S(2)}, u32[]{:S(2)}) collective-permute-start(bf16[512,768]{1,0:T(8,128)(2,1)S(1)} %copy-done.20), channel_id=1, source_target_pairs={{0,16},{8,24},{16,0},{24,8},{1,17},{9,25},{17,1},{25,9},{2,18},{10... | collective-permute-start | bytes 2359304 | tf_op jit(solution)/shard_map/ppermute | solution.py:426
  65.8 9.4 %copy-start.22 = (bf16[512,768]{1,0:T(8,128)(2,1)}, bf16[512,768]{1,0:T(8,128)(2,1)S(1)}, u32[]{:S(2)}) copy-start(bf16[512,768]{1,0:T(8,128)(2,1)S(1)} %collective-permute-done.1.refs_2_.refs_5_) | copy-start | bytes 2359300
  65.8 7.1 %collective-permute-start.6 = (bf16[512,768]{1,0:T(8,128)(2,1)S(1)}, bf16[512,768]{1,0:T(8,128)(2,1)S(1)}, u32[]{:S(2)}, u32[]{:S(2)}) collective-permute-start(bf16[512,768]{1,0:T(8,128)(2,1)S(1)} %collective-permute-done.1.refs_2_.refs_5_), channel_id=1, source_target_pairs={{0,8},{8,0},{16,24},{24,16},{1,9},{9,1},{17,25},{25,17},{2,10},{10... | collective-permute-start | bytes 2359304 | tf_op jit(solution)/shard_map/ppermute | solution.py:426
  72.9 2.3 copy-start.23
  72.9 2.3 collective-permute-start.8
  72.9 2.3 copy-start.24
  134.6 15.9 %collective-permute-start.15 = (bf16[392,768]{1,0:T(8,128)(2,1)}, bf16[392,768]{1,0:T(8,128)(2,1)S(1)}, u32[]{:S(2)}, u32[]{:S(2)}) collective-permute-start(bf16[392,768]{1,0:T(8,128)(2,1)} %get-tuple-element.86), channel_id=1, source_target_pairs={{0,1},{1,0},{2,3},{3,2},{4,5},{5,4},{6,7},{7,6},{8,9},{9,8},{10,11... | collective-permute-start | bytes 1806344 | tf_op jit(solution)/shard_map/ppermute | solution.py:426
  150.5 2.5 copy-start.14
  151.9 1.0 copy-start.3
  153.7 9.2 %collective-permute-start.18 = (bf16[104,768]{1,0:T(8,128)(2,1)}, bf16[104,768]{1,0:T(8,128)(2,1)}, u32[]{:S(2)}, u32[]{:S(2)}) collective-permute-start(bf16[104,768]{1,0:T(8,128)(2,1)} %get-tuple-element.102), channel_id=1, source_target_pairs={{0,6},{1,7},{2,4},{3,5},{4,2},{5,3},{6,0},{7,1},{8,14},{9,15},{10,... | collective-permute-start | bytes 479240 | tf_op jit(solution)/shard_map/ppermute | solution.py:426
  154.4 28.2 %collective-permute-start.17 = (bf16[104,768]{1,0:T(8,128)(2,1)S(1)}, bf16[104,768]{1,0:T(8,128)(2,1)}, u32[]{:S(2)}, u32[]{:S(2)}) collective-permute-start(bf16[104,768]{1,0:T(8,128)(2,1)S(1)} %get-tuple-element.101), channel_id=1, source_target_pairs={{0,4},{1,5},{2,6},{3,7},{4,0},{5,1},{6,2},{7,3},{8,12},{9,13},{10,... | collective-permute-start | bytes 479240 | tf_op jit(solution)/shard_map/ppermute | solution.py:426
  156.0 26.6 %collective-permute-start.16 = (bf16[104,768]{1,0:T(8,128)(2,1)S(1)}, bf16[104,768]{1,0:T(8,128)(2,1)}, u32[]{:S(2)}, u32[]{:S(2)}) collective-permute-start(bf16[104,768]{1,0:T(8,128)(2,1)S(1)} %get-tuple-element.100), channel_id=1, source_target_pairs={{0,2},{1,3},{2,0},{3,1},{4,6},{5,7},{6,4},{7,5},{8,10},{9,11},{10,... | collective-permute-start | bytes 479240 | tf_op jit(solution)/shard_map/ppermute | solution.py:426
  158.1 30.8 %collective-permute-start.11 = (bf16[1024,768]{1,0:T(8,128)(2,1)}, bf16[1024,768]{1,0:T(8,128)(2,1)S(1)}, u32[]{:S(2)}, u32[]{:S(2)}) collective-permute-start(bf16[1024,768]{1,0:T(8,128)(2,1)} %get-tuple-element.76), channel_id=1, source_target_pairs={{0,8},{8,0},{16,24},{24,16},{1,9},{9,1},{17,25},{25,17},{2,10},{10... | collective-permute-start | bytes 4718600 | tf_op jit(solution)/shard_map/ppermute | solution.py:426
  158.8 50.8 %collective-permute-start.9 = (bf16[1024,768]{1,0:T(8,128)(2,1)}, bf16[1024,768]{1,0:T(8,128)(2,1)S(1)}, u32[]{:S(2)}, u32[]{:S(2)}) collective-permute-start(bf16[1024,768]{1,0:T(8,128)(2,1)} %get-tuple-element.73), channel_id=1, source_target_pairs={{0,8},{8,0},{16,24},{24,16},{1,9},{9,1},{17,25},{25,17},{2,10},{10... | collective-permute-start | bytes 4718600 | tf_op jit(solution)/shard_map/ppermute | solution.py:426
  159.3 32.5 %copy-start.6 = (bf16[512,768]{1,0:T(8,128)(2,1)S(1)}, bf16[512,768]{1,0:T(8,128)(2,1)}, u32[]{:S(2)}) copy-start(bf16[512,768]{1,0:T(8,128)(2,1)} %get-tuple-element.77) | copy-start | bytes 2359300
  162.9 44.7 %collective-permute-start.13 = (bf16[1024,768]{1,0:T(8,128)(2,1)}, bf16[1024,768]{1,0:T(8,128)(2,1)S(1)}, u32[]{:S(2)}, u32[]{:S(2)}) collective-permute-start(bf16[1024,768]{1,0:T(8,128)(2,1)} %get-tuple-element.79), channel_id=1, source_target_pairs={{0,8},{8,0},{16,24},{24,16},{1,9},{9,1},{17,25},{25,17},{2,10},{10... | collective-permute-start | bytes 4718600 | tf_op jit(solution)/shard_map/ppermute | solution.py:426
  184.5 14.4 %collective-permute-start.21 = (bf16[96,768]{1,0:T(8,128)(2,1)}, bf16[96,768]{1,0:T(8,128)(2,1)S(1)}, u32[]{:S(2)}, u32[]{:S(2)}) collective-permute-start(bf16[96,768]{1,0:T(8,128)(2,1)} %add_convert_fusion.3.refs_1_), channel_id=1, source_target_pairs={{0,2},{1,3},{2,0},{3,1},{4,6},{5,7},{6,4},{7,5},{8,10},{9,11},{10,... | collective-permute-start | bytes 442376 | tf_op jit(solution)/shard_map/ppermute | solution.py:426
  184.5 20.5 %collective-permute-start.22 = (bf16[96,768]{1,0:T(8,128)(2,1)}, bf16[96,768]{1,0:T(8,128)(2,1)S(1)}, u32[]{:S(2)}, u32[]{:S(2)}) collective-permute-start(bf16[96,768]{1,0:T(8,128)(2,1)} %add_convert_fusion.3.refs_1_), channel_id=1, source_target_pairs={{0,4},{1,5},{2,6},{3,7},{4,0},{5,1},{6,2},{7,3},{8,12},{9,13},{10,... | collective-permute-start | bytes 442376 | tf_op jit(solution)/shard_map/ppermute | solution.py:426
  188.9 18.6 %copy-start.1 = (bf16[1024,768]{1,0:T(8,128)(2,1)}, bf16[1024,768]{1,0:T(8,128)(2,1)S(1)}, u32[]{:S(2)}) copy-start(bf16[1024,768]{1,0:T(8,128)(2,1)S(1)} %collective-permute-done.11.refs_5_) | copy-start | bytes 4718596
  188.9 17.8 %collective-permute-start.23 = (bf16[96,768]{1,0:T(8,128)(2,1)}, bf16[96,768]{1,0:T(8,128)(2,1)S(1)}, u32[]{:S(2)}, u32[]{:S(2)}) collective-permute-start(bf16[96,768]{1,0:T(8,128)(2,1)} %add_convert_fusion.3.refs_1_), channel_id=1, source_target_pairs={{0,6},{1,7},{2,4},{3,5},{4,2},{5,3},{6,0},{7,1},{8,14},{9,15},{10,... | collective-permute-start | bytes 442376 | tf_op jit(solution)/shard_map/ppermute | solution.py:426
  191.8 15.9 %copy-start.7 = (bf16[512,768]{1,0:T(8,128)(2,1)S(1)}, bf16[512,768]{1,0:T(8,128)(2,1)}, u32[]{:S(2)}) copy-start(bf16[512,768]{1,0:T(8,128)(2,1)} %get-tuple-element.80) | copy-start | bytes 2359300
  192.9 16.7 %copy-start.8 = (bf16[512,768]{1,0:T(8,128)(2,1)S(1)}, bf16[512,768]{1,0:T(8,128)(2,1)}, u32[]{:S(2)}) copy-start(bf16[512,768]{1,0:T(8,128)(2,1)} %get-tuple-element.74) | copy-start | bytes 2359300
  198.9 10.1 %copy-start.9 = (bf16[96,768]{1,0:T(8,128)(2,1)}, bf16[96,768]{1,0:T(8,128)(2,1)S(1)}, u32[]{:S(2)}) copy-start(bf16[96,768]{1,0:T(8,128)(2,1)S(1)} %collective-permute-done.21.refs_2_) | copy-start | bytes 442372
  198.9 13.5 %collective-permute-start.19 = (f32[2,768]{1,0:T(2,128)S(1)}, f32[2,768]{1,0:T(2,128)S(1)}, u32[]{:S(2)}, u32[]{:S(2)}) collective-permute-start(f32[2,768]{1,0:T(2,128)S(1)} %slice_bitcast_fusion.3), channel_id=1, source_target_pairs={{0,8},{8,0},{16,24},{24,16},{1,9},{9,1},{17,25},{25,17},{2,10},{10... | collective-permute-start | bytes 18440 | tf_op jit(solution)/shard_map/ppermute | solution.py:426
  205.0 4.0 %copy-start.10 = (bf16[96,768]{1,0:T(8,128)(2,1)}, bf16[96,768]{1,0:T(8,128)(2,1)S(1)}, u32[]{:S(2)}) copy-start(bf16[96,768]{1,0:T(8,128)(2,1)S(1)} %collective-permute-done.22.refs_3_) | copy-start | bytes 442372
  205.0 57.0 %collective-permute-start.12 = (bf16[512,768]{1,0:T(8,128)(2,1)}, bf16[512,768]{1,0:T(8,128)(2,1)}, u32[]{:S(2)}, u32[]{:S(2)}) collective-permute-start(bf16[512,768]{1,0:T(8,128)(2,1)} %add_convert_fusion.1), channel_id=1, source_target_pairs={{0,16},{8,24},{16,0},{24,8},{1,17},{9,25},{17,1},{25,9},{2,18},{10... | collective-permute-start | bytes 2359304 | tf_op jit(solution)/shard_map/ppermute | solution.py:426
  206.7 2.3 copy-start.11
  207.5 50.8 %collective-permute-start.25 = (bf16[288,768]{1,0:T(8,128)(2,1)}, bf16[288,768]{1,0:T(8,128)(2,1)}, u32[]{:S(2)}, u32[]{:S(2)}) collective-permute-start(bf16[288,768]{1,0:T(8,128)(2,1)} %pad_maximum_fusion), channel_id=1, source_target_pairs={{0,1},{1,0},{2,3},{3,2},{4,5},{5,4},{6,7},{7,6},{8,9},{9,8},{10,11... | collective-permute-start | bytes 1327112 | tf_op jit(solution)/shard_map/ppermute | solution.py:426
  207.6 3.3 %copy-start.2 = (bf16[1024,768]{1,0:T(8,128)(2,1)}, bf16[1024,768]{1,0:T(8,128)(2,1)S(1)}, u32[]{:S(2)}) copy-start(bf16[1024,768]{1,0:T(8,128)(2,1)S(1)} %collective-permute-done.13.refs_8_) | copy-start | bytes 4718596
  209.0 46.0 %copy-start.13 = (f32[768]{0:T(1024)S(1)}, f32[768]{0:T(1024)}, u32[]{:S(2)}) copy-start(f32[768]{0:T(1024)} %refs_2_.5) | copy-start | bytes 9220
  209.0 53.0 %collective-permute-start.14 = (bf16[512,768]{1,0:T(8,128)(2,1)}, bf16[512,768]{1,0:T(8,128)(2,1)S(1)}, u32[]{:S(2)}, u32[]{:S(2)}) collective-permute-start(bf16[512,768]{1,0:T(8,128)(2,1)} %add_convert_fusion), channel_id=1, source_target_pairs={{0,16},{8,24},{16,0},{24,8},{1,17},{9,25},{17,1},{25,9},{2,18},{10... | collective-permute-start | bytes 2359304 | tf_op jit(solution)/shard_map/ppermute | solution.py:426
  209.6 52.4 %copy-start = (bf16[1024,768]{1,0:T(8,128)(2,1)}, bf16[1024,768]{1,0:T(8,128)(2,1)S(1)}, u32[]{:S(2)}) copy-start(bf16[1024,768]{1,0:T(8,128)(2,1)S(1)} %collective-permute-done.9.refs_5_) | copy-start | bytes 4718596
  210.9 78.4 %collective-permute-start.10 = (bf16[512,768]{1,0:T(8,128)(2,1)}, bf16[512,768]{1,0:T(8,128)(2,1)S(1)}, u32[]{:S(2)}, u32[]{:S(2)}) collective-permute-start(bf16[512,768]{1,0:T(8,128)(2,1)} %add_convert_fusion.2), channel_id=1, source_target_pairs={{0,16},{8,24},{16,0},{24,8},{1,17},{9,25},{17,1},{25,9},{2,18},{10... | collective-permute-start | bytes 2359304 | tf_op jit(solution)/shard_map/ppermute | solution.py:426
  212.5 40.5 %collective-permute-start.20 = (f32[2,768]{1,0:T(2,128)S(1)}, f32[2,768]{1,0:T(2,128)S(1)}, u32[]{:S(2)}, u32[]{:S(2)}) collective-permute-start(f32[2,768]{1,0:T(2,128)S(1)} %fusion), channel_id=1, source_target_pairs={{0,16},{8,24},{16,0},{24,8},{1,17},{9,25},{17,1},{25,9},{2,18},{10... | collective-permute-start | bytes 18440 | tf_op jit(solution)/shard_map/ppermute | solution.py:426
  252.9 5.4 %collective-permute-start.24 = (bf16[96,768]{1,0:T(8,128)(2,1)}, bf16[96,768]{1,0:T(8,128)(2,1)S(1)}, u32[]{:S(2)}, u32[]{:S(2)}) collective-permute-start(bf16[96,768]{1,0:T(8,128)(2,1)} %add_convert_fusion.3.refs_1_), channel_id=1, source_target_pairs={{0,1},{1,0},{2,3},{3,2},{4,5},{5,4},{6,7},{7,6},{8,9},{9,8},{10,11... | collective-permute-start | bytes 442376 | tf_op jit(solution)/shard_map/ppermute | solution.py:426
  (5 other events, 4.3 us)
Sparse Core Ops, SparseCore 0:
  159.4 125.6 all-reduce.1

commit v4 on v3

--- a/solution.py
+++ b/solution.py
@@ -82,7 +82,7 @@
         acc, accb = take(2)
     buf, w1, w2, b1, o_s, n_s, sem, weight_sem, prior_sem, o_sem, n_sem = take(11)
     if last:
-        acc, sum_s, sum_sem = take(3)
+        (acc,) = take(1)
     rows = packs[0].shape[0] // 2
     width = w1.shape[0]
     inv_sqrt2 = 2.0**-0.5
@@ -102,13 +102,13 @@
     for load in loads:
         load.start()
     held = [pltpu.make_async_copy(prior[j], to, prior_sem.at[j]) for j, to in enumerate((acc, accb))] if prior else []
-    for copy in held:
-        copy.start()
     if not prior:
         acc[...] = jnp.zeros(acc.shape, F32)
         accb[...] = jnp.zeros(accb.shape, F32)
     for load in loads:
         load.wait()
+    for copy in held:
+        copy.start()
 
     def step(k, carry):
         slot = k & 1
@@ -156,11 +156,8 @@
 
     lax.fori_loop(0, blocks, step, 0)
     if last:
-        sum_s[...] = acc[...].astype(BF16)
-        out = pltpu.make_async_copy(sum_s, summed, sum_sem)
-        out.start()
         accb[2:3] = as_row(jnp.sum(w1[...].astype(F32) * acc[0:width], axis=1, keepdims=True))
-        out.wait()
+        summed[...] = acc[...].astype(BF16)
     for k in range(blocks - 2, blocks):
         for write in writes(k, k & 1):
             write.wait()
@@ -472,16 +469,12 @@
         ]
         if last:
             outs += [((width + hidden, width), BF16), ((8, width), F32)]
-            scratch += [
-                pltpu.VMEM((width + hidden, width), F32),
-                pltpu.VMEM((width + hidden, width), BF16),
-                pltpu.SemaphoreType.DMA,
-            ]
+            scratch += [pltpu.VMEM((width + hidden, width), F32)]
         else:
             outs += [((width + hidden, width), F32), ((8, width), F32)]
         res = call(
             functools.partial(ff_kernel, first, last, count, first), outs, 0,
-            *packs, w_fc1, w_fc2, b1, *state, n_any=count + 3 + len(state), any_outs=3 if last else 2,
+            *packs, w_fc1, w_fc2, b1, *state, n_any=count + 3 + len(state), any_outs=2,
             scratch=scratch, flops=12 * count * rows * width * hidden,
         )
         return res[0], res[1], res[2:]

time: 301 us -> 299 us (level)
    psum x1, waiting for transfers between devices: 16.9 us -> 12 us  [block(): fc = lax.psum(ff_out, 'dp')]
    ppermute x26, waiting for transfers between devices: 104 us -> 109 us  [swap(): return lax.ppermute(v, axis, [(i, i ^ mask) for i in range(count)])]
where the time goes in v4:
time: 299 us
  waiting for transfers between devices  121 us (40%)
  Pallas kernels  116 us (39%)
  starting transfers between devices  21.1 us (7%)
  between operations  14.3 us (5%)
  other arithmetic  14.1 us (5%)
  local copies, waits for them, and re-layouts  12.3 us (4%)
    ppermute x26, waiting for transfers between devices, swap(): return lax.ppermute(v, axis, [(i, i ^ mask) for i in range(count)])  109 us
    pallas_call x8, Pallas kernels, call(): pl.pallas_call(kernel, out_shape=[jax.ShapeDtypeStruct(s, d) for s, d in...  107 us
    ppermute x26, starting transfers between devices, swap(): return lax.ppermute(v, axis, [(i, i ^ mask) for i in range(count)])  21.1 us
    psum x1, waiting for transfers between devices, block(): fc = lax.psum(ff_out, 'dp')  12 us
    pallas_call x2, Pallas kernels, finish(): pl.pallas_call(functools.partial(final_kernel, end - begin), grid=(end -...  8.81 us
  transfers between devices with their start and end apart: 27, of which 12 were waited for; matrix products, arithmetic and copies ran while one was open for 6% of the time, Pallas kernels for 17%

profile of v4, /device:TPU:0, one launch (start us, length us, event | category | flops | bytes accessed | tf_op | source)
XLA Modules:
  0.0 298.6 jit_solution(92289114090192571)
XLA Ops:
  7.2 4.0 %shard_map.203 = (bf16[512,768]{1,0:T(8,128)(2,1)}, bf16[512,768]{1,0:T(8,128)(2,1)}, bf16[512,768]{1,0:T(8,128)(2,1)}) custom-call(bf16[3,256,768]{2,1,0:T(8,128)(2,1)} %refs_0_.3, bf16[3,256,768]{2,1,0:T(8,128)(2,1)} %refs_1_.3, f32[768]{0:T(1024)} %refs_2_.5), custom_call_target="tpu_custom_call" | custom-call | bytes 4721664 | tf_op jit(solution)/shard_map/pallas_call | solution.py:31
  12.3 2.6 collective-permute-start.3
  15.1 1.0 collective-permute-done.4.refs_3_.refs_4_
  16.1 0.9 copy-done.21
  17.0 17.8 %shard_map.204 = (bf16[1536,768]{1,0:T(8,128)(2,1)}, bf16[1536,768]{1,0:T(8,128)(2,1)}, f32[1536,768]{1,0:T(8,128)}, f32[8,768]{1,0:T(8,128)}) custom-call(bf16[512,768]{1,0:T(8,128)(2,1)} %get-tuple-element.52.refs_0_.refs_3_, bf16[512,768]{1,0:T(8,128)(2,1)} %collective-permute-done.2.refs_1_.refs_4_, bf16[512,768]{1,0:T(8,128)(2,1)} %get-tuple-element.53.refs_2_.refs_3_, ...), custom_call_target="tpu_custom_call" | custom-call | flops 10871635968 | bytes 16542720 | tf_op jit(solution)/shard_map/pallas_call | solution.py:31
  35.3 2.6 collective-permute-start.1
  38.0 0.8 reshape.36.refs_13_.refs_14_
  38.8 0.8 reshape.37.refs_14_.refs_15_
  40.1 9.5 %shard_map.205 = (bf16[512,768]{1,0:T(8,128)(2,1)}, bf16[512,768]{1,0:T(8,128)(2,1)}, f32[1536,768]{1,0:T(8,128)}, f32[8,768]{1,0:T(8,128)}) custom-call(bf16[512,768]{1,0:T(8,128)(2,1)} %collective-permute-done.3.refs_0_.refs_5_, bf16[512,768]{1,0:T(8,128)(2,1)} %collective-permute-done.5.refs_1_.refs_6_, bf16[768,768]{1,0:T(8,128)(2,1)} %refs_4_.3, ...), custom_call_target="tpu_custom_call" | custom-call | flops 3623878656 | bytes 14994432 | tf_op jit(solution)/shard_map/pallas_call | solution.py:31
  49.7 15.7 %shard_map.206 = (bf16[512,768]{1,0:T(8,128)(2,1)}, bf16[512,768]{1,0:T(8,128)(2,1)}, bf16[1024,768]{1,0:T(8,128)(2,1)}, f32[768,768]{1,0:T(8,128)}, f32[384,1]{1,0:T(8,128)}) custom-call(s32[1]{0:T(128)} %get-tuple-element.105.refs_0_, s32[1]{0:T(128)} %bitcast.refs_1_, s32[1]{0:T(128)} %bitcast.1.refs_2_, ...), custom_call_target="tpu_custom_call" | custom-call | flops 14495514624 | bytes 16124940 | tf_op jit(solution)/shard_map/pallas_call | solution.py:31
  65.6 7.3 %collective-permute-done.7.refs_0_.refs_5_ = bf16[512,768]{1,0:T(8,128)(2,1)S(1)} collective-permute-done((bf16[512,768]{1,0:T(8,128)(2,1)S(1)}, bf16[512,768]{1,0:T(8,128)(2,1)S(1)}, u32[]{:S(2)}, u32[]{:S(2)}) %collective-permute-start.7) | collective-permute-done | bytes 786464 | tf_op jit(solution)/shard_map/ppermute | solution.py:423
  72.9 2.3 collective-permute-done.8.refs_1_.refs_6_
  75.2 0.9 copy-done.25
  76.0 13.7 %shard_map.207 = (bf16[1024,768]{1,0:T(8,128)(2,1)}, bf16[1024,768]{1,0:T(8,128)(2,1)}, bf16[1536,768]{1,0:T(8,128)(2,1)}, f32[8,768]{1,0:T(8,128)}) custom-call(bf16[512,768]{1,0:T(8,128)(2,1)} %copy-done.23, bf16[512,768]{1,0:T(8,128)(2,1)} %copy-done.25, bf16[512,768]{1,0:T(8,128)(2,1)} %copy-done.22, bf16[512,768]{1,0:T(8,128)(2,1)} %copy-done.24, ...), custom_call_target="tpu_custom_call" | custom-call | flops 7247757312 | bytes 15780864 | tf_op jit(solution)/shard_map/pallas_call | solution.py:31
  89.7 20.6 %shard_map.208 = (bf16[512,768]{1,0:T(8,128)(2,1)}, bf16[512,768]{1,0:T(8,128)(2,1)}, bf16[1024,768]{1,0:T(8,128)(2,1)}, f32[768,768]{1,0:T(8,128)}, f32[384,1]{1,0:T(8,128)}) custom-call(s32[1]{0:T(128)} %get-tuple-element.103.refs_0_, s32[1]{0:T(128)} %bitcast.refs_1_, s32[1]{0:T(128)} %bitcast.1.refs_2_, ...), custom_call_target="tpu_custom_call" | custom-call | flops 14495514624 | bytes 20058636 | tf_op jit(solution)/shard_map/pallas_call | solution.py:31
  110.3 23.1 %shard_map.209 = (bf16[512,768]{1,0:T(8,128)(2,1)}, bf16[512,768]{1,0:T(8,128)(2,1)}, bf16[1024,768]{1,0:T(8,128)(2,1)}, f32[384,768]{1,0:T(8,128)}, bf16[392,768]{1,0:T(8,128)(2,1)}, /*index=5*/bf16[8,768]{1,0:T(8,128)(2,1)}) custom-call(s32[1]{0:T(128)} %get-tuple-element.104.refs_0_, s32[1]{0:T(128)} %bitcast.refs_1_, s32[1]{0:T(128)} %bitcast.1.refs_2_, ...), custom_call_target="tpu_custom_call" | custom-call | flops 14495514624 | bytes 19516428 | tf_op jit(solution)/shard_map/pallas_call | solution.py:31
  133.6 15.8 %collective-permute-done.15 = bf16[392,768]{1,0:T(8,128)(2,1)S(1)} collective-permute-done((bf16[392,768]{1,0:T(8,128)(2,1)}, bf16[392,768]{1,0:T(8,128)(2,1)S(1)}, u32[]{:S(2)}, u32[]{:S(2)}) %collective-permute-start.15) | collective-permute-done | bytes 602144 | tf_op jit(solution)/shard_map/ppermute | solution.py:423
  149.4 1.4 convert_add_fusion
  150.8 1.0 copy-done.3
  151.9 0.7 pad_maximum_fusion.3
  152.9 1.6 collective-permute-start.17
  154.5 2.5 collective-permute-start.16
  157.0 0.7 pad_add_fusion.refs_0_
  158.2 3.6 %collective-permute-done.18 = bf16[104,768]{1,0:T(8,128)(2,1)} collective-permute-done((bf16[104,768]{1,0:T(8,128)(2,1)}, bf16[104,768]{1,0:T(8,128)(2,1)}, u32[]{:S(2)}, u32[]{:S(2)}) %collective-permute-start.18) | collective-permute-done | bytes 159776 | tf_op jit(solution)/shard_map/ppermute | solution.py:423
  161.8 19.2 %collective-permute-done.17 = bf16[104,768]{1,0:T(8,128)(2,1)} collective-permute-done((bf16[104,768]{1,0:T(8,128)(2,1)S(1)}, bf16[104,768]{1,0:T(8,128)(2,1)}, u32[]{:S(2)}, u32[]{:S(2)}) %collective-permute-start.17) | collective-permute-done | bytes 159776 | tf_op jit(solution)/shard_map/ppermute | solution.py:423
  181.0 1.9 add_convert_fusion.3.refs_1_
  182.9 2.3 collective-permute-start.22
  185.1 0.7 slice_bitcast_fusion
  185.8 0.7 slice_bitcast_fusion.1
  186.5 0.7 slice_bitcast_fusion.2
  187.9 2.2 collective-permute-start.23
  190.1 1.1 add_convert_fusion.1
  191.2 6.5 %collective-permute-done.21.refs_2_ = bf16[96,768]{1,0:T(8,128)(2,1)S(1)} collective-permute-done((bf16[96,768]{1,0:T(8,128)(2,1)}, bf16[96,768]{1,0:T(8,128)(2,1)S(1)}, u32[]{:S(2)}, u32[]{:S(2)}) %collective-permute-start.21) | collective-permute-done | bytes 147488 | tf_op jit(solution)/shard_map/ppermute | solution.py:423
  197.7 5.8 %collective-permute-done.22.refs_3_ = bf16[96,768]{1,0:T(8,128)(2,1)S(1)} collective-permute-done((bf16[96,768]{1,0:T(8,128)(2,1)}, bf16[96,768]{1,0:T(8,128)(2,1)S(1)}, u32[]{:S(2)}, u32[]{:S(2)}) %collective-permute-start.22) | collective-permute-done | bytes 147488 | tf_op jit(solution)/shard_map/ppermute | solution.py:423
  203.5 1.3 collective-permute-start.12
  204.9 0.8 pad_maximum_fusion
  206.2 1.3 add_convert_fusion
  208.2 1.4 add_convert_fusion.2
  209.6 1.5 collective-permute-start.10
  211.7 41.2 %collective-permute-done.20 = f32[2,768]{1,0:T(2,128)S(1)} collective-permute-done((f32[2,768]{1,0:T(2,128)S(1)}, f32[2,768]{1,0:T(2,128)S(1)}, u32[]{:S(2)}, u32[]{:S(2)}) %collective-permute-start.20) | collective-permute-done | bytes 6176 | tf_op jit(solution)/shard_map/ppermute | solution.py:423
  255.6 5.7 %collective-permute-done.24.refs_5_ = bf16[96,768]{1,0:T(8,128)(2,1)S(1)} collective-permute-done((bf16[96,768]{1,0:T(8,128)(2,1)}, bf16[96,768]{1,0:T(8,128)(2,1)S(1)}, u32[]{:S(2)}, u32[]{:S(2)}) %collective-permute-start.24) | collective-permute-done | bytes 147488 | tf_op jit(solution)/shard_map/ppermute | solution.py:423
  261.9 3.0 %shard_map.212 = (f32[576,768]{1,0:T(8,128)}, f32[192,768]{1,0:T(8,128)}) custom-call(s32[2]{0:T(128)} %pad_add_fusion.refs_0_, bf16[96,768]{1,0:T(8,128)(2,1)} %add_convert_fusion.3.refs_1_, bf16[96,768]{1,0:T(8,128)(2,1)} %copy-done.9, bf16[96,768]{1,0:T(8,128)(2,1)} %copy-done.10, bf16[96,768]{1,0:T(8,128)(2,1)} %copy-done.11, ...), custom_call_target="tpu_custom_call" | custom-call | bytes 3538952 | tf_op jit(solution)/shard_map/pallas_call | solution.py:31
  265.0 1.0 copy-done.5
  265.9 5.3 %shard_map.210 = (bf16[3,256,768]{2,1,0:T(8,128)(2,1)}, f32[3,256,768]{2,1,0:T(8,128)}) custom-call(bf16[3,256,768]{2,1,0:T(8,128)(2,1)} %refs_0_.3, bf16[3,256,768]{2,1,0:T(8,128)(2,1)} %refs_1_.3, f32[768]{0:T(1024)} %refs_2_.5, f32[768]{0:T(1024)} %refs_3_.5, bf16[512,768]{1,0:T(8,128)(2,1)} %get-tuple-element.75.refs_4_, bf16[1024,768]{1,0:T(8,128)(2,1)} %copy-done.1, ...), custom_call_target="tpu_custom_call" | custom-call | tf_op jit(solution)/shard_map/pallas_call | solution.py:604
  271.2 12.0 %all-reduce.2.cloned.1.call-done = bf16[1536,768]{1,0:T(8,128)(2,1)} async-done(((bf16[1536,768]{1,0:T(8,128)(2,1)}), bf16[1536,768]{1,0:T(8,128)(2,1)}) %all-reduce.2.cloned.1.call-update) | async-done | bytes 2359312 | tf_op jit(solution)/shard_map/psum | solution.py:580
  283.2 4.2 %slice_convert_fusion = (f32[768,768]{1,0:T(8,128)}, f32[768,768]{1,0:T(8,128)}) fusion(bf16[1536,768]{1,0:T(8,128)(2,1)} %all-reduce.2.cloned.1.call-done), kind=kLoop, calls=%fused_computation.3 | loop fusion | flops 1179648 | bytes 7077888 | tf_op jit(solution)/shard_map/convert_element_type | solution.py:595
  287.4 0.9 copy-done.4
  288.2 3.5 %shard_map.211 = (bf16[3,256,768]{2,1,0:T(8,128)(2,1)}, f32[3,256,768]{2,1,0:T(8,128)}) custom-call(bf16[3,256,768]{2,1,0:T(8,128)(2,1)} %refs_0_.3, bf16[3,256,768]{2,1,0:T(8,128)(2,1)} %refs_1_.3, f32[768]{0:T(1024)} %refs_2_.5, f32[768]{0:T(1024)} %refs_3_.5, ...), custom_call_target="tpu_custom_call", output_to_operand_aliasing={{0}: (7, {}), {1}: (8, {})} | custom-call | tf_op jit(solution)/shard_map/pallas_call | solution.py:604
  (98 shorter events, 9.5 us)
Async XLA Ops:
  7.2 276.0 %all-reduce.2.cloned.1.call-start = ((), (), s32[]{:S(2)}) async-start(), calls=%async_computation | async-start | bytes 4718592 | tf_op jit(solution)/shard_map/psum | solution.py:580
  11.2 3.7 %collective-permute-start = (bf16[512,768]{1,0:T(8,128)(2,1)}, bf16[512,768]{1,0:T(8,128)(2,1)S(1)}, u32[]{:S(2)}, u32[]{:S(2)}) collective-permute-start(bf16[512,768]{1,0:T(8,128)(2,1)} %get-tuple-element.51.refs_4_.refs_3_), channel_id=1, source_target_pairs={{0,8},{8,0},{16,24},{24,16},{1,9},{9,1},{17,25},{25,17},{2,10},{10... | collective-permute-start | bytes 2359304 | tf_op jit(solution)/shard_map/ppermute | solution.py:423
  11.7 3.4 %collective-permute-start.2 = (bf16[512,768]{1,0:T(8,128)(2,1)}, bf16[512,768]{1,0:T(8,128)(2,1)}, u32[]{:S(2)}, u32[]{:S(2)}) collective-permute-start(bf16[512,768]{1,0:T(8,128)(2,1)} %get-tuple-element.52.refs_0_.refs_3_), channel_id=1, source_target_pairs={{0,8},{8,0},{16,24},{24,16},{1,9},{9,1},{17,25},{25,17},{2,10},{10... | collective-permute-start | bytes 2359304 | tf_op jit(solution)/shard_map/ppermute | solution.py:423
  11.8 23.5 %copy-start.18 = (bf16[512,768]{1,0:T(8,128)(2,1)S(1)}, bf16[512,768]{1,0:T(8,128)(2,1)}, u32[]{:S(2)}) copy-start(bf16[512,768]{1,0:T(8,128)(2,1)} %get-tuple-element.51.refs_4_.refs_3_) | copy-start | bytes 2359300
  11.8 26.1 %copy-start.20 = (bf16[512,768]{1,0:T(8,128)(2,1)S(1)}, bf16[512,768]{1,0:T(8,128)(2,1)}, u32[]{:S(2)}) copy-start(bf16[512,768]{1,0:T(8,128)(2,1)} %get-tuple-element.53.refs_2_.refs_3_) | copy-start | bytes 2359300
  11.8 26.2 %copy-start.16 = (f32[3,64]{1,0:T(4,128)S(1)}, f32[3,64]{1,0:T(4,128)}, u32[]{:S(2)}) copy-start(f32[3,64]{1,0:T(4,128)} %param.16) | copy-start | bytes 2308
  11.8 26.9 %copy-start.17 = (f32[3,64]{1,0:T(4,128)S(1)}, f32[3,64]{1,0:T(4,128)}, u32[]{:S(2)}) copy-start(f32[3,64]{1,0:T(4,128)} %param.17) | copy-start | bytes 2308
  11.8 27.7 %copy-start.15 = (s32[3]{0:T(128)S(1)}, s32[3]{0:T(128)}, u32[]{:S(2)}) copy-start(s32[3]{0:T(128)} %param.13) | copy-start | bytes 40
  11.8 4.3 %collective-permute-start.4 = (bf16[512,768]{1,0:T(8,128)(2,1)}, bf16[512,768]{1,0:T(8,128)(2,1)S(1)}, u32[]{:S(2)}, u32[]{:S(2)}) collective-permute-start(bf16[512,768]{1,0:T(8,128)(2,1)} %get-tuple-element.53.refs_2_.refs_3_), channel_id=1, source_target_pairs={{0,8},{8,0},{16,24},{24,16},{1,9},{9,1},{17,25},{25,17},{2,10},{10... | collective-permute-start | bytes 2359304 | tf_op jit(solution)/shard_map/ppermute | solution.py:423
  12.3 22.5 %collective-permute-start.3 = (bf16[512,768]{1,0:T(8,128)(2,1)}, bf16[512,768]{1,0:T(8,128)(2,1)}, u32[]{:S(2)}, u32[]{:S(2)}) collective-permute-start(bf16[512,768]{1,0:T(8,128)(2,1)} %get-tuple-element.52.refs_0_.refs_3_), channel_id=1, source_target_pairs={{0,16},{8,24},{16,0},{24,8},{1,17},{9,25},{17,1},{25,9},{2,18},{10... | collective-permute-start | bytes 2359304 | tf_op jit(solution)/shard_map/ppermute | solution.py:423
  14.9 1.2 copy-start.19
  34.8 5.3 %collective-permute-start.5 = (bf16[512,768]{1,0:T(8,128)(2,1)}, bf16[512,768]{1,0:T(8,128)(2,1)}, u32[]{:S(2)}, u32[]{:S(2)}) collective-permute-start(bf16[512,768]{1,0:T(8,128)(2,1)} %collective-permute-done.3.refs_0_.refs_5_), channel_id=1, source_target_pairs={{0,8},{8,0},{16,24},{24,16},{1,9},{9,1},{17,25},{25,17},{2,10},{10... | collective-permute-start | bytes 2359304 | tf_op jit(solution)/shard_map/ppermute | solution.py:423
  35.3 30.1 %collective-permute-start.1 = (bf16[512,768]{1,0:T(8,128)(2,1)S(1)}, bf16[512,768]{1,0:T(8,128)(2,1)S(1)}, u32[]{:S(2)}, u32[]{:S(2)}) collective-permute-start(bf16[512,768]{1,0:T(8,128)(2,1)S(1)} %copy-done.18), channel_id=1, source_target_pairs={{0,16},{8,24},{16,0},{24,8},{1,17},{9,25},{17,1},{25,9},{2,18},{10... | collective-permute-start | bytes 2359304 | tf_op jit(solution)/shard_map/ppermute | solution.py:423
  37.9 34.9 %collective-permute-start.7 = (bf16[512,768]{1,0:T(8,128)(2,1)S(1)}, bf16[512,768]{1,0:T(8,128)(2,1)S(1)}, u32[]{:S(2)}, u32[]{:S(2)}) collective-permute-start(bf16[512,768]{1,0:T(8,128)(2,1)S(1)} %copy-done.20), channel_id=1, source_target_pairs={{0,16},{8,24},{16,0},{24,8},{1,17},{9,25},{17,1},{25,9},{2,18},{10... | collective-permute-start | bytes 2359304 | tf_op jit(solution)/shard_map/ppermute | solution.py:423
  65.4 9.8 %copy-start.22 = (bf16[512,768]{1,0:T(8,128)(2,1)}, bf16[512,768]{1,0:T(8,128)(2,1)S(1)}, u32[]{:S(2)}) copy-start(bf16[512,768]{1,0:T(8,128)(2,1)S(1)} %collective-permute-done.1.refs_2_.refs_5_) | copy-start | bytes 2359300
  65.4 7.5 %collective-permute-start.6 = (bf16[512,768]{1,0:T(8,128)(2,1)S(1)}, bf16[512,768]{1,0:T(8,128)(2,1)S(1)}, u32[]{:S(2)}, u32[]{:S(2)}) collective-permute-start(bf16[512,768]{1,0:T(8,128)(2,1)S(1)} %collective-permute-done.1.refs_2_.refs_5_), channel_id=1, source_target_pairs={{0,8},{8,0},{16,24},{24,16},{1,9},{9,1},{17,25},{25,17},{2,10},{10... | collective-permute-start | bytes 2359304 | tf_op jit(solution)/shard_map/ppermute | solution.py:423
  72.9 2.3 copy-start.23
  72.9 2.3 collective-permute-start.8
  72.9 2.3 copy-start.24
  133.5 15.9 %collective-permute-start.15 = (bf16[392,768]{1,0:T(8,128)(2,1)}, bf16[392,768]{1,0:T(8,128)(2,1)S(1)}, u32[]{:S(2)}, u32[]{:S(2)}) collective-permute-start(bf16[392,768]{1,0:T(8,128)(2,1)} %get-tuple-element.86), channel_id=1, source_target_pairs={{0,1},{1,0},{2,3},{3,2},{4,5},{5,4},{6,7},{7,6},{8,9},{9,8},{10,11... | collective-permute-start | bytes 1806344 | tf_op jit(solution)/shard_map/ppermute | solution.py:423
  149.4 2.5 copy-start.14
  150.8 1.0 copy-start.3
  152.6 9.2 %collective-permute-start.18 = (bf16[104,768]{1,0:T(8,128)(2,1)}, bf16[104,768]{1,0:T(8,128)(2,1)}, u32[]{:S(2)}, u32[]{:S(2)}) collective-permute-start(bf16[104,768]{1,0:T(8,128)(2,1)} %get-tuple-element.102), channel_id=1, source_target_pairs={{0,6},{1,7},{2,4},{3,5},{4,2},{5,3},{6,0},{7,1},{8,14},{9,15},{10,... | collective-permute-start | bytes 479240 | tf_op jit(solution)/shard_map/ppermute | solution.py:423
  152.9 28.1 %collective-permute-start.17 = (bf16[104,768]{1,0:T(8,128)(2,1)S(1)}, bf16[104,768]{1,0:T(8,128)(2,1)}, u32[]{:S(2)}, u32[]{:S(2)}) collective-permute-start(bf16[104,768]{1,0:T(8,128)(2,1)S(1)} %get-tuple-element.101), channel_id=1, source_target_pairs={{0,4},{1,5},{2,6},{3,7},{4,0},{5,1},{6,2},{7,3},{8,12},{9,13},{10,... | collective-permute-start | bytes 479240 | tf_op jit(solution)/shard_map/ppermute | solution.py:423
  154.5 26.5 %collective-permute-start.16 = (bf16[104,768]{1,0:T(8,128)(2,1)S(1)}, bf16[104,768]{1,0:T(8,128)(2,1)}, u32[]{:S(2)}, u32[]{:S(2)}) collective-permute-start(bf16[104,768]{1,0:T(8,128)(2,1)S(1)} %get-tuple-element.100), channel_id=1, source_target_pairs={{0,2},{1,3},{2,0},{3,1},{4,6},{5,7},{6,4},{7,5},{8,10},{9,11},{10,... | collective-permute-start | bytes 479240 | tf_op jit(solution)/shard_map/ppermute | solution.py:423
  156.9 31.0 %collective-permute-start.11 = (bf16[1024,768]{1,0:T(8,128)(2,1)}, bf16[1024,768]{1,0:T(8,128)(2,1)S(1)}, u32[]{:S(2)}, u32[]{:S(2)}) collective-permute-start(bf16[1024,768]{1,0:T(8,128)(2,1)} %get-tuple-element.76), channel_id=1, source_target_pairs={{0,8},{8,0},{16,24},{24,16},{1,9},{9,1},{17,25},{25,17},{2,10},{10... | collective-permute-start | bytes 4718600 | tf_op jit(solution)/shard_map/ppermute | solution.py:423
  157.6 50.6 %collective-permute-start.9 = (bf16[1024,768]{1,0:T(8,128)(2,1)}, bf16[1024,768]{1,0:T(8,128)(2,1)S(1)}, u32[]{:S(2)}, u32[]{:S(2)}) collective-permute-start(bf16[1024,768]{1,0:T(8,128)(2,1)} %get-tuple-element.73), channel_id=1, source_target_pairs={{0,8},{8,0},{16,24},{24,16},{1,9},{9,1},{17,25},{25,17},{2,10},{10... | collective-permute-start | bytes 4718600 | tf_op jit(solution)/shard_map/ppermute | solution.py:423
  158.1 32.0 %copy-start.6 = (bf16[512,768]{1,0:T(8,128)(2,1)S(1)}, bf16[512,768]{1,0:T(8,128)(2,1)}, u32[]{:S(2)}) copy-start(bf16[512,768]{1,0:T(8,128)(2,1)} %get-tuple-element.77) | copy-start | bytes 2359300
  161.8 44.5 %collective-permute-start.13 = (bf16[1024,768]{1,0:T(8,128)(2,1)}, bf16[1024,768]{1,0:T(8,128)(2,1)S(1)}, u32[]{:S(2)}, u32[]{:S(2)}) collective-permute-start(bf16[1024,768]{1,0:T(8,128)(2,1)} %get-tuple-element.79), channel_id=1, source_target_pairs={{0,8},{8,0},{16,24},{24,16},{1,9},{9,1},{17,25},{25,17},{2,10},{10... | collective-permute-start | bytes 4718600 | tf_op jit(solution)/shard_map/ppermute | solution.py:423
  182.9 14.8 %collective-permute-start.21 = (bf16[96,768]{1,0:T(8,128)(2,1)}, bf16[96,768]{1,0:T(8,128)(2,1)S(1)}, u32[]{:S(2)}, u32[]{:S(2)}) collective-permute-start(bf16[96,768]{1,0:T(8,128)(2,1)} %add_convert_fusion.3.refs_1_), channel_id=1, source_target_pairs={{0,2},{1,3},{2,0},{3,1},{4,6},{5,7},{6,4},{7,5},{8,10},{9,11},{10,... | collective-permute-start | bytes 442376 | tf_op jit(solution)/shard_map/ppermute | solution.py:423
  182.9 20.7 %collective-permute-start.22 = (bf16[96,768]{1,0:T(8,128)(2,1)}, bf16[96,768]{1,0:T(8,128)(2,1)S(1)}, u32[]{:S(2)}, u32[]{:S(2)}) collective-permute-start(bf16[96,768]{1,0:T(8,128)(2,1)} %add_convert_fusion.3.refs_1_), channel_id=1, source_target_pairs={{0,4},{1,5},{2,6},{3,7},{4,0},{5,1},{6,2},{7,3},{8,12},{9,13},{10,... | collective-permute-start | bytes 442376 | tf_op jit(solution)/shard_map/ppermute | solution.py:423
  187.9 17.8 %copy-start.1 = (bf16[1024,768]{1,0:T(8,128)(2,1)}, bf16[1024,768]{1,0:T(8,128)(2,1)S(1)}, u32[]{:S(2)}) copy-start(bf16[1024,768]{1,0:T(8,128)(2,1)S(1)} %collective-permute-done.11.refs_5_) | copy-start | bytes 4718596
  187.9 16.9 %collective-permute-start.23 = (bf16[96,768]{1,0:T(8,128)(2,1)}, bf16[96,768]{1,0:T(8,128)(2,1)S(1)}, u32[]{:S(2)}, u32[]{:S(2)}) collective-permute-start(bf16[96,768]{1,0:T(8,128)(2,1)} %add_convert_fusion.3.refs_1_), channel_id=1, source_target_pairs={{0,6},{1,7},{2,4},{3,5},{4,2},{5,3},{6,0},{7,1},{8,14},{9,15},{10,... | collective-permute-start | bytes 442376 | tf_op jit(solution)/shard_map/ppermute | solution.py:423
  190.1 16.1 %copy-start.7 = (bf16[512,768]{1,0:T(8,128)(2,1)S(1)}, bf16[512,768]{1,0:T(8,128)(2,1)}, u32[]{:S(2)}) copy-start(bf16[512,768]{1,0:T(8,128)(2,1)} %get-tuple-element.80) | copy-start | bytes 2359300
  191.2 17.0 %copy-start.8 = (bf16[512,768]{1,0:T(8,128)(2,1)S(1)}, bf16[512,768]{1,0:T(8,128)(2,1)}, u32[]{:S(2)}) copy-start(bf16[512,768]{1,0:T(8,128)(2,1)} %get-tuple-element.74) | copy-start | bytes 2359300
  197.7 9.9 %copy-start.9 = (bf16[96,768]{1,0:T(8,128)(2,1)}, bf16[96,768]{1,0:T(8,128)(2,1)S(1)}, u32[]{:S(2)}) copy-start(bf16[96,768]{1,0:T(8,128)(2,1)S(1)} %collective-permute-done.21.refs_2_) | copy-start | bytes 442372
  197.7 13.4 %collective-permute-start.19 = (f32[2,768]{1,0:T(2,128)S(1)}, f32[2,768]{1,0:T(2,128)S(1)}, u32[]{:S(2)}, u32[]{:S(2)}) collective-permute-start(f32[2,768]{1,0:T(2,128)S(1)} %slice_bitcast_fusion.3), channel_id=1, source_target_pairs={{0,8},{8,0},{16,24},{24,16},{1,9},{9,1},{17,25},{25,17},{2,10},{10... | collective-permute-start | bytes 18440 | tf_op jit(solution)/shard_map/ppermute | solution.py:423
  203.5 4.0 %copy-start.10 = (bf16[96,768]{1,0:T(8,128)(2,1)}, bf16[96,768]{1,0:T(8,128)(2,1)S(1)}, u32[]{:S(2)}) copy-start(bf16[96,768]{1,0:T(8,128)(2,1)S(1)} %collective-permute-done.22.refs_3_) | copy-start | bytes 442372
  203.5 61.4 %collective-permute-start.12 = (bf16[512,768]{1,0:T(8,128)(2,1)}, bf16[512,768]{1,0:T(8,128)(2,1)}, u32[]{:S(2)}, u32[]{:S(2)}) collective-permute-start(bf16[512,768]{1,0:T(8,128)(2,1)} %add_convert_fusion.1), channel_id=1, source_target_pairs={{0,16},{8,24},{16,0},{24,8},{1,17},{9,25},{17,1},{25,9},{2,18},{10... | collective-permute-start | bytes 2359304 | tf_op jit(solution)/shard_map/ppermute | solution.py:423
  204.9 2.7 copy-start.11
  205.7 55.6 %collective-permute-start.25 = (bf16[288,768]{1,0:T(8,128)(2,1)}, bf16[288,768]{1,0:T(8,128)(2,1)}, u32[]{:S(2)}, u32[]{:S(2)}) collective-permute-start(bf16[288,768]{1,0:T(8,128)(2,1)} %pad_maximum_fusion), channel_id=1, source_target_pairs={{0,1},{1,0},{2,3},{3,2},{4,5},{5,4},{6,7},{7,6},{8,9},{9,8},{10,11... | collective-permute-start | bytes 1327112 | tf_op jit(solution)/shard_map/ppermute | solution.py:423
  206.2 3.4 %copy-start.2 = (bf16[1024,768]{1,0:T(8,128)(2,1)}, bf16[1024,768]{1,0:T(8,128)(2,1)S(1)}, u32[]{:S(2)}) copy-start(bf16[1024,768]{1,0:T(8,128)(2,1)S(1)} %collective-permute-done.13.refs_8_) | copy-start | bytes 4718596
  207.6 47.4 %copy-start.13 = (f32[768]{0:T(1024)S(1)}, f32[768]{0:T(1024)}, u32[]{:S(2)}) copy-start(f32[768]{0:T(1024)} %refs_2_.5) | copy-start | bytes 9220
  207.6 57.4 %collective-permute-start.14 = (bf16[512,768]{1,0:T(8,128)(2,1)}, bf16[512,768]{1,0:T(8,128)(2,1)S(1)}, u32[]{:S(2)}, u32[]{:S(2)}) collective-permute-start(bf16[512,768]{1,0:T(8,128)(2,1)} %add_convert_fusion), channel_id=1, source_target_pairs={{0,16},{8,24},{16,0},{24,8},{1,17},{9,25},{17,1},{25,9},{2,18},{10... | collective-permute-start | bytes 2359304 | tf_op jit(solution)/shard_map/ppermute | solution.py:423
  208.2 56.7 %copy-start = (bf16[1024,768]{1,0:T(8,128)(2,1)}, bf16[1024,768]{1,0:T(8,128)(2,1)S(1)}, u32[]{:S(2)}) copy-start(bf16[1024,768]{1,0:T(8,128)(2,1)S(1)} %collective-permute-done.9.refs_5_) | copy-start | bytes 4718596
  209.6 77.8 %collective-permute-start.10 = (bf16[512,768]{1,0:T(8,128)(2,1)}, bf16[512,768]{1,0:T(8,128)(2,1)S(1)}, u32[]{:S(2)}, u32[]{:S(2)}) collective-permute-start(bf16[512,768]{1,0:T(8,128)(2,1)} %add_convert_fusion.2), channel_id=1, source_target_pairs={{0,16},{8,24},{16,0},{24,8},{1,17},{9,25},{17,1},{25,9},{2,18},{10... | collective-permute-start | bytes 2359304 | tf_op jit(solution)/shard_map/ppermute | solution.py:423
  211.1 41.9 %collective-permute-start.20 = (f32[2,768]{1,0:T(2,128)S(1)}, f32[2,768]{1,0:T(2,128)S(1)}, u32[]{:S(2)}, u32[]{:S(2)}) collective-permute-start(f32[2,768]{1,0:T(2,128)S(1)} %fusion), channel_id=1, source_target_pairs={{0,16},{8,24},{16,0},{24,8},{1,17},{9,25},{17,1},{25,9},{2,18},{10... | collective-permute-start | bytes 18440 | tf_op jit(solution)/shard_map/ppermute | solution.py:423
  252.9 8.3 %collective-permute-start.24 = (bf16[96,768]{1,0:T(8,128)(2,1)}, bf16[96,768]{1,0:T(8,128)(2,1)S(1)}, u32[]{:S(2)}, u32[]{:S(2)}) collective-permute-start(bf16[96,768]{1,0:T(8,128)(2,1)} %add_convert_fusion.3.refs_1_), channel_id=1, source_target_pairs={{0,1},{1,0},{2,3},{3,2},{4,5},{5,4},{6,7},{7,6},{8,9},{9,8},{10,11... | collective-permute-start | bytes 442376 | tf_op jit(solution)/shard_map/ppermute | solution.py:423
  (5 other events, 4.3 us)
Sparse Core Ops, SparseCore 0:
  158.3 124.8 all-reduce.1
